TPU v7x, 32 devices: a whole 2x2x4 slice. The times are simulated.
32 devices in a mesh: shard: 8 (over z, y), seq: 4 (over x, core).
Axes of the slice: x: 2, y: 2, z: 4, core: 2. Of those that a mesh axis runs over, the one named last changes fastest.
Arguments:
- tokens: bfloat16 [16384, 768], P(('shard', 'seq')), may hold values from -6 to 6
- segment_ids: int32 [8, 2048], P('shard'), may hold values from 0 to 15, never falling along the last dimension, each value on 1 to 1024 neighbouring positions
- qkv_weight: bfloat16 [768, 2304], P('shard'), may hold values from -0.21875 to 0.21875
- out_weight: bfloat16 [768, 768], P('shard'), may hold values from -1.25 to 1.25
- up_weight: bfloat16 [768, 3072], P('shard'), may hold values from -0.21875 to 0.21875
- down_weight: bfloat16 [3072, 768], P('shard'), may hold values from -0.109375 to 0.109375
- first_gain: bfloat16 [768], P('shard'), may hold values from 0.5 to 1.5
- first_bias: bfloat16 [768], P('shard'), may hold values from -3 to 3
- second_gain: bfloat16 [768], P('shard'), may hold values from 0.5 to 1.5
- second_bias: bfloat16 [768], P('shard'), may hold values from -3 to 3
- out_grad: bfloat16 [16384, 768], P(('shard', 'seq')), may hold values from -6 to 6
Outputs:
- layer_output: bfloat16 [16384, 768], P(('shard', 'seq'))
- input_grad: float32 [16384, 768], P(('shard', 'seq'))
- qkv_grad: float32 [768, 2304], P('shard')
- mixer_grad: float32 [768, 768], P('shard')
- widen_grad: float32 [768, 3072], P('shard')
- narrow_grad: float32 [3072, 768], P('shard')
- first_gain_grad: float32 [768], P('shard')
- first_bias_grad: float32 [768], P('shard')
- second_gain_grad: float32 [768], P('shard')
- second_bias_grad: float32 [768], P('shard')
Inputs may be any that keep to these rules, and one draw needn't show every extreme that they name: `segment_ids`: in each row the ids never decrease; every document holds 1 to 1024 tokens and one holds exactly 1024.
All inputs are finite; a program needn't handle non-finite values.
Results may differ from a plain program's by a relative error of at most 0.02.
Values may be sent and summed in bfloat16 or wider, within the bound.
No kernel may reach another device: no remote copies, remote signals or barrier semaphores. Data moves between devices by JAX's collectives and lax.ppermute only.
A program may use at most 128 MiB of HBM per device.

v0:
```python
from functools import partial

import jax
import jax.numpy as jnp
from jax import lax
from jax.experimental import pallas as pl
from jax.experimental.pallas import tpu as pltpu
from jax.sharding import PartitionSpec as P

HEADS = 12
HEAD_DIM = 64
TRIO = 3 * HEAD_DIM
GROUPS = 16
EPSILON = 1e-12
FAR = -(2.0**30)
SCALE = HEAD_DIM**-0.5
TILE = 256
UNROLL = 2
BF = jnp.bfloat16
F32 = jnp.float32
VMEM = pl.BlockSpec(memory_space=pltpu.VMEM)
SMEM = pl.BlockSpec(memory_space=pltpu.SMEM)
FREE = pl.CostEstimate(flops=1, bytes_accessed=1, transcendentals=0)


def dot(a, b, ca, cb):
    return lax.dot_general(a, b, (((ca,), (cb,)), ((), ())), preferred_element_type=F32)


def shape(dims, kind):
    return jax.ShapeDtypeStruct(dims, kind)


def params(mebi):
    return pltpu.CompilerParams(vmem_limit_bytes=mebi << 20)


def assemble_kernel(offsets, info, *refs):
    out, sem = refs[-2:]
    copies = []
    for ref, rel in zip(refs[:-2], offsets):
        block = ref.shape[1]
        for i, r in enumerate(rel):
            at = pl.multiple_of((info[0] ^ r) * block, block)
            copies.append(
                pltpu.make_async_copy(ref.at[i], out.at[pl.ds(at, block), :], sem.at[len(copies)])
            )
    for copy in copies:
        copy.start()
    for copy in copies:
        copy.wait()


def assemble(pieces, offsets, me):
    block, cols = pieces[0].shape[1:]
    count = sum(len(r) for r in offsets)
    if block % 16:
        value = jnp.concatenate(pieces)
        order = [r for rel in offsets for r in rel]
        place = jnp.array([order.index(r) for r in range(count)], jnp.int32)
        return value[place[me ^ jnp.arange(count)]].reshape(count * block, cols)
    return pl.pallas_call(
        partial(assemble_kernel, offsets),
        out_shape=shape((count * block, cols), BF),
        in_specs=[SMEM] + [pl.BlockSpec(memory_space=pl.ANY)] * len(pieces),
        out_specs=VMEM,
        scratch_shapes=[pltpu.SemaphoreType.DMA((count,))],
        compiler_params=params(12),
        cost_estimate=FREE,
        name="assemble",
    )(me[None], *pieces)


def prepare_kernel(info, qkv_far, out_far, *refs):
    vectors, (part_a, part_b, qkv, out_weight, rows, scratch, sem) = refs[:4], refs[4:]
    block, width = out_weight.shape
    half, quarter = width // 2, width // 4
    copies = [
        pltpu.make_async_copy(qkv_far, qkv, sem.at[0]),
        pltpu.make_async_copy(out_far, out_weight, sem.at[1]),
    ] + [pltpu.make_async_copy(v, rows.at[i], sem.at[2 + i]) for i, v in enumerate(vectors)]
    for copy in copies:
        copy.start()
    scratch[...] = jnp.zeros_like(scratch)
    for copy in copies:
        copy.wait()
    for i in range(4):
        scratch[i : i + 1, :block] = rows[i].astype(F32)
    part_a[:, TRIO:] = scratch[...].T[:block, : 256 - TRIO].astype(BF)
    for x in range(2):
        for c in range(2):

            @pl.when(jnp.logical_and(info[0] == x, info[1] == c))
            def _():
                at = c * half + x * quarter
                trio = [qkv[:, i * width + at : i * width + at + quarter] for i in range(3)]
                for j in range(3):
                    piece = jnp.concatenate(
                        [t[:, j * HEAD_DIM : (j + 1) * HEAD_DIM] for t in trio], 1
                    )
                    if j == 0:
                        part_a[:, :TRIO] = piece
                    else:
                        part_b[:, (j - 1) * TRIO : j * TRIO] = piece
                part_b[:, 2 * TRIO :] = out_weight[:, c * half : (c + 1) * half]


def prepare(info, qkv, out_weight, vectors):
    block, width = out_weight.shape
    far = [qkv, out_weight] + [v[None] for v in vectors]
    return pl.pallas_call(
        prepare_kernel,
        out_shape=(shape((block, 256), BF), shape((block, 2 * TRIO + width // 2), BF)),
        in_specs=[SMEM] + [pl.BlockSpec(memory_space=pltpu.HBM)] * 6,
        out_specs=(VMEM, VMEM),
        scratch_shapes=[
            pltpu.VMEM(qkv.shape, BF),
            pltpu.VMEM(out_weight.shape, BF),
            pltpu.VMEM((4, 1, block), BF),
            pltpu.VMEM((128, 128), F32),
            pltpu.SemaphoreType.DMA((6,)),
        ],
        compiler_params=params(8),
        cost_estimate=FREE,
        name="prepare",
    )(info, *[pltpu.with_memory_space_constraint(v, pltpu.HBM) for v in far])


def vectors_kernel(part, out):
    out[...] = part[:, 128:].astype(F32).T[TRIO - 128 : TRIO - 120]


def vectors_of(part):
    return pl.pallas_call(
        vectors_kernel,
        out_shape=shape((8, part.shape[0]), F32),
        in_specs=[VMEM],
        out_specs=VMEM,
        compiler_params=params(8),
        cost_estimate=FREE,
        name="vectors",
    )(part)


def doc_rows(ids_ref, same, other):
    ids = ids_ref[...]
    rows = lax.broadcasted_iota(jnp.int32, (GROUPS, ids.shape[1]), 0)
    return jnp.where(rows == ids, same, other).astype(BF)


def plan_kernel(ids_s, ids_v, place, plan, row):
    total = ids_v.shape[1]
    tiles = total // TILE
    chunk = total // 4
    me = place[0] * 2 + place[1]
    entries = (plan.shape[0] - 1) // 2
    for i in range(2 * entries):
        plan[1 + i] = jnp.int32(tiles)
    first = [ids_s[0, i * TILE] for i in range(tiles)]
    last = [ids_s[0, i * TILE + TILE - 1] for i in range(tiles)]
    flip = me * (chunk // TILE)
    count = jnp.int32(0)
    for i in range(tiles):
        for j in range(tiles):
            meet = jnp.logical_and(first[i] <= last[j], first[j] <= last[i])

            @pl.when(meet)
            def _():
                plan[1 + 2 * UNROLL + count] = i ^ flip
                plan[1 + entries + 2 * UNROLL + count] = j ^ flip

            count = count + meet.astype(jnp.int32)
    plan[0] = (count + UNROLL - 1) // UNROLL
    for r in range(4):
        at = pl.multiple_of((me ^ r) * chunk, chunk)
        row[:, r * chunk : (r + 1) * chunk] = ids_v[:, pl.ds(at, chunk)]


def make_plan(ids, place):
    total = ids.shape[1]
    entries = (total // TILE) ** 2 + 4 * UNROLL
    return pl.pallas_call(
        plan_kernel,
        out_shape=(shape((1 + 2 * entries,), jnp.int32), shape((1, total), jnp.int32)),
        in_specs=[SMEM, VMEM, SMEM],
        out_specs=(SMEM, VMEM),
        compiler_params=params(8),
        cost_estimate=FREE,
        name="plan",
    )(ids, ids, place)


def tile_of(plan, entry):
    return pl.multiple_of(plan[1 + entry] * TILE, TILE)


def attend_kernel(
    plan, tok0, tok1, tok2, tok3, weight, ids_ref, ctx_own, ctx_send, ctx_full, lse,
    q_t, k_nat, v_t, s_ref, p_ref, fade, top, sums, acc,
):
    total = ids_ref.shape[1]
    half = total // 2
    entries = (plan.shape[0] - 1) // 2
    weight_t = weight[...].T
    keys = weight[:, HEAD_DIM : 2 * HEAD_DIM]
    for i, tok in enumerate((tok0, tok1, tok2, tok3)):
        rows = tok[...]
        at, end = i * rows.shape[0], (i + 1) * rows.shape[0]
        trio = dot(weight_t, rows, 1, 1).astype(BF)
        q_t[:HEAD_DIM, at:end] = trio[:HEAD_DIM] * SCALE
        v_t[:, at:end] = trio[2 * HEAD_DIM :]
        k_nat[at:end, :HEAD_DIM] = dot(rows, keys, 1, 0).astype(BF)
    q_t[HEAD_DIM : HEAD_DIM + GROUPS, :total] = doc_rows(ids_ref, 0.0, FAR)
    q_t[HEAD_DIM + GROUPS :, :total] = jnp.zeros((128 - HEAD_DIM - GROUPS, total), BF)
    docs = jnp.concatenate(
        [doc_rows(ids_ref, 1.0, 0.0), jnp.zeros((128 - HEAD_DIM - GROUPS, total), BF)], 0
    )
    k_nat[:total, HEAD_DIM:] = docs.T
    top[...] = jnp.full_like(top, -3e38)
    sums[...] = jnp.zeros_like(sums)
    acc[...] = jnp.zeros_like(acc)

    def step(j, carry):
        i = j * UNROLL
        for u in range(UNROLL):
            q, k = tile_of(plan, i + u), tile_of(plan, entries + i + u)
            acc[:, pl.ds(q, TILE)] = acc[:, pl.ds(q, TILE)] * fade[u] + dot(
                v_t[:, pl.ds(k, TILE)], p_ref[u], 1, 0
            )
        peaks = [jnp.max(s_ref[u], 0, keepdims=True) for u in range(UNROLL)]
        for u in range(UNROLL):
            q = tile_of(plan, i + UNROLL + u)
            old = top[:, pl.ds(q, TILE)]
            new = jnp.maximum(old, peaks[u])
            powers = jnp.exp(s_ref[u] - new)
            decay = jnp.exp(old - new)
            top[:, pl.ds(q, TILE)] = new
            sums[:, pl.ds(q, TILE)] = sums[:, pl.ds(q, TILE)] * decay + jnp.sum(
                powers, 0, keepdims=True
            )
            fade[u] = decay
            p_ref[u] = powers.astype(BF)
        for u in range(UNROLL):
            q = tile_of(plan, i + 2 * UNROLL + u)
            k = tile_of(plan, entries + i + 2 * UNROLL + u)
            s_ref[u] = dot(k_nat[pl.ds(k, TILE), :], q_t[:, pl.ds(q, TILE)], 1, 0)
        return carry

    lax.fori_loop(0, plan[0] + 2, step, 0)
    ctx_full[...] = acc[:, :total] / sums[:, :total]
    lse[...] = top[:, :total] + jnp.log(sums[:, :total])
    ctx_own[...] = ctx_full[:, :half].astype(BF)
    ctx_send[...] = ctx_full[:, half:].astype(BF)


def attend(plan, toks, weight, ids):
    total = ids.shape[1]
    half = total // 2
    padded = total + TILE
    return pl.pallas_call(
        attend_kernel,
        out_shape=(
            shape((HEAD_DIM, half), BF),
            shape((HEAD_DIM, half), BF),
            shape((HEAD_DIM, total), F32),
            shape((1, total), F32),
        ),
        in_specs=[SMEM] + [VMEM] * 6,
        out_specs=(VMEM,) * 4,
        scratch_shapes=[
            pltpu.VMEM((128, padded), BF),
            pltpu.VMEM((padded, 128), BF),
            pltpu.VMEM((HEAD_DIM, padded), BF),
            pltpu.VMEM((UNROLL, TILE, TILE), F32),
            pltpu.VMEM((UNROLL, TILE, TILE), BF),
            pltpu.VMEM((UNROLL, 1, TILE), F32),
            pltpu.VMEM((1, padded), F32),
            pltpu.VMEM((1, padded), F32),
            pltpu.VMEM((HEAD_DIM, padded), F32),
        ],
        compiler_params=params(20),
        cost_estimate=FREE,
        name="attend",
    )(plan, *toks, weight, ids)


def attend_back_kernel(
    order, plan, place, tok0, tok1, tok2, tok3, weight, ids_ref, g_own, g_recv, ctx_full, lse_in,
    sums, before, keep, send, grad_out,
    q_t, kvd, k_t, g_t, qg_nat, lse, row_term, s_ref, d_ref, p_ref, e_ref, acc, dq_t, w_grad, out,
):
    total = ids_ref.shape[1]
    half = total // 2
    entries = (plan.shape[0] - 1) // 2
    toks = (tok0, tok1, tok2, tok3)
    chunk = tok0.shape[0]
    weight_t = weight[:, : 2 * HEAD_DIM].T
    natural_w = weight[:, HEAD_DIM:]
    for at, grad in ((0, g_own), (half, g_recv)):
        g_t[HEAD_DIM:, at : at + half] = grad[...]
    g_t[:HEAD_DIM, :total] = jnp.zeros((HEAD_DIM, total), BF)
    for i, tok in enumerate(toks):
        at, end = i * chunk, (i + 1) * chunk
        rows = tok[...]
        pair = dot(weight_t, rows, 1, 1).astype(BF)
        q_t[:HEAD_DIM, at:end] = pair[:HEAD_DIM] * SCALE
        k_t[:, at:end] = pair[HEAD_DIM:]
        kvd[at:end, :128] = dot(rows, natural_w, 1, 0).astype(BF)
    qg_nat[:total, :] = jnp.concatenate([q_t[:HEAD_DIM, :total], g_t[HEAD_DIM:, :total]], 0).T
    q_t[HEAD_DIM:128, :total] = jnp.zeros((128 - HEAD_DIM, total), BF)
    q_t[128 : 128 + GROUPS, :total] = doc_rows(ids_ref, 0.0, FAR)
    q_t[128 + GROUPS :, :total] = jnp.zeros((128 - GROUPS, total), BF)
    kvd[:total, 128:] = jnp.concatenate(
        [doc_rows(ids_ref, 1.0, 0.0), jnp.zeros((128 - GROUPS, total), BF)], 0
    ).T
    acc[...] = jnp.zeros_like(acc)
    dq_t[...] = jnp.zeros_like(dq_t)
    lse[:, :total] = lse_in[...]
    row_term[:, :total] = jnp.sum(
        ctx_full[...] * g_t[HEAD_DIM:, :total].astype(F32), 0, keepdims=True
    )
    left = lax.broadcasted_iota(jnp.int32, (TILE, 128), 1) < HEAD_DIM

    def step(j, carry):
        i = j * UNROLL
        for u in range(UNROLL):
            q, k = tile_of(plan, i + u), tile_of(plan, entries + i + u)
            grad_scores, chance = e_ref[u], p_ref[u]
            natural = qg_nat[pl.ds(q, TILE), :]
            dq_t[:, pl.ds(q, TILE)] += dot(k_t[:, pl.ds(k, TILE)], grad_scores, 1, 0)
            acc[pl.ds(k, TILE), :] += jnp.where(
                left, dot(grad_scores, natural, 1, 0), dot(chance, natural, 1, 0)
            )
        for u in range(UNROLL):
            q = tile_of(plan, i + UNROLL + u)
            chance = jnp.exp(s_ref[u] - lse[:, pl.ds(q, TILE)])
            p_ref[u] = chance.astype(BF)
            e_ref[u] = (chance * (d_ref[u] - row_term[:, pl.ds(q, TILE)])).astype(BF)
        for u in range(UNROLL):
            q = tile_of(plan, i + 2 * UNROLL + u)
            rows = kvd[pl.ds(tile_of(plan, entries + i + 2 * UNROLL + u), TILE), :]
            s_ref[u] = dot(rows, q_t[:, pl.ds(q, TILE)], 1, 0)
            d_ref[u] = dot(rows[:, :128], g_t[:, pl.ds(q, TILE)], 1, 0)
        return carry

    lax.fori_loop(0, plan[0] + 2, step, 0)
    out[:HEAD_DIM, :] = (dq_t[:, :total] * SCALE).astype(BF)
    out[HEAD_DIM:, :] = acc[:total, :].T.astype(BF)
    keep[...] = out[:, :half]
    send[...] = out[:, half:]
    for i, tok in enumerate(toks):
        part = dot(out[:, i * chunk : (i + 1) * chunk], tok[...], 1, 0)
        w_grad[:TRIO, :] = part if i == 0 else w_grad[:TRIO, :] + part
    if sums is not None:
        w_grad[TRIO : TRIO + 8, :] = sums[...]
        w_grad[TRIO + 8 :, :] = jnp.zeros((256 - TRIO - 8, w_grad.shape[1]), F32)
    else:
        w_grad[TRIO:, :] = jnp.zeros((256 - TRIO, w_grad.shape[1]), F32)
    natural = w_grad[...].T
    block = grad_out.shape[1]
    for b in range(len(order)):
        to = order_of(order, place[2], b)
        value = natural[b * block : (b + 1) * block].astype(BF)
        if before is None:
            grad_out[to] = value
        else:
            ahead = before.shape[2]
            grad_out[to, :, :ahead] = before[to]
            grad_out[to, :, ahead:] = value


def order_of(order, me, b):
    rel = me ^ b
    bits = len(order).bit_length() - 1
    place = 0
    for i in range(bits):
        place = place | (((rel >> i) & 1) << (bits - 1 - i))
    return place


def attend_back(plan, place, toks, weight, ids, g_own, g_recv, ctx_full, lse, sums, before, n_shard):
    total = ids.shape[1]
    width = weight.shape[0]
    padded = total + TILE
    extra = [value for value in (sums, before) if value is not None]
    cols = 256 + (0 if before is None else before.shape[2])

    def kernel(*refs):
        refs = list(refs)
        if sums is None:
            refs.insert(12, None)
        if before is None:
            refs.insert(13, None)
        attend_back_kernel(range(n_shard), *refs)

    return pl.pallas_call(
        kernel,
        out_shape=(shape((TRIO, total // 2), BF),) * 2
        + (shape((n_shard, width // n_shard, cols), BF),),
        in_specs=[SMEM, SMEM] + [VMEM] * (10 + len(extra)),
        out_specs=(VMEM,) * 3,
        scratch_shapes=[
            pltpu.VMEM((256, padded), BF),
            pltpu.VMEM((padded, 256), BF),
            pltpu.VMEM((HEAD_DIM, padded), BF),
            pltpu.VMEM((128, padded), BF),
            pltpu.VMEM((padded, 128), BF),
            pltpu.VMEM((1, padded), F32),
            pltpu.VMEM((1, padded), F32),
            pltpu.VMEM((UNROLL, TILE, TILE), F32),
            pltpu.VMEM((UNROLL, TILE, TILE), F32),
            pltpu.VMEM((UNROLL, TILE, TILE), BF),
            pltpu.VMEM((UNROLL, TILE, TILE), BF),
            pltpu.VMEM((padded, 128), F32),
            pltpu.VMEM((HEAD_DIM, padded), F32),
            pltpu.VMEM((256, width), F32),
            pltpu.VMEM((TRIO, total), BF),
        ],
        compiler_params=params(24),
        cost_estimate=FREE,
        name="attend_back",
    )(plan, place, *toks, weight, ids, g_own, g_recv, ctx_full, lse, *extra)


def input_back_kernel(*refs):
    grads, weights, (own, send), (tall, wide) = refs[:6], refs[6:12], refs[12:14], refs[14:]
    rows = own.shape[0]
    step = 256
    for i, (grad, weight) in enumerate(zip(grads, weights)):
        tall[i * TRIO : (i + 1) * TRIO, :] = grad[...]
        wide[:, i * TRIO : (i + 1) * TRIO] = weight[:, :TRIO]

    def body(i, carry):
        at = pl.multiple_of(i * step, step)
        part = dot(tall[:, pl.ds(at, step)].T, wide[...], 1, 1)

        @pl.when(at < rows)
        def _():
            own[pl.ds(at, step), :] = part

        @pl.when(at >= rows)
        def _():
            send[pl.ds(pl.multiple_of(at - rows, step), step), :] = part.astype(BF)

        return carry

    lax.fori_loop(0, 2 * rows // step, body, 0)


def input_back(grads, weights, rows):
    width = weights[0].shape[0]
    return pl.pallas_call(
        input_back_kernel,
        out_shape=(shape((rows, width), F32), shape((rows, width), BF)),
        in_specs=[VMEM] * 12,
        out_specs=(VMEM,) * 2,
        scratch_shapes=[pltpu.VMEM((6 * TRIO, 2 * rows), BF), pltpu.VMEM((width, 6 * TRIO), BF)],
        compiler_params=params(24),
        cost_estimate=FREE,
        name="input_back",
    )(*grads, *weights)


def place_qkv_kernel(start, info, chip, other, out, sums_out):
    part = out.shape[1] // 3
    x, c = info[0] == 0, info[1] == 0
    values = [
        ref[:, start + dx * 768 : start + (dx + 1) * 768].astype(F32)
        for ref in (chip, other)
        for dx in range(2)
    ]
    tail = [v[:, 2 * 256 + TRIO : 2 * 256 + TRIO + 8] for v in values]
    sums_out[...] = tail[0] + tail[1] + tail[2] + tail[3]
    for sec in range(3):
        at = sec * HEAD_DIM
        near, near_x, far, far_x = [
            jnp.concatenate(
                [v[:, j * 256 + at : j * 256 + at + HEAD_DIM] for j in range(3)], 1
            )
            for v in values
        ]
        near, near_x = jnp.where(x, near, near_x), jnp.where(x, near_x, near)
        far, far_x = jnp.where(x, far, far_x), jnp.where(x, far_x, far)
        out[:, sec * part : (sec + 1) * part] = jnp.concatenate(
            [
                jnp.where(c, near, far),
                jnp.where(c, near_x, far_x),
                jnp.where(c, far, near),
                jnp.where(c, far_x, near_x),
            ],
            1,
        )


def place_qkv(info, chip, other, start, width):
    block = chip.shape[0]
    return pl.pallas_call(
        partial(place_qkv_kernel, start),
        out_shape=(shape((block, 3 * width), F32), shape((block, 8), F32)),
        in_specs=[SMEM] + [VMEM] * 2,
        out_specs=(VMEM, VMEM),
        compiler_params=params(8),
        cost_estimate=FREE,
        name="place_qkv",
    )(info, chip, other)


def gelu_both(u):
    root = 0.7978845608028654
    cube = 0.044715 * root
    square = u * u
    t = jnp.tanh(u * (root + cube * square))
    half = 0.5 * (1.0 + t)
    act = u * half
    slope = half + act * (1.0 - t) * (root + 3.0 * cube * square)
    return act, slope


def feed_up_kernel(low0, low1, low2, low3, up, act_out, act_t, slope_out, low_t, low):
    step = low0.shape[0]
    for p, piece in enumerate((low0, low1, low2, low3)):
        low[p * step : (p + 1) * step, :] = piece[...]

    def body(i, carry):
        at = pl.multiple_of(i * step, step)
        value = low[pl.ds(at, step), :]
        low_t[:, pl.ds(at, step)] = value.T
        act, slope = gelu_both(dot(value, up[...], 1, 0))
        act = act.astype(BF)
        act_out[pl.ds(at, step), :] = act
        act_t[:, pl.ds(at, step)] = act.T
        slope_out[pl.ds(at, step), :] = slope.astype(BF)
        return carry

    lax.fori_loop(0, 4, body, 0)


def feed_up(lows, up):
    rows, width = lows[0].shape
    hidden = up.shape[1]
    return pl.pallas_call(
        feed_up_kernel,
        out_shape=(
            shape((4 * rows, hidden), BF),
            shape((hidden, 4 * rows), BF),
            shape((4 * rows, hidden), BF),
            shape((width, 4 * rows), BF),
        ),
        in_specs=[VMEM] * 5,
        out_specs=(VMEM,) * 4,
        scratch_shapes=[pltpu.VMEM((4 * rows, width), BF)],
        compiler_params=params(32),
        cost_estimate=FREE,
        name="feed_up",
    )(*lows, up)


def feed_down_kernel(act, down, own, send):
    rows = own.shape[0]
    step = 256

    def body(i, carry):
        at = pl.multiple_of(i * step, step)
        part = dot(act[pl.ds(at, step), :], down[...], 1, 0)

        @pl.when(at < rows)
        def _():
            own[pl.ds(at, step), :] = part

        @pl.when(at >= rows)
        def _():
            send[pl.ds(pl.multiple_of(at - rows, step), step), :] = part.astype(BF)

        return carry

    lax.fori_loop(0, 2 * rows // step, body, 0)


def feed_down(act, down):
    rows, hidden = act.shape
    width = down.shape[1]
    return pl.pallas_call(
        feed_down_kernel,
        out_shape=(shape((rows // 2, width), F32), shape((rows // 2, width), BF)),
        in_specs=[VMEM] * 2,
        out_specs=(VMEM,) * 2,
        compiler_params=params(24),
        cost_estimate=FREE,
        name="feed_down",
    )(act, down)


def feed_back_kernel(
    grad_own, grad_other, slope, up, down, own, send0, send1, pre_out, grad, send
):
    rows = grad_own.shape[0]
    step = 256
    grad[:rows, :] = grad_own[...]
    grad[rows:, :] = grad_other[...]

    def body(i, carry):
        at = pl.multiple_of(i * step, step)
        pre = dot(grad[pl.ds(at, step), :], down[...], 1, 1)
        pre = (pre * slope[pl.ds(at, step), :].astype(F32)).astype(BF)
        pre_out[pl.ds(at, step), :] = pre
        part = dot(pre, up[...], 1, 1)

        @pl.when(at < rows)
        def _():
            own[pl.ds(at, step), :] = part

        @pl.when(at >= rows)
        def _():
            send[pl.ds(pl.multiple_of(at - rows, step), step), :] = part.astype(BF)

        return carry

    lax.fori_loop(0, 2 * rows // step, body, 0)
    send0[...] = send[: rows // 2, :]
    send1[...] = send[rows // 2 :, :]


def feed_back(grad_own, grad_other, slope, up, down):
    rows, width = grad_own.shape
    hidden = up.shape[1]
    return pl.pallas_call(
        feed_back_kernel,
        out_shape=(
            shape((rows, width), F32),
            shape((rows // 2, width), BF),
            shape((rows // 2, width), BF),
            shape((2 * rows, hidden), BF),
        ),
        in_specs=[VMEM] * 5,
        out_specs=(VMEM,) * 4,
        scratch_shapes=[pltpu.VMEM((2 * rows, width), BF), pltpu.VMEM((rows, width), BF)],
        compiler_params=params(32),
        cost_estimate=FREE,
        name="feed_back",
    )(grad_own, grad_other, slope, up, down)


def weight_grad_kernel(blocks, reverse, shard, left, right_own, right_other, out):
    rows, cols = left.shape[0], out.shape[2]
    half = left.shape[1] // 2
    step = 256
    block = out.shape[1]
    lone = right_other is None

    def body(i, carry):
        at = pl.multiple_of(i * step, step)
        if lone:
            value = dot(left[...], right_own[:, pl.ds(at, step)], 1, 0)
        else:
            value = dot(left[:, :half], right_own[:, pl.ds(at, step)], 1, 0) + dot(
                left[:, half:], right_other[:, pl.ds(at, step)], 1, 0
            )
        for b in range(blocks):
            to = order_of(range(blocks), shard[0], b) if reverse else shard[0] ^ b
            out[to, :, pl.ds(at, step)] = value[
                b * block : (b + 1) * block
            ].astype(BF)
        return carry

    lax.fori_loop(0, cols // step, body, 0)


def weight_grad(shard, left, rights, blocks, reverse=True):
    rows, cols = left.shape[0], rights[0].shape[1]

    def kernel(*refs):
        refs = list(refs)
        if len(rights) == 1:
            refs.insert(3, None)
        weight_grad_kernel(blocks, reverse, *refs)

    return pl.pallas_call(
        kernel,
        out_shape=shape((blocks, rows // blocks, cols), BF),
        in_specs=[SMEM, VMEM] + [VMEM] * len(rights),
        out_specs=VMEM,
        compiler_params=params(24),
        cost_estimate=FREE,
        name="weight_grad",
    )(shard[None], left, *rights)


def mix_back_kernel(mixer, grad0, grad1, grad2, grad3, g_own, g_send):
    quarter = g_own.shape[0]
    rows = grad0.shape[0]
    for p, grad in enumerate((grad0, grad1, grad2, grad3)):
        value = dot(mixer[...], grad[...], 1, 1).astype(BF)
        g_own[:, p * rows : (p + 1) * rows] = value[:quarter]
        g_send[:, p * rows : (p + 1) * rows] = value[quarter:]


def mix_back(mixer, grads):
    half_width = mixer.shape[0]
    rows = grads[0].shape[0] * 4
    return pl.pallas_call(
        mix_back_kernel,
        out_shape=(shape((half_width // 2, rows), BF),) * 2,
        in_specs=[VMEM] * 5,
        out_specs=(VMEM,) * 2,
        compiler_params=params(16),
        cost_estimate=FREE,
        name="mix_back",
    )(mixer, *grads)


def mix_grad_kernel(info, context, grad0, grad1, grad2, grad3, own, send):
    rows = grad0.shape[0]
    half_width = own.shape[1]
    for out, half in ((own, info[1]), (send, 1 - info[1])):
        at = pl.multiple_of(half * half_width, half_width)
        total = None
        for p, grad in enumerate((grad0, grad1, grad2, grad3)):
            part = dot(
                context[:, p * rows : (p + 1) * rows], grad[:, pl.ds(at, half_width)], 1, 0
            )
            total = part if total is None else total + part
        out[...] = total.astype(BF)


def mix_grad(info, context, grads):
    half_width = context.shape[0]
    return pl.pallas_call(
        mix_grad_kernel,
        out_shape=(shape((half_width, half_width), BF),) * 2,
        in_specs=[SMEM] + [VMEM] * 5,
        out_specs=(VMEM,) * 2,
        compiler_params=params(16),
        cost_estimate=FREE,
        name="mix_grad",
    )(info, context, *grads)


def mix_place_kernel(blocks, info, own, recv, out, scratch):
    half_width = own.shape[1]
    quarter = half_width // 2
    x, c, shard = info[0], info[1], info[2]
    for ref, dc in ((own, 0), (recv, 1)):
        for dx in range(2):
            at = pl.multiple_of((c ^ dc) * half_width + (x ^ dx) * quarter, quarter)
            scratch[pl.ds(at, quarter), :] = ref[dx * quarter : (dx + 1) * quarter, :].astype(F32)
    block = out.shape[1]
    for b in range(blocks):
        out[order_of(range(blocks), shard, b)] = scratch[b * block : (b + 1) * block, :].astype(BF)


def mix_place(info, own, recv, blocks):
    half_width = own.shape[1]
    return pl.pallas_call(
        partial(mix_place_kernel, blocks),
        out_shape=shape((blocks, 2 * half_width // blocks, half_width), BF),
        in_specs=[SMEM, VMEM, VMEM],
        out_specs=VMEM,
        scratch_shapes=[pltpu.VMEM((2 * half_width, half_width), F32)],
        compiler_params=params(8),
        cost_estimate=FREE,
        name="mix_place",
    )(info, own, recv)


def row_tiles(rows, step, body):
    lax.fori_loop(0, rows // step, lambda i, c: body(pl.ds(pl.multiple_of(i * step, step), step), c), 0)


def mean_of(value):
    return jnp.mean(value, -1, keepdims=True)


def first_norm_kernel(
    tokens, mixed, recv0, recv1, vectors, low0, low1, normed_out, inverse_out, recv, low
):
    gain, bias = vectors[0:1, :], vectors[1:2, :]
    half = recv0.shape[0]
    recv[:half, :] = recv0[...]
    recv[half:, :] = recv1[...]

    def body(at, carry):
        hidden = tokens[at, :].astype(F32) + mixed[at, :] + recv[at, :].astype(F32)
        centred = hidden - mean_of(hidden)
        inverse = lax.rsqrt(mean_of(centred * centred) + EPSILON)
        normed = centred * inverse
        normed_out[at, :] = normed
        inverse_out[at, :] = inverse
        low[at, :] = (normed * gain + bias).astype(BF)
        return carry

    row_tiles(tokens.shape[0], 128, body)
    low0[...] = low[:half, :]
    low1[...] = low[half:, :]


def first_norm(tokens, mixed, recvs, vectors):
    rows, width = tokens.shape
    return pl.pallas_call(
        first_norm_kernel,
        grid=(1,),
        out_shape=(shape((rows // 2, width), BF),) * 2
        + (shape((rows, width), F32), shape((rows, 1), F32)),
        in_specs=[pl.BlockSpec((rows, width), lambda i: (0, 0))] * 2
        + [pl.BlockSpec((rows // 2, width), lambda i: (0, 0))] * 2
        + [pl.BlockSpec(vectors.shape, lambda i: (0, 0))],
        scratch_shapes=[pltpu.VMEM((rows, width), BF)] * 2,
        out_specs=(pl.BlockSpec((rows // 2, width), lambda i: (0, 0)),) * 2
        + (
            pl.BlockSpec((rows, width), lambda i: (0, 0)),
            pl.BlockSpec((rows, 1), lambda i: (0, 0)),
        ),
        compiler_params=params(24),
        cost_estimate=FREE,
        name="first_norm",
    )(tokens, mixed, *recvs, vectors)


def second_norm_kernel(normed_one, mlp, recv, vectors, grad, result, grad_two, grad_low, sums):
    gain_one, bias_one = vectors[0:1, :], vectors[1:2, :]
    gain, bias = vectors[2:3, :], vectors[3:4, :]
    sums[...] = jnp.zeros_like(sums)

    def body(at, carry):
        hidden = normed_one[at, :] * gain_one + bias_one + mlp[at, :] + recv[at, :].astype(F32)
        centred = hidden - mean_of(hidden)
        inverse = lax.rsqrt(mean_of(centred * centred) + EPSILON)
        normed = centred * inverse
        result[at, :] = (normed * gain + bias).astype(BF)
        grad_y = grad[at, :].astype(F32)
        grad_n = grad_y * gain
        value = inverse * (grad_n - mean_of(grad_n) - normed * mean_of(grad_n * normed))
        grad_two[at, :] = value
        grad_low[at, :] = value.astype(BF)
        sums[2:3, :] += jnp.sum(grad_y * normed, 0, keepdims=True)
        sums[3:4, :] += jnp.sum(grad_y, 0, keepdims=True)
        return carry

    row_tiles(grad.shape[0], 128, body)


def second_norm(normed_one, mlp, recv, vectors, grad):
    rows, width = grad.shape
    return pl.pallas_call(
        second_norm_kernel,
        out_shape=(
            shape((rows, width), BF),
            shape((rows, width), F32),
            shape((rows, width), BF),
            shape((8, width), F32),
        ),
        in_specs=[VMEM] * 5,
        out_specs=(VMEM,) * 4,
        compiler_params=params(24),
        cost_estimate=FREE,
        name="second_norm",
    )(normed_one, mlp, recv, vectors, grad)


def first_back_kernel(
    grad_two, own, recv0, recv1, normed_one, inverse_one, vectors, late,
    grad_one, low0, low1, sums, grad_low, recv,
):
    gain = vectors[0:1, :]
    half = low0.shape[0]
    recv[:half, :] = recv0[...]
    recv[half:, :] = recv1[...]
    sums[...] = late[...]

    def body(at, carry):
        normed = normed_one[at, :]
        grad_y = grad_two[at, :] + own[at, :] + recv[at, :].astype(F32)
        grad_n = grad_y * gain
        value = inverse_one[at, :] * (grad_n - mean_of(grad_n) - normed * mean_of(grad_n * normed))
        grad_one[at, :] = value
        grad_low[at, :] = value.astype(BF)
        sums[0:1, :] += jnp.sum(grad_y * normed, 0, keepdims=True)
        sums[1:2, :] += jnp.sum(grad_y, 0, keepdims=True)
        return carry

    row_tiles(grad_two.shape[0], 128, body)
    low0[...] = grad_low[:half, :]
    low1[...] = grad_low[half:, :]


def first_back(grad_two, own, recvs, normed_one, inverse_one, vectors, late):
    rows, width = grad_two.shape
    return pl.pallas_call(
        first_back_kernel,
        out_shape=(shape((rows, width), F32),)
        + (shape((rows // 2, width), BF),) * 2
        + (shape((8, width), F32),),
        in_specs=[VMEM] * 8,
        out_specs=(VMEM,) * 4,
        scratch_shapes=[pltpu.VMEM((rows, width), BF)] * 2,
        compiler_params=params(24),
        cost_estimate=FREE,
        name="first_back",
    )(grad_two, own, *recvs, normed_one, inverse_one, vectors, late)


def after(value, *earlier):
    return lax.optimization_barrier((value,) + earlier)[0]


def shards(
    n_shard,
    tokens,
    segment_ids,
    qkv_weight,
    out_weight,
    up_weight,
    down_weight,
    first_gain,
    first_bias,
    second_gain,
    second_bias,
    out_grad,
):
    rows, width = tokens.shape
    half_width = width // 2
    quarter = width // 4
    ff_half = up_weight.shape[1] // 2
    block = qkv_weight.shape[0]
    shard = lax.axis_index("shard").astype(jnp.int32)
    seq = lax.axis_index("seq").astype(jnp.int32)
    xb, cb = seq // 2, seq % 2
    bits = [1 << b for b in range(n_shard.bit_length() - 1)]
    top = bits[-1]
    owner = (shard // top) % 2 == cb
    low_shard = shard % top
    place = jnp.stack([xb, cb, shard])

    def swap(value, mask):
        return lax.ppermute(value, "shard", [(i, i ^ mask) for i in range(n_shard)])

    def swap_core(value):
        return lax.ppermute(value, "seq", [(i, i ^ 1) for i in range(4)])

    def swap_x(value):
        return lax.ppermute(value, "seq", [(i, i ^ 2) for i in range(4)])

    def to_core(value, to_owner):
        pairs = []
        for sh in range(n_shard):
            for se in range(4):
                sends = (sh // top == se % 2) != to_owner
                pairs.append((sh * 4 + se, (sh ^ top) * 4 + se if sends else sh * 4 + (se ^ 1)))
        return lax.ppermute(value, ("shard", "seq"), pairs)

    def join(pieces):
        return jnp.concatenate(pieces) if len(pieces) > 1 else pieces[0]

    class Gather:
        def __init__(self, own_block, over):
            self.pieces, self.offsets, self.over = [own_block[None]], [[0]], list(over)

        def swap(self, value, rel, bit):
            got = swap(value, bit)
            self.pieces.append(got)
            self.offsets.append([r ^ bit for r in rel])
            return got

        def steps(self, count, *gate):
            for bit in [self.over.pop(0) for _ in range(count)]:
                held, rel = join(self.pieces), [r for o in self.offsets for r in o]
                self.pieces, self.offsets = [held], [rel]
                gate = (self.swap(after(held, *gate), rel, bit),)
            return gate[0]

        def part(self, index, *gate):
            return self.swap(after(self.pieces[index], *gate), self.offsets[index], self.over[0])

    def fold(value, got):
        return (value[: value.shape[0] // 2].astype(F32) + got.astype(F32)).astype(BF)

    def upper(value):
        return value[value.shape[0] // 2 :]

    def add_x(value):
        return (value.astype(F32) + swap_x(value).astype(F32)).astype(BF)

    def pick(value, flag, axis):
        return jnp.where(
            flag == 0,
            lax.index_in_dim(value, 0, axis, False),
            lax.index_in_dim(value, 1, axis, False),
        )

    def ordered(flag, own, other, axis):
        return jnp.where(
            flag == 0, jnp.concatenate([own, other], axis), jnp.concatenate([other, own], axis)
        )

    over_x = swap_x(tokens)
    over_core = swap_core(tokens)
    toks = [tokens, over_core, over_x]
    plan, ids_row = make_plan(segment_ids, place)

    own_a, own_b = prepare(
        place, qkv_weight, out_weight, (first_gain, first_bias, second_gain, second_bias)
    )
    up_half = lax.dynamic_slice_in_dim(up_weight, cb * ff_half, ff_half, 1)
    down_rows = down_weight.shape[0] // 2
    down_half = lax.dynamic_slice_in_dim(down_weight, xb * down_rows, down_rows, 0)
    middle = len(bits) - 2
    gather_a = Gather(own_a, bits[::-1])
    gather_b = Gather(own_b, bits[::-1])
    gather_up = Gather(up_half, bits[::-1])
    a1 = gather_a.steps(1)
    b1 = gather_b.steps(1, a1)
    a2 = gather_a.steps(middle, plan)
    a3 = gather_a.steps(1)
    b2 = gather_b.steps(middle, a2, up_half, down_half)
    d1 = to_core(after(down_half, b1), False)
    toks.append(swap_core(after(over_x, b2)))
    b3 = gather_b.steps(1, a3)
    part_a = assemble(gather_a.pieces, gather_a.offsets, shard)
    vectors = vectors_of(part_a)
    far_a = swap_x(part_a)

    saved, own_ctx, sends = [], [], []

    def head(j, weight, *gate):
        ctx_own, ctx_send, ctx_full, lse = attend(
            plan, toks, weight, after(ids_row, *gate)
        )
        own_ctx.append(ctx_own)
        sends.append(ctx_send)
        saved.append((ctx_full, lse))
        return ctx_own

    ctx = head(0, part_a[:, :TRIO], b2, vectors)
    d1, b3 = after(d1, ctx), after(b3, ctx)
    gather_b.pieces[1] = b3
    gather_down = Gather(jnp.where(owner, down_half, d1), bits[-2::-1])
    d2 = gather_down.steps(middle)
    u1 = gather_up.steps(1, ctx)
    part_b = assemble(gather_b.pieces, gather_b.offsets, shard)
    far_b = swap_x(part_b[:, : 2 * TRIO])
    ctx = head(1, part_b[:, :TRIO], gather_down.pieces[0])
    d2, u1 = after(d2, ctx), after(u1, ctx)
    gather_down.pieces[1], gather_up.pieces[1] = d2, u1
    d3 = gather_down.steps(1)
    u2 = gather_up.steps(middle)
    ctx = head(2, part_b[:, TRIO : 2 * TRIO], gather_down.pieces[0], gather_up.pieces[0], far_a, far_b)
    d3, u2 = after(d3, ctx), after(u2, ctx)
    gather_down.pieces[1], gather_up.pieces[1] = d3, u2
    held_up = join(gather_up.pieces)
    held = join(gather_down.pieces)
    gather_up.offsets = [[r for o in gather_up.offsets for r in o]]
    sends[2], held_up, held = lax.optimization_barrier((sends[2], held_up, held))
    gather_up.pieces = [held_up]
    gather_up.part(0)
    others = [swap_x(value) for value in sends]
    rel = [2 * r for o in gather_down.offsets for r in o]
    widen = assemble(gather_up.pieces, gather_up.offsets, shard)
    held_far = swap_x(held)
    head_weights = [part_a[:, :TRIO], part_b[:, :TRIO], part_b[:, TRIO : 2 * TRIO]]
    far_weights = [far_a, far_b[:, :TRIO], far_b[:, TRIO:]]
    mixer = part_b[:, 2 * TRIO :].reshape(2, half_width, half_width)
    mixer = ordered(cb, pick(mixer, cb, 0), swap_core(pick(mixer, 1 - cb, 0)), 1)
    mixer = jnp.where(xb == 0, mixer, jnp.concatenate([mixer[quarter:], mixer[:quarter]]))
    context = jnp.concatenate(own_ctx + others)

    mixed = dot(context, mixer, 0, 0)
    low0, low1, normed_one, inverse_one = first_norm(
        tokens,
        mixed,
        [swap_core(mixed[at : at + rows // 2].astype(BF)) for at in (rows, rows + rows // 2)],
        vectors,
    )
    act_low, act_t, slope, low_t = feed_up([low0, low1, swap_core(low0), swap_core(low1)], widen)
    held_far = after(held_far, act_low)
    narrow = assemble([held, held_far], [rel, [r + 1 for r in rel]], low_shard * 2 + xb)
    mlp_own, mlp_send = feed_down(act_low, narrow)
    result, grad_two, grad_mlp, late = second_norm(
        normed_one, mlp_own, swap_core(mlp_send), vectors, out_grad
    )

    grad_mlp = [grad_mlp, swap_core(grad_mlp)]
    narrow_grad = weight_grad(low_shard, act_t, grad_mlp, n_shard // 2, False)
    n1 = swap(upper(narrow_grad), bits[-2])
    first_own, send0, send1, grad_pre = feed_back(
        after(grad_mlp[0], narrow_grad), grad_mlp[1], slope, widen, narrow
    )
    widen_grad = weight_grad(shard, low_t, [grad_pre], n_shard)
    w1 = swap(upper(widen_grad), bits[0])
    recv0, recv1, _ = lax.optimization_barrier((swap_core(send0), swap_core(send1), widen_grad))
    grad_one, attn0, attn1, sums = first_back(
        grad_two, first_own, [recv0, recv1], normed_one, inverse_one, vectors, late
    )
    attn = [attn0, attn1, swap_core(attn0), swap_core(attn1)]
    g_own, g_send = mix_back(mixer, attn)
    mixer_own, mixer_send = mix_grad(place, after(context, g_send), attn)
    g_recv = swap_x(g_send)
    mixer_grad = mix_place(place, mixer_own, swap_core(mixer_send), n_shard)

    def head_back(j, before, *gate):
        at = j * HEAD_DIM
        return attend_back(
            plan, place, toks, head_weights[j], after(ids_row, *gate),
            g_own[at : at + HEAD_DIM], g_recv[at : at + HEAD_DIM], *saved[j],
            sums if j == 2 else None, before, n_shard,
        )

    keeps, sends = [None] * 3, [None] * 3
    keeps[0], sends[0], early = head_back(0, mixer_grad)
    fars = [swap_x(sends[0])]
    narrow_grad = fold(narrow_grad, after(n1, early))
    for bit in bits[-3:0:-1]:
        narrow_grad = fold(narrow_grad, swap(upper(narrow_grad), bit))
    n2 = swap(upper(narrow_grad), bits[0])
    widen_grad = fold(widen_grad, after(w1, narrow_grad))
    for bit in bits[1:-2]:
        widen_grad = fold(widen_grad, swap(upper(widen_grad), bit))
    w2 = swap(upper(widen_grad), bits[-2])
    keeps[1], sends[1], part = head_back(1, None, narrow_grad, widen_grad)
    fars.append(swap_x(sends[1]))
    narrow_grad = fold(narrow_grad, after(n2, part))[0]
    n3 = to_core(narrow_grad, True)
    widen_grad = fold(widen_grad, after(w2, narrow_grad, fars[0]))
    w3 = swap(upper(widen_grad), bits[-1])
    early = after(early, narrow_grad, widen_grad)
    e1 = swap(upper(early), bits[0])
    keeps[2], sends[2], late = head_back(2, part, narrow_grad, widen_grad)
    fars.append(swap_x(sends[2]))
    widen_grad = fold(widen_grad, after(w3, late, fars[1]))[0]
    early = fold(early, after(e1, widen_grad))
    e2 = swap(upper(early), bits[1])
    late = after(late, widen_grad, early)
    l1 = swap(upper(late), bits[0])
    w4 = swap_x(widen_grad)
    late = fold(late, after(l1, fars[2]))
    l2 = swap(upper(late), bits[1])
    fars[2] = after(fars[2], late)
    back_own, back_core = input_back(keeps + fars, head_weights + far_weights, rows)
    back_near = swap_core(back_core)
    late = fold(late, after(l2, w4, back_core))
    for bit in bits[2:-1]:
        late = fold(late, swap(upper(late), bit))
    l3 = swap(upper(late), bits[-1])
    early = fold(early, after(e2, late))
    for bit in bits[2:-1]:
        early = fold(early, swap(upper(early), bit))
    e3 = swap(upper(early), bits[-1])
    narrow_grad = (narrow_grad.astype(F32) + after(n3, early).astype(F32)).astype(BF)
    halves = narrow_grad.reshape(2, -1, width)
    narrow_half = swap_core(pick(halves, 1 - cb, 0))
    narrow_half = jnp.where(owner, pick(halves, cb, 0), narrow_half)
    n4 = swap_x(narrow_half)
    widen_grad = (widen_grad.astype(F32) + after(w4, late).astype(F32)).astype(BF)
    widen_other = swap_core(widen_grad)
    input_grad = grad_one + back_own + after(back_near, late).astype(F32)
    early = fold(early, after(e3, narrow_half))[0]
    late = fold(late, after(l3, early))[0]
    mine = jnp.concatenate([early, late], 1)
    theirs = swap_x(mine)
    narrow_half = (narrow_half.astype(F32) + after(n4, mine).astype(F32)).astype(BF)
    narrow_other = swap_core(narrow_half)
    widen_grad = ordered(cb, widen_grad, widen_other, 1)
    narrow_grad = ordered(cb, narrow_half, narrow_other, 0)
    narrow_grad, widen_grad = narrow_grad.astype(F32), widen_grad.astype(F32)
    theirs = after(theirs, narrow_grad, widen_grad, input_grad)
    mixer_grad = (mine[:, :half_width].astype(F32) + theirs[:, :half_width].astype(F32)).astype(BF)
    chip = jnp.concatenate([mixer_grad, mine[:, half_width:], theirs[:, half_width:]], 1)
    other = swap_core(chip)
    mixer_grad = ordered(cb, mixer_grad, other[:, :half_width], 1)
    qkv_grad, sums = place_qkv(place, chip, other, half_width, width)
    return (
        result,
        input_grad,
        qkv_grad,
        mixer_grad.astype(F32),
        widen_grad,
        narrow_grad,
        sums[:, 0],
        sums[:, 1],
        sums[:, 2],
        sums[:, 3],
    )


def solution(mesh):
    placed = (
        P(("shard", "seq"), None),
        P("shard", None),
        P("shard", None),
        P("shard", None),
        P("shard", None),
        P("shard", None),
        P("shard"),
        P("shard"),
        P("shard"),
        P("shard"),
        P(("shard", "seq"), None),
    )
    return jax.shard_map(
        partial(shards, mesh.shape["shard"]),
        mesh=mesh,
        in_specs=placed,
        out_specs=(
            P(("shard", "seq"), None),
            P(("shard", "seq"), None),
            P("shard", None),
            P("shard", None),
            P("shard", None),
            P("shard", None),
            P("shard"),
            P("shard"),
            P("shard"),
            P("shard"),
        ),
        check_vma=False,
    )
```

profile of v0, /device:TPU:0, one launch (start us, length us, event | category | flops | bytes accessed | tf_op | source)
XLA Modules:
  0.0 262.5 jit_solution(11661563085607356343)
XLA Ops:
  2.7 4.1 %collective-permute-start.2 = (bf16[1,96,256]{2,1,0:T(8,128)(2,1)S(1)}, bf16[1,96,256]{2,1,0:T(8,128)(2,1)S(1)}, u32[]{:S(2)}, u32[]{:S(2)}) collective-permute-start(bf16[1,96,256]{2,1,0:T(8,128)(2,1)S(1)} %bitcast.32), channel_id=1, source_target_pairs={{0,16},{4,20},{8,24},{12,28},{16,0},{20,4},{24,8},{28,12},{1,17},{... | collective-permute-start | bytes 147464 | tf_op jit(solution)/shard_map/ppermute | solution.py:934
  9.4 2.4 collective-permute-start.3
  15.1 2.0 collective-permute-start.4
  21.7 6.1 %collective-permute-done.5 = bf16[2,96,768]{2,1,0:T(8,128)(2,1)S(1)} collective-permute-done((bf16[2,96,768]{2,1,0:T(8,128)(2,1)S(1)}, bf16[2,96,768]{2,1,0:T(8,128)(2,1)S(1)}, u32[]{:S(2)}, u32[]{:S(2)}) %collective-permute-start.5) | collective-permute-done | bytes 294944 | tf_op jit(solution)/shard_map/ppermute | solution.py:934
  30.5 4.8 %collective-permute-done.7.refs_1_ = bf16[4,96,256]{2,1,0:T(8,128)(2,1)S(1)} collective-permute-done((bf16[4,96,256]{2,1,0:T(8,128)(2,1)S(1)}, bf16[4,96,256]{2,1,0:T(8,128)(2,1)S(1)}, u32[]{:S(2)}, u32[]{:S(2)}) %collective-permute-start.7) | collective-permute-done | bytes 196640 | tf_op jit(solution)/shard_map/ppermute | solution.py:934
  42.9 8.5 %attend.3 = (bf16[64,1024]{1,0:T(8,128)(2,1)S(1)}, bf16[64,1024]{1,0:T(8,128)(2,1)S(1)}, f32[64,2048]{1,0:T(8,128)S(1)}, f32[1,2048]{1,0:T(1,128)S(1)}) custom-call(s32[145]{0:T(256)S(1)} %get-tuple-element.110.plan.refs_0_, bf16[512,768]{1,0:T(8,128)(2,1)S(1)} %copy-done.2, bf16[512,768]{1,0:T(8,128)(2,1)S(1)} %collective-permute-done.tok1.refs_3_, ...), custom_call_target="tpu_custom_call" | custom-call | flops 1 | bytes 1 | tf_op jit(solution)/shard_map/attend/pallas_call | solution.py:260
  54.6 2.2 collective-permute-start.10
  57.9 8.5 %attend.4 = (bf16[64,1024]{1,0:T(8,128)(2,1)S(1)}, bf16[64,1024]{1,0:T(8,128)(2,1)S(1)}, f32[64,2048]{1,0:T(8,128)S(1)}, f32[1,2048]{1,0:T(1,128)S(1)}) custom-call(s32[145]{0:T(256)S(1)} %get-tuple-element.110.plan.refs_0_, bf16[512,768]{1,0:T(8,128)(2,1)S(1)} %copy-done.2, bf16[512,768]{1,0:T(8,128)(2,1)S(1)} %collective-permute-done.tok1.refs_3_, ...), custom_call_target="tpu_custom_call" | custom-call | flops 1 | bytes 1 | tf_op jit(solution)/shard_map/attend/pallas_call | solution.py:260
  69.0 2.3 collective-permute-done.11
  73.9 8.9 %attend.5 = (bf16[64,1024]{1,0:T(8,128)(2,1)S(1)}, bf16[64,1024]{1,0:T(8,128)(2,1)S(1)}, f32[64,2048]{1,0:T(8,128)S(1)}, f32[1,2048]{1,0:T(1,128)S(1)}) custom-call(s32[145]{0:T(256)S(1)} %get-tuple-element.110.plan.refs_0_, bf16[512,768]{1,0:T(8,128)(2,1)S(1)} %copy-done.2, bf16[512,768]{1,0:T(8,128)(2,1)S(1)} %collective-permute-done.tok1.refs_3_, ...), custom_call_target="tpu_custom_call" | custom-call | flops 1 | bytes 1 | tf_op jit(solution)/shard_map/attend/pallas_call | solution.py:260
  82.8 3.7 %collective-permute-done.17 = bf16[2,192,768]{2,1,0:T(8,128)(2,1)S(1)} collective-permute-done((bf16[2,192,768]{2,1,0:T(8,128)(2,1)S(1)}, bf16[2,192,768]{2,1,0:T(8,128)(2,1)S(1)}, u32[]{:S(2)}, u32[]{:S(2)}) %collective-permute-start.17) | collective-permute-done | bytes 589856 | tf_op jit(solution)/shard_map/ppermute | solution.py:934
  92.9 2.5 collective-permute-done.18
  98.9 2.0 first_norm.1
  103.2 13.3 %collective-permute-done.24.refs_1_ = bf16[4,96,1536]{2,1,0:T(8,128)(2,1)} collective-permute-done((bf16[4,96,1536]{2,1,0:T(8,128)(2,1)}, bf16[4,96,1536]{2,1,0:T(8,128)(2,1)}, u32[]{:S(2)}, u32[]{:S(2)}) %collective-permute-start.24) | collective-permute-done | bytes 1179680 | tf_op jit(solution)/shard_map/ppermute | solution.py:934
  118.2 6.9 %feed_up.1 = (bf16[1024,1536]{1,0:T(8,128)(2,1)S(1)}, bf16[1536,1024]{1,0:T(8,128)(2,1)S(1)}, bf16[1024,1536]{1,0:T(8,128)(2,1)S(1)}, bf16[768,1024]{1,0:T(8,128)(2,1)S(1)}) custom-call(bf16[256,768]{1,0:T(8,128)(2,1)} %get-tuple-element.138.low0, bf16[256,768]{1,0:T(8,128)(2,1)} %get-tuple-element.139.low1, bf16[256,768]{1,0:T(8,128)(2,1)} %collective-permute-done.22.low2, ...), custom_call_target="tpu_custom_call" | custom-call | flops 1 | bytes 1 | tf_op jit(solution)/shard_map/feed_up/pallas_call | solution.py:541
  126.8 3.2 %feed_down.1 = (f32[512,768]{1,0:T(8,128)S(1)}, bf16[512,768]{1,0:T(8,128)(2,1)S(1)}) custom-call(bf16[1024,1536]{1,0:T(8,128)(2,1)S(1)} %get-tuple-element.141.act, bf16[1536,768]{1,0:T(8,128)(2,1)S(1)} %assemble.7.down), custom_call_target="tpu_custom_call" | custom-call | flops 1 | bytes 1 | tf_op jit(solution)/shard_map/feed_down/pallas_call | solution.py:582
  130.1 2.3 collective-permute-done.26.recv
  132.4 2.3 second_norm.1
  134.9 2.1 collective-permute-done.27.refs_3_.grad_other
  137.0 2.9 %weight_grad.2 = bf16[4,384,768]{2,1,0:T(8,128)(2,1)S(1)} custom-call(s32[1]{0:T(128)} %bitcast.12.refs_0_, bf16[1536,1024]{1,0:T(8,128)(2,1)S(1)} %get-tuple-element.149.refs_1_, bf16[512,768]{1,0:T(8,128)(2,1)S(1)} %get-tuple-element.150.refs_2_.grad_own, bf16[512,768]{1,0:T(8,128)(2,1)S(1)} %collective-permute-done.27.refs_3_.grad_other), custom_call_target="tpu_custom_call" | custom-call | flops 1 | bytes 1 | tf_op jit(solution)/shard_map/weight_grad/pallas_call | solution.py:677
  140.0 6.5 %feed_back.1 = (f32[512,768]{1,0:T(8,128)S(1)}, bf16[256,768]{1,0:T(8,128)(2,1)S(1)}, bf16[256,768]{1,0:T(8,128)(2,1)S(1)}, bf16[1024,1536]{1,0:T(8,128)(2,1)S(1)}) custom-call(bf16[512,768]{1,0:T(8,128)(2,1)S(1)} %get-tuple-element.150.refs_2_.grad_own, bf16[512,768]{1,0:T(8,128)(2,1)S(1)} %collective-permute-done.27.refs_3_.grad_other, ...), custom_call_target="tpu_custom_call" | custom-call | flops 1 | bytes 1 | tf_op jit(solution)/shard_map/feed_back/pallas_call | solution.py:626
  147.8 3.5 %weight_grad.3 = bf16[8,96,1536]{2,1,0:T(8,128)(2,1)S(1)} custom-call(s32[1]{0:T(128)} %bitcast.2.info.refs_0_, bf16[768,1024]{1,0:T(8,128)(2,1)S(1)} %get-tuple-element.155.refs_1_, bf16[1024,1536]{1,0:T(8,128)(2,1)S(1)} %get-tuple-element.156.refs_2_), custom_call_target="tpu_custom_call" | custom-call | flops 1 | bytes 1 | tf_op jit(solution)/shard_map/weight_grad/pallas_call | solution.py:677
  160.9 6.0 %collective-permute-done.32 = bf16[192,1024]{1,0:T(8,128)(2,1)S(1)} collective-permute-done((bf16[192,1024]{1,0:T(8,128)(2,1)S(1)}, bf16[192,1024]{1,0:T(8,128)(2,1)S(1)}, u32[]{:S(2)}, u32[]{:S(2)}) %collective-permute-start.32) | collective-permute-done | bytes 393248 | tf_op jit(solution)/shard_map/ppermute | solution.py:940
  166.9 13.5 %attend_back.3 = (bf16[192,1024]{1,0:T(8,128)(2,1)S(1)}, bf16[192,1024]{1,0:T(8,128)(2,1)S(1)}, bf16[8,96,640]{2,1,0:T(8,128)(2,1)S(1)}) custom-call(s32[145]{0:T(256)S(1)} %get-tuple-element.110.plan.refs_0_, s32[3]{0:T(128)S(1)} %pad_add_fusion.place.info.refs_1_, bf16[512,768]{1,0:T(8,128)(2,1)S(1)} %copy-done.2, ...), custom_call_target="tpu_custom_call" | custom-call | flops 1 | bytes 1 | tf_op jit(solution)/shard_map/attend_back/pallas_call | solution.py:396
  186.3 13.3 %attend_back.4 = (bf16[192,1024]{1,0:T(8,128)(2,1)S(1)}, bf16[192,1024]{1,0:T(8,128)(2,1)S(1)}, bf16[8,96,256]{2,1,0:T(8,128)(2,1)S(1)}) custom-call(s32[145]{0:T(256)S(1)} %get-tuple-element.110.plan.refs_0_, s32[3]{0:T(128)S(1)} %pad_add_fusion.place.info.refs_1_, bf16[512,768]{1,0:T(8,128)(2,1)S(1)} %copy-done.2, ...), custom_call_target="tpu_custom_call" | custom-call | flops 1 | bytes 1 | tf_op jit(solution)/shard_map/attend_back/pallas_call | solution.py:396
  201.6 13.3 %attend_back.5 = (bf16[192,1024]{1,0:T(8,128)(2,1)S(1)}, bf16[192,1024]{1,0:T(8,128)(2,1)S(1)}, bf16[8,96,512]{2,1,0:T(8,128)(2,1)S(1)}) custom-call(s32[145]{0:T(256)S(1)} %get-tuple-element.110.plan.refs_0_, s32[3]{0:T(128)S(1)} %pad_add_fusion.place.info.refs_1_, bf16[512,768]{1,0:T(8,128)(2,1)S(1)} %copy-done.2, ...), custom_call_target="tpu_custom_call" | custom-call | flops 1 | bytes 1 | tf_op jit(solution)/shard_map/attend_back/pallas_call | solution.py:396
  218.2 8.8 %collective-permute-done.40.refs_5_ = bf16[192,1024]{1,0:T(8,128)(2,1)S(1)} collective-permute-done((bf16[192,1024]{1,0:T(8,128)(2,1)S(1)}, bf16[192,1024]{1,0:T(8,128)(2,1)S(1)}, u32[]{:S(2)}, u32[]{:S(2)}) %collective-permute-start.40) | collective-permute-done | bytes 393248 | tf_op jit(solution)/shard_map/ppermute | solution.py:940
  228.1 3.6 %input_back.1 = (f32[512,768]{1,0:T(8,128)S(1)}, bf16[512,768]{1,0:T(8,128)(2,1)S(1)}) custom-call(bf16[192,1024]{1,0:T(8,128)(2,1)S(1)} %get-tuple-element.171.refs_0_, bf16[192,1024]{1,0:T(8,128)(2,1)S(1)} %get-tuple-element.178.refs_1_, bf16[192,1024]{1,0:T(8,128)(2,1)S(1)} %get-tuple-element.187.refs_2_, ...), custom_call_target="tpu_custom_call" | custom-call | flops 1 | bytes 1 | tf_op jit(solution)/shard_map/input_back/pallas_call | solution.py:452
  231.8 4.0 %collective-permute-done.45 = bf16[2,96,512]{2,1,0:T(8,128)(2,1)S(1)} collective-permute-done((bf16[2,96,512]{2,1,0:T(8,128)(2,1)S(1)}, bf16[2,96,512]{2,1,0:T(8,128)(2,1)S(1)}, u32[]{:S(2)}, u32[]{:S(2)}) %collective-permute-start.45) | collective-permute-done | bytes 196640 | tf_op jit(solution)/shard_map/ppermute | solution.py:934
  241.5 5.7 %collective-permute-done.48 = bf16[1,96,640]{2,1,0:T(8,128)(2,1)S(1)} collective-permute-done((bf16[1,96,640]{2,1,0:T(8,128)(2,1)S(1)}, bf16[1,96,640]{2,1,0:T(8,128)(2,1)S(1)}, u32[]{:S(2)}, u32[]{:S(2)}) %collective-permute-start.48) | collective-permute-done | bytes 122912 | tf_op jit(solution)/shard_map/ppermute | solution.py:934
  247.2 2.0 collective-permute-done.51
  249.3 2.3 collective-permute-start.52
  (239 shorter events, 87.1 us)
Async XLA Ops:
  6.8 21.1 %collective-permute-start.1 = (bf16[512,768]{1,0:T(8,128)(2,1)}, bf16[512,768]{1,0:T(8,128)(2,1)S(1)}, u32[]{:S(2)}, u32[]{:S(2)}) collective-permute-start(bf16[512,768]{1,0:T(8,128)(2,1)} %refs_2_.5), channel_id=1, source_target_pairs={{0,2},{1,3},{2,0},{3,1},{4,6},{5,7},{6,4},{7,5},{8,10},{9,11},{10,... | collective-permute-start | bytes 2359304 | tf_op jit(solution)/shard_map/ppermute | solution.py:940
  21.7 21.1 %collective-permute-start = (bf16[512,768]{1,0:T(8,128)(2,1)S(1)}, bf16[512,768]{1,0:T(8,128)(2,1)S(1)}, u32[]{:S(2)}, u32[]{:S(2)}) collective-permute-start(bf16[512,768]{1,0:T(8,128)(2,1)S(1)} %copy-done.2), channel_id=1, source_target_pairs={{0,1},{1,0},{2,3},{3,2},{4,5},{5,4},{6,7},{7,6},{8,9},{9,8},{10,11... | collective-permute-start | bytes 2359304 | tf_op jit(solution)/shard_map/ppermute | solution.py:937
  27.9 15.0 %collective-permute-start.6 = (bf16[512,768]{1,0:T(8,128)(2,1)S(1)}, bf16[512,768]{1,0:T(8,128)(2,1)}, u32[]{:S(2)}, u32[]{:S(2)}) collective-permute-start(bf16[512,768]{1,0:T(8,128)(2,1)S(1)} %collective-permute-done.1.tok2.refs_4_), channel_id=1, source_target_pairs={{0,1},{1,0},{2,3},{3,2},{4,5},{5,4},{6,7},{7,6},{8,9},{9,8},{10,11... | collective-permute-start | bytes 2359304 | tf_op jit(solution)/shard_map/ppermute | solution.py:937
  36.0 15.6 %collective-permute-start.8 = (bf16[4,96,768]{2,1,0:T(8,128)(2,1)S(1)}, bf16[4,96,768]{2,1,0:T(8,128)(2,1)}, u32[]{:S(2)}, u32[]{:S(2)}) collective-permute-start(bf16[4,96,768]{2,1,0:T(8,128)(2,1)S(1)} %pad_maximum_fusion.2.refs_0_), channel_id=1, source_target_pairs={{0,4},{4,0},{8,12},{12,8},{16,20},{20,16},{24,28},{28,24},{1,5},{5... | collective-permute-start | bytes 1769480 | tf_op jit(solution)/shard_map/ppermute | solution.py:934
  37.5 13.9 %collective-permute-start.9 = (bf16[192,768]{1,0:T(8,128)(2,1)}, bf16[192,768]{1,0:T(8,128)(2,1)}, u32[]{:S(2)}, u32[]{:S(2)}) collective-permute-start(bf16[192,768]{1,0:T(8,128)(2,1)} %constant_dynamic-slice_fusion), channel_id=1, source_target_pairs={{0,16},{1,0},{2,18},{3,2},{4,20},{5,4},{6,22},{7,6},{8,24},{9,8},{... | collective-permute-start | bytes 884744 | tf_op jit(solution)/shard_map/ppermute | solution.py:948
  41.4 31.0 %collective-permute-start.12 = (bf16[768,256]{1,0:T(8,128)(2,1)S(1)}, bf16[768,256]{1,0:T(8,128)(2,1)S(1)}, u32[]{:S(2)}, u32[]{:S(2)}) collective-permute-start(bf16[768,256]{1,0:T(8,128)(2,1)S(1)} %assemble.4.part), channel_id=1, source_target_pairs={{0,2},{1,3},{2,0},{3,1},{4,6},{5,7},{6,4},{7,5},{8,10},{9,11},{10,... | collective-permute-start | bytes 1179656 | tf_op jit(solution)/shard_map/ppermute | solution.py:940
  54.5 16.8 %collective-permute-start.11 = (bf16[1,96,1536]{2,1,0:T(8,128)(2,1)S(1)}, bf16[1,96,1536]{2,1,0:T(8,128)(2,1)S(1)}, u32[]{:S(2)}, u32[]{:S(2)}) collective-permute-start(bf16[1,96,1536]{2,1,0:T(8,128)(2,1)S(1)} %copy-done.28), channel_id=1, source_target_pairs={{0,16},{4,20},{8,24},{12,28},{16,0},{20,4},{24,8},{28,12},{1,17},{... | collective-permute-start | bytes 884744 | tf_op jit(solution)/shard_map/ppermute | solution.py:934
  54.6 13.7 %collective-permute-start.10 = (bf16[1,192,768]{2,1,0:T(8,128)(2,1)S(1)}, bf16[1,192,768]{2,1,0:T(8,128)(2,1)S(1)}, u32[]{:S(2)}, u32[]{:S(2)}) collective-permute-start(bf16[1,192,768]{2,1,0:T(8,128)(2,1)S(1)} %select_bitcast_fusion), channel_id=1, source_target_pairs={{0,8},{4,12},{8,0},{12,4},{16,24},{20,28},{24,16},{28,20},{1,9},{5... | collective-permute-start | bytes 884744 | tf_op jit(solution)/shard_map/ppermute | solution.py:934
  56.8 17.1 %collective-permute-start.13 = (bf16[768,384]{1,0:T(8,128)(2,1)S(1)}, bf16[768,384]{1,0:T(8,128)(2,1)S(1)}, u32[]{:S(2)}, u32[]{:S(2)}) collective-permute-start(bf16[768,384]{1,0:T(8,128)(2,1)S(1)} %slice.223), channel_id=1, source_target_pairs={{0,2},{1,3},{2,0},{3,1},{4,6},{5,7},{6,4},{7,5},{8,10},{9,11},{10,... | collective-permute-start | bytes 1769480 | tf_op jit(solution)/shard_map/ppermute | solution.py:940
  57.8 13.9 %collective-permute-start.19 = (bf16[384,384]{1,0:T(8,128)(2,1)S(1)}, bf16[384,384]{1,0:T(8,128)(2,1)S(1)}, u32[]{:S(2)}, u32[]{:S(2)}) collective-permute-start(bf16[384,384]{1,0:T(8,128)(2,1)S(1)} %get-tuple-element.217), channel_id=1, source_target_pairs={{0,1},{1,0},{2,3},{3,2},{4,5},{5,4},{6,7},{7,6},{8,9},{9,8},{10,11... | collective-permute-start | bytes 884744 | tf_op jit(solution)/shard_map/ppermute | solution.py:937
  68.3 21.3 %collective-permute-start.14 = (bf16[64,1024]{1,0:T(8,128)(2,1)S(1)}, bf16[64,1024]{1,0:T(8,128)(2,1)S(1)}, u32[]{:S(2)}, u32[]{:S(2)}) collective-permute-start(bf16[64,1024]{1,0:T(8,128)(2,1)S(1)} %get-tuple-element.131), channel_id=1, source_target_pairs={{0,2},{1,3},{2,0},{3,1},{4,6},{5,7},{6,4},{7,5},{8,10},{9,11},{10,... | collective-permute-start | bytes 393224 | tf_op jit(solution)/shard_map/ppermute | solution.py:940
  71.3 15.3 %collective-permute-start.17 = (bf16[2,192,768]{2,1,0:T(8,128)(2,1)S(1)}, bf16[2,192,768]{2,1,0:T(8,128)(2,1)S(1)}, u32[]{:S(2)}, u32[]{:S(2)}) collective-permute-start(bf16[2,192,768]{2,1,0:T(8,128)(2,1)S(1)} %pad_maximum_fusion.3), channel_id=1, source_target_pairs={{0,4},{4,0},{8,12},{12,8},{16,20},{20,16},{24,28},{28,24},{1,5},{5... | collective-permute-start | bytes 1769480 | tf_op jit(solution)/shard_map/ppermute | solution.py:934
  71.7 15.1 %collective-permute-start.16 = (bf16[2,96,1536]{2,1,0:T(8,128)(2,1)S(1)}, bf16[2,96,1536]{2,1,0:T(8,128)(2,1)S(1)}, u32[]{:S(2)}, u32[]{:S(2)}) collective-permute-start(bf16[2,96,1536]{2,1,0:T(8,128)(2,1)S(1)} %pad_maximum_fusion.4), channel_id=1, source_target_pairs={{0,8},{4,12},{8,0},{12,4},{16,24},{20,28},{24,16},{28,20},{1,9},{5... | collective-permute-start | bytes 1769480 | tf_op jit(solution)/shard_map/ppermute | solution.py:934
  72.5 17.1 %collective-permute-start.15 = (bf16[64,1024]{1,0:T(8,128)(2,1)S(1)}, bf16[64,1024]{1,0:T(8,128)(2,1)S(1)}, u32[]{:S(2)}, u32[]{:S(2)}) collective-permute-start(bf16[64,1024]{1,0:T(8,128)(2,1)S(1)} %get-tuple-element.132), channel_id=1, source_target_pairs={{0,2},{1,3},{2,0},{3,1},{4,6},{5,7},{6,4},{7,5},{8,10},{9,11},{10,... | collective-permute-start | bytes 393224 | tf_op jit(solution)/shard_map/ppermute | solution.py:940
  89.6 26.9 %collective-permute-start.24 = (bf16[4,96,1536]{2,1,0:T(8,128)(2,1)}, bf16[4,96,1536]{2,1,0:T(8,128)(2,1)}, u32[]{:S(2)}, u32[]{:S(2)}) collective-permute-start(bf16[4,96,1536]{2,1,0:T(8,128)(2,1)} %pad_maximum_fusion.refs_0_), channel_id=1, source_target_pairs={{0,4},{4,0},{8,12},{12,8},{16,20},{20,16},{24,28},{28,24},{1,5},{5... | collective-permute-start | bytes 3538952 | tf_op jit(solution)/shard_map/ppermute | solution.py:934
  91.3 33.8 %collective-permute-start.25 = (bf16[4,192,768]{2,1,0:T(8,128)(2,1)}, bf16[4,192,768]{2,1,0:T(8,128)(2,1)}, u32[]{:S(2)}, u32[]{:S(2)}) collective-permute-start(bf16[4,192,768]{2,1,0:T(8,128)(2,1)} %pad_maximum_fusion.1.refs_0_), channel_id=1, source_target_pairs={{0,2},{1,3},{2,0},{3,1},{4,6},{5,7},{6,4},{7,5},{8,10},{9,11},{10,... | collective-permute-start | bytes 3538952 | tf_op jit(solution)/shard_map/ppermute | solution.py:940
  102.7 15.5 %collective-permute-start.22 = (bf16[256,768]{1,0:T(8,128)(2,1)}, bf16[256,768]{1,0:T(8,128)(2,1)}, u32[]{:S(2)}, u32[]{:S(2)}) collective-permute-start(bf16[256,768]{1,0:T(8,128)(2,1)} %get-tuple-element.138.low0), channel_id=1, source_target_pairs={{0,1},{1,0},{2,3},{3,2},{4,5},{5,4},{6,7},{7,6},{8,9},{9,8},{10,11... | collective-permute-start | bytes 1179656 | tf_op jit(solution)/shard_map/ppermute | solution.py:937
  102.8 15.4 %collective-permute-start.23 = (bf16[256,768]{1,0:T(8,128)(2,1)}, bf16[256,768]{1,0:T(8,128)(2,1)}, u32[]{:S(2)}, u32[]{:S(2)}) collective-permute-start(bf16[256,768]{1,0:T(8,128)(2,1)} %get-tuple-element.139.low1), channel_id=1, source_target_pairs={{0,1},{1,0},{2,3},{3,2},{4,5},{5,4},{6,7},{7,6},{8,9},{9,8},{10,11... | collective-permute-start | bytes 1179656 | tf_op jit(solution)/shard_map/ppermute | solution.py:937
  147.1 33.3 %collective-permute-start.34 = (bf16[2,384,768]{2,1,0:T(8,128)(2,1)S(1)}, bf16[2,384,768]{2,1,0:T(8,128)(2,1)S(1)}, u32[]{:S(2)}, u32[]{:S(2)}) collective-permute-start(bf16[2,384,768]{2,1,0:T(8,128)(2,1)S(1)} %slice.232), channel_id=1, source_target_pairs={{0,8},{4,12},{8,0},{12,4},{16,24},{20,28},{24,16},{28,20},{1,9},{5... | collective-permute-start | bytes 3538952 | tf_op jit(solution)/shard_map/ppermute | solution.py:934
  153.2 28.0 %collective-permute-start.35 = (bf16[4,96,1536]{2,1,0:T(8,128)(2,1)S(1)}, bf16[4,96,1536]{2,1,0:T(8,128)(2,1)S(1)}, u32[]{:S(2)}, u32[]{:S(2)}) collective-permute-start(bf16[4,96,1536]{2,1,0:T(8,128)(2,1)S(1)} %slice.234), channel_id=1, source_target_pairs={{0,4},{4,0},{8,12},{12,8},{16,20},{20,16},{24,28},{28,24},{1,5},{5... | collective-permute-start | bytes 3538952 | tf_op jit(solution)/shard_map/ppermute | solution.py:934
  181.2 18.9 %collective-permute-start.36 = (bf16[1,384,768]{2,1,0:T(8,128)(2,1)S(1)}, bf16[1,384,768]{2,1,0:T(8,128)(2,1)S(1)}, u32[]{:S(2)}, u32[]{:S(2)}) collective-permute-start(bf16[1,384,768]{2,1,0:T(8,128)(2,1)S(1)} %slice.237), channel_id=1, source_target_pairs={{0,4},{4,0},{8,12},{12,8},{16,20},{20,16},{24,28},{28,24},{1,5},{5... | collective-permute-start | bytes 1769480 | tf_op jit(solution)/shard_map/ppermute | solution.py:934
  183.2 17.1 %collective-permute-start.37 = (bf16[2,96,1536]{2,1,0:T(8,128)(2,1)S(1)}, bf16[2,96,1536]{2,1,0:T(8,128)(2,1)S(1)}, u32[]{:S(2)}, u32[]{:S(2)}) collective-permute-start(bf16[2,96,1536]{2,1,0:T(8,128)(2,1)S(1)} %slice.239), channel_id=1, source_target_pairs={{0,8},{4,12},{8,0},{12,4},{16,24},{20,28},{24,16},{28,20},{1,9},{5... | collective-permute-start | bytes 1769480 | tf_op jit(solution)/shard_map/ppermute | solution.py:934
  184.7 15.6 %collective-permute-start.38 = (bf16[192,1024]{1,0:T(8,128)(2,1)S(1)}, bf16[192,1024]{1,0:T(8,128)(2,1)S(1)}, u32[]{:S(2)}, u32[]{:S(2)}) collective-permute-start(bf16[192,1024]{1,0:T(8,128)(2,1)S(1)} %get-tuple-element.181), channel_id=1, source_target_pairs={{0,2},{1,3},{2,0},{3,1},{4,6},{5,7},{6,4},{7,5},{8,10},{9,11},{10,... | collective-permute-start | bytes 1179656 | tf_op jit(solution)/shard_map/ppermute | solution.py:940
  199.6 17.0 %collective-permute-start.39 = (bf16[192,1024]{1,0:T(8,128)(2,1)S(1)}, bf16[192,1024]{1,0:T(8,128)(2,1)S(1)}, u32[]{:S(2)}, u32[]{:S(2)}) collective-permute-start(bf16[192,1024]{1,0:T(8,128)(2,1)S(1)} %get-tuple-element.188), channel_id=1, source_target_pairs={{0,2},{1,3},{2,0},{3,1},{4,6},{5,7},{6,4},{7,5},{8,10},{9,11},{10,... | collective-permute-start | bytes 1179656 | tf_op jit(solution)/shard_map/ppermute | solution.py:940
  200.5 16.1 %collective-permute-start.41 = (bf16[1,96,1536]{2,1,0:T(8,128)(2,1)S(1)}, bf16[1,96,1536]{2,1,0:T(8,128)(2,1)S(1)}, u32[]{:S(2)}, u32[]{:S(2)}) collective-permute-start(bf16[1,96,1536]{2,1,0:T(8,128)(2,1)S(1)} %slice.242), channel_id=1, source_target_pairs={{0,16},{4,20},{8,24},{12,28},{16,0},{20,4},{24,8},{28,12},{1,17},{... | collective-permute-start | bytes 884744 | tf_op jit(solution)/shard_map/ppermute | solution.py:934
  200.6 16.1 %collective-permute-start.42 = (bf16[4,96,640]{2,1,0:T(8,128)(2,1)S(1)}, bf16[4,96,640]{2,1,0:T(8,128)(2,1)S(1)}, u32[]{:S(2)}, u32[]{:S(2)}) collective-permute-start(bf16[4,96,640]{2,1,0:T(8,128)(2,1)S(1)} %slice.196), channel_id=1, source_target_pairs={{0,4},{4,0},{8,12},{12,8},{16,20},{20,16},{24,28},{28,24},{1,5},{5... | collective-permute-start | bytes 1474568 | tf_op jit(solution)/shard_map/ppermute | solution.py:934
  217.6 18.4 %collective-permute-start.49 = (bf16[384,768]{1,0:T(8,128)(2,1)S(1)}, bf16[384,768]{1,0:T(8,128)(2,1)S(1)}, u32[]{:S(2)}, u32[]{:S(2)}) collective-permute-start(bf16[384,768]{1,0:T(8,128)(2,1)S(1)} %fusion), channel_id=1, source_target_pairs={{0,1},{1,17},{2,3},{3,19},{4,5},{5,21},{6,7},{7,23},{8,9},{9,25},{... | collective-permute-start | bytes 1769480 | tf_op jit(solution)/shard_map/ppermute | solution.py:948
  217.6 14.2 %collective-permute-start.46 = (bf16[96,1536]{1,0:T(8,128)(2,1)S(1)}, bf16[96,1536]{1,0:T(8,128)(2,1)S(1)}, u32[]{:S(2)}, u32[]{:S(2)}) collective-permute-start(bf16[96,1536]{1,0:T(8,128)(2,1)S(1)} %fusion.3), channel_id=1, source_target_pairs={{0,2},{1,3},{2,0},{3,1},{4,6},{5,7},{6,4},{7,5},{8,10},{9,11},{10,... | collective-permute-start | bytes 884744 | tf_op jit(solution)/shard_map/ppermute | solution.py:940
  218.0 17.9 %collective-permute-start.47 = (bf16[2,96,640]{2,1,0:T(8,128)(2,1)S(1)}, bf16[2,96,640]{2,1,0:T(8,128)(2,1)S(1)}, u32[]{:S(2)}, u32[]{:S(2)}) collective-permute-start(bf16[2,96,640]{2,1,0:T(8,128)(2,1)S(1)} %slice.248), channel_id=1, source_target_pairs={{0,8},{4,12},{8,0},{12,4},{16,24},{20,28},{24,16},{28,20},{1,9},{5... | collective-permute-start | bytes 737288 | tf_op jit(solution)/shard_map/ppermute | solution.py:934
  231.7 21.2 %collective-permute-start.44 = (bf16[512,768]{1,0:T(8,128)(2,1)S(1)}, bf16[512,768]{1,0:T(8,128)(2,1)S(1)}, u32[]{:S(2)}, u32[]{:S(2)}) collective-permute-start(bf16[512,768]{1,0:T(8,128)(2,1)S(1)} %get-tuple-element.198), channel_id=1, source_target_pairs={{0,1},{1,0},{2,3},{3,2},{4,5},{5,4},{6,7},{7,6},{8,9},{9,8},{10,11... | collective-permute-start | bytes 2359304 | tf_op jit(solution)/shard_map/ppermute | solution.py:937
  236.3 15.3 %collective-permute-start.55 = (bf16[96,1536]{1,0:T(8,128)(2,1)S(1)}, bf16[96,1536]{1,0:T(8,128)(2,1)S(1)}, u32[]{:S(2)}, u32[]{:S(2)}) collective-permute-start(bf16[96,1536]{1,0:T(8,128)(2,1)S(1)} %add_convert_fusion.7), channel_id=1, source_target_pairs={{0,1},{1,0},{2,3},{3,2},{4,5},{5,4},{6,7},{7,6},{8,9},{9,8},{10,11... | collective-permute-start | bytes 884744 | tf_op jit(solution)/shard_map/ppermute | solution.py:937
  239.8 12.9 %collective-permute-start.53 = (bf16[192,768]{1,0:T(8,128)(2,1)S(1)}, bf16[192,768]{1,0:T(8,128)(2,1)S(1)}, u32[]{:S(2)}, u32[]{:S(2)}) collective-permute-start(bf16[192,768]{1,0:T(8,128)(2,1)S(1)} %select_select_fusion), channel_id=1, source_target_pairs={{0,2},{1,3},{2,0},{3,1},{4,6},{5,7},{6,4},{7,5},{8,10},{9,11},{10,... | collective-permute-start | bytes 884744 | tf_op jit(solution)/shard_map/ppermute | solution.py:940
  (57 other events, 376.0 us)
where the time goes:
time: 263 us
  Pallas kernels  112 us (43%)
  waiting for transfers between devices  76.6 us (29%)
  starting transfers between devices  49.4 us (19%)
  local copies, waits for them, and re-layouts  11 us (4%)
  other arithmetic  10.3 us (4%)
    ppermute x22, waiting for transfers between devices, swap(): return lax.ppermute(value, 'shard', [(i, i ^ mask) for i in range(n_shard)])  48.2 us
    pallas_call x3, Pallas kernels, attend_back(): pl.pallas_call(kernel, out_shape=(shape((TRIO, total // 2), BF),) * 2 + (...  40.1 us
    ppermute x22, starting transfers between devices, swap(): return lax.ppermute(value, 'shard', [(i, i ^ mask) for i in range(n_shard)])  27.7 us
    pallas_call x3, Pallas kernels, attend(): pl.pallas_call(attend_kernel, out_shape=(shape((HEAD_DIM, half), BF), sha...  25.9 us
    ppermute x14, waiting for transfers between devices, swap_x(): return lax.ppermute(value, 'seq', [(i, i ^ 2) for i in range(4)])  18.9 us
    ppermute x14, starting transfers between devices, swap_x(): return lax.ppermute(value, 'seq', [(i, i ^ 2) for i in range(4)])  17.7 us
    ppermute x19, waiting for transfers between devices, swap_core(): return lax.ppermute(value, 'seq', [(i, i ^ 1) for i in range(4)])  9.5 us
    pallas_call x1, Pallas kernels, feed_up(): pl.pallas_call(feed_up_kernel, out_shape=(shape((4 * rows, hidden), BF),...  6.87 us
  transfers between devices with their start and end apart: 57, of which 24 were waited for; matrix products, arithmetic and copies ran while one was open for 5% of the time, Pallas kernels for 35%

commit v1 on v0

--- a/solution.py
+++ b/solution.py
@@ -62,13 +62,13 @@
     return pl.pallas_call(
         partial(assemble_kernel, offsets),
         out_shape=shape((count * block, cols), BF),
-        in_specs=[SMEM] + [pl.BlockSpec(memory_space=pl.ANY)] * len(pieces),
+        in_specs=[SMEM] + [pl.BlockSpec(memory_space=pltpu.HBM)] * len(pieces),
         out_specs=VMEM,
         scratch_shapes=[pltpu.SemaphoreType.DMA((count,))],
         compiler_params=params(12),
         cost_estimate=FREE,
         name="assemble",
-    )(me[None], *pieces)
+    )(me[None], *[pltpu.with_memory_space_constraint(p, pltpu.HBM) for p in pieces])
 
 
 def prepare_kernel(info, qkv_far, out_far, *refs):
@@ -1013,10 +1013,11 @@
     b2 = gather_b.steps(middle, a2, up_half, down_half)
     d1 = to_core(after(down_half, b1), False)
     toks.append(swap_core(after(over_x, b2)))
-    b3 = gather_b.steps(1, a3)
+    b2 = after(b2, a3)
+    gather_b.pieces[1] = b2
+    b3 = gather_b.steps(1)
     part_a = assemble(gather_a.pieces, gather_a.offsets, shard)
     vectors = vectors_of(part_a)
-    far_a = swap_x(part_a)
 
     saved, own_ctx, sends = [], [], []
 
@@ -1029,31 +1030,29 @@
         saved.append((ctx_full, lse))
         return ctx_own
 
-    ctx = head(0, part_a[:, :TRIO], b2, vectors)
-    d1, b3 = after(d1, ctx), after(b3, ctx)
-    gather_b.pieces[1] = b3
     gather_down = Gather(jnp.where(owner, down_half, d1), bits[-2::-1])
     d2 = gather_down.steps(middle)
-    u1 = gather_up.steps(1, ctx)
-    part_b = assemble(gather_b.pieces, gather_b.offsets, shard)
-    far_b = swap_x(part_b[:, : 2 * TRIO])
-    ctx = head(1, part_b[:, :TRIO], gather_down.pieces[0])
-    d2, u1 = after(d2, ctx), after(u1, ctx)
-    gather_down.pieces[1], gather_up.pieces[1] = d2, u1
+    u1 = gather_up.steps(1, gather_down.pieces[0])
+    ctx = head(0, part_a[:, :TRIO], b2, vectors, gather_down.pieces[0])
+    b3, d2, u1 = after(b3, ctx), after(d2, ctx), after(u1, ctx)
+    gather_b.pieces[1], gather_down.pieces[1], gather_up.pieces[1] = b3, d2, u1
     d3 = gather_down.steps(1)
     u2 = gather_up.steps(middle)
-    ctx = head(2, part_b[:, TRIO : 2 * TRIO], gather_down.pieces[0], gather_up.pieces[0], far_a, far_b)
+    part_b = assemble(gather_b.pieces, gather_b.offsets, shard)
+    far_a = swap_x(after(part_a, ctx))
+    far_b = swap_x(part_b[:, : 2 * TRIO])
+    ctx = head(1, part_b[:, :TRIO], gather_down.pieces[0], gather_up.pieces[0])
     d3, u2 = after(d3, ctx), after(u2, ctx)
     gather_down.pieces[1], gather_up.pieces[1] = d3, u2
     held_up = join(gather_up.pieces)
+    gather_up.offsets = [[r for o in gather_up.offsets for r in o]]
+    gather_up.pieces = [held_up]
+    u3 = gather_up.part(0)
     held = join(gather_down.pieces)
-    gather_up.offsets = [[r for o in gather_up.offsets for r in o]]
-    sends[2], held_up, held = lax.optimization_barrier((sends[2], held_up, held))
-    gather_up.pieces = [held_up]
-    gather_up.part(0)
+    ctx = head(2, part_b[:, TRIO : 2 * TRIO], held_up, held)
+    sends[2], held, far_a, far_b = lax.optimization_barrier((sends[2], held, far_a, far_b))
     others = [swap_x(value) for value in sends]
     rel = [2 * r for o in gather_down.offsets for r in o]
-    widen = assemble(gather_up.pieces, gather_up.offsets, shard)
     held_far = swap_x(held)
     head_weights = [part_a[:, :TRIO], part_b[:, :TRIO], part_b[:, TRIO : 2 * TRIO]]
     far_weights = [far_a, far_b[:, :TRIO], far_b[:, TRIO:]]
@@ -1062,13 +1061,14 @@
     mixer = jnp.where(xb == 0, mixer, jnp.concatenate([mixer[quarter:], mixer[:quarter]]))
     context = jnp.concatenate(own_ctx + others)
 
-    mixed = dot(context, mixer, 0, 0)
+    mixed = after(dot(context, mixer, 0, 0), u3)
+    recv0, recv1 = [
+        swap_core(mixed[at : at + rows // 2].astype(BF)) for at in (rows, rows + rows // 2)
+    ]
     low0, low1, normed_one, inverse_one = first_norm(
-        tokens,
-        mixed,
-        [swap_core(mixed[at : at + rows // 2].astype(BF)) for at in (rows, rows + rows // 2)],
-        vectors,
+        tokens, mixed, [recv0, recv1], vectors
     )
+    widen = assemble(gather_up.pieces, gather_up.offsets, shard)
     act_low, act_t, slope, low_t = feed_up([low0, low1, swap_core(low0), swap_core(low1)], widen)
     held_far = after(held_far, act_low)
     narrow = assemble([held, held_far], [rel, [r + 1 for r in rel]], low_shard * 2 + xb)

time: 263 us -> 258 us (0.981)
  waiting for transfers between devices: 76.6 us -> 66.4 us
  starting transfers between devices: 49.4 us -> 56.2 us
  local copies, waits for them, and re-layouts: 11 us -> 6.33 us
  other arithmetic: 10.3 us -> 14.8 us
    ppermute x22, waiting for transfers between devices: 48.2 us -> 31.7 us  [swap(): return lax.ppermute(value, 'shard', [(i, i ^ mask) for i in range(n_shard)])]
    ppermute x22, starting transfers between devices: 27.7 us -> 34.9 us  [swap(): return lax.ppermute(value, 'shard', [(i, i ^ mask) for i in range(n_shard)])]
    ppermute x2, waiting for transfers between devices: 0.01 us -> 4.57 us  [to_core(): return lax.ppermute(value, ('shard', 'seq'), pairs)]
    unnamed x69 -> x65, local copies, waits for them, and re-layouts: 6.82 us -> 2.89 us
    concatenate x8, other arithmetic: 3.4 us -> 6.15 us  [join(): return jnp.concatenate(pieces) if len(pieces) > 1 else pieces[0]]
  transfers between devices with their start and end apart: 57 -> 57, of which waited for: 24 -> 25; matrix products, arithmetic and copies ran while one was open for 5% -> 7% of each run, Pallas kernels for 35% -> 35%
where the time goes in v1:
time: 258 us; the launch traced here: 257 us
  Pallas kernels  110 us (43%)
  waiting for transfers between devices  66.4 us (26%)
  starting transfers between devices  56.2 us (22%)
  other arithmetic  14.8 us (6%)
  local copies, waits for them, and re-layouts  6.33 us (2%)
    pallas_call x3, Pallas kernels, attend_back(): pl.pallas_call(kernel, out_shape=(shape((TRIO, total // 2), BF),) * 2 + (...  38.8 us
    ppermute x22, starting transfers between devices, swap(): return lax.ppermute(value, 'shard', [(i, i ^ mask) for i in range(n_shard)])  34.9 us
    ppermute x22, waiting for transfers between devices, swap(): return lax.ppermute(value, 'shard', [(i, i ^ mask) for i in range(n_shard)])  31.7 us
    pallas_call x3, Pallas kernels, attend(): pl.pallas_call(attend_kernel, out_shape=(shape((HEAD_DIM, half), BF), sha...  24.8 us
    ppermute x14, waiting for transfers between devices, swap_x(): return lax.ppermute(value, 'seq', [(i, i ^ 2) for i in range(4)])  19.7 us
    ppermute x14, starting transfers between devices, swap_x(): return lax.ppermute(value, 'seq', [(i, i ^ 2) for i in range(4)])  16.8 us
    ppermute x19, waiting for transfers between devices, swap_core(): return lax.ppermute(value, 'seq', [(i, i ^ 1) for i in range(4)])  10.4 us
    pallas_call x1, Pallas kernels, feed_up(): pl.pallas_call(feed_up_kernel, out_shape=(shape((4 * rows, hidden), BF),...  6.87 us
  transfers between devices with their start and end apart: 57, of which 25 were waited for; matrix products, arithmetic and copies ran while one was open for 7% of the time, Pallas kernels for 35%

profile of v1, /device:TPU:0, one launch (start us, length us, event | category | flops | bytes accessed | tf_op | source)
XLA Modules:
  0.0 256.6 jit_solution(8354378317407894565)
XLA Ops:
  2.7 4.1 %collective-permute-start.2 = (bf16[1,96,256]{2,1,0:T(8,128)(2,1)S(1)}, bf16[1,96,256]{2,1,0:T(8,128)(2,1)S(1)}, u32[]{:S(2)}, u32[]{:S(2)}) collective-permute-start(bf16[1,96,256]{2,1,0:T(8,128)(2,1)S(1)} %bitcast.32), channel_id=1, source_target_pairs={{0,16},{4,20},{8,24},{12,28},{16,0},{20,4},{24,8},{28,12},{1,17},{... | collective-permute-start | bytes 147464 | tf_op jit(solution)/shard_map/ppermute | solution.py:934
  9.4 2.4 collective-permute-start.3
  15.1 2.0 collective-permute-start.4
  17.9 2.0 collective-permute-done.4
  23.3 4.5 %collective-permute-done.5 = bf16[2,96,768]{2,1,0:T(8,128)(2,1)S(1)} collective-permute-done((bf16[2,96,768]{2,1,0:T(8,128)(2,1)S(1)}, bf16[2,96,768]{2,1,0:T(8,128)(2,1)S(1)}, u32[]{:S(2)}, u32[]{:S(2)}) %collective-permute-start.5) | collective-permute-done | bytes 294944 | tf_op jit(solution)/shard_map/ppermute | solution.py:934
  31.3 4.6 %collective-permute-done.8 = bf16[192,768]{1,0:T(8,128)(2,1)} collective-permute-done((bf16[192,768]{1,0:T(8,128)(2,1)}, bf16[192,768]{1,0:T(8,128)(2,1)}, u32[]{:S(2)}, u32[]{:S(2)}) %collective-permute-start.8) | collective-permute-done | bytes 294944 | tf_op jit(solution)/shard_map/ppermute | solution.py:948
  37.6 3.5 %collective-permute-start.11 = (bf16[1,96,1536]{2,1,0:T(8,128)(2,1)S(1)}, bf16[1,96,1536]{2,1,0:T(8,128)(2,1)}, u32[]{:S(2)}, u32[]{:S(2)}) collective-permute-start(bf16[1,96,1536]{2,1,0:T(8,128)(2,1)S(1)} %fusion.17), channel_id=1, source_target_pairs={{0,16},{4,20},{8,24},{12,28},{16,0},{20,4},{24,8},{28,12},{1,17},{... | collective-permute-start | bytes 884744 | tf_op jit(solution)/shard_map/ppermute | solution.py:934
  42.3 4.5 %collective-permute-start.10 = (bf16[1,192,768]{2,1,0:T(8,128)(2,1)}, bf16[1,192,768]{2,1,0:T(8,128)(2,1)S(1)}, u32[]{:S(2)}, u32[]{:S(2)}) collective-permute-start(bf16[1,192,768]{2,1,0:T(8,128)(2,1)} %select_bitcast_fusion), channel_id=1, source_target_pairs={{0,8},{4,12},{8,0},{12,4},{16,24},{20,28},{24,16},{28,20},{1,9},{5... | collective-permute-start | bytes 884744 | tf_op jit(solution)/shard_map/ppermute | solution.py:934
  46.8 8.2 %attend.3 = (bf16[64,1024]{1,0:T(8,128)(2,1)S(1)}, bf16[64,1024]{1,0:T(8,128)(2,1)S(1)}, f32[64,2048]{1,0:T(8,128)S(1)}, f32[1,2048]{1,0:T(1,128)S(1)}) custom-call(s32[145]{0:T(256)S(1)} %get-tuple-element.112.plan.refs_0_, bf16[512,768]{1,0:T(8,128)(2,1)S(1)} %copy-done.2, bf16[512,768]{1,0:T(8,128)(2,1)S(1)} %collective-permute-done.tok1.refs_3_, ...), custom_call_target="tpu_custom_call" | custom-call | flops 1 | bytes 1 | tf_op jit(solution)/shard_map/attend/pallas_call | solution.py:260
  62.2 8.2 %attend.4 = (bf16[64,1024]{1,0:T(8,128)(2,1)S(1)}, bf16[64,1024]{1,0:T(8,128)(2,1)S(1)}, f32[64,2048]{1,0:T(8,128)S(1)}, f32[1,2048]{1,0:T(1,128)S(1)}) custom-call(s32[145]{0:T(256)S(1)} %get-tuple-element.112.plan.refs_0_, bf16[512,768]{1,0:T(8,128)(2,1)S(1)} %copy-done.2, bf16[512,768]{1,0:T(8,128)(2,1)S(1)} %collective-permute-done.tok1.refs_3_, ...), custom_call_target="tpu_custom_call" | custom-call | flops 1 | bytes 1 | tf_op jit(solution)/shard_map/attend/pallas_call | solution.py:260
  72.1 3.4 %collective-permute-done.12 = bf16[2,96,1536]{2,1,0:T(8,128)(2,1)S(1)} collective-permute-done((bf16[2,96,1536]{2,1,0:T(8,128)(2,1)S(1)}, bf16[2,96,1536]{2,1,0:T(8,128)(2,1)S(1)}, u32[]{:S(2)}, u32[]{:S(2)}) %collective-permute-start.12) | collective-permute-done | bytes 589856 | tf_op jit(solution)/shard_map/ppermute | solution.py:934
  79.5 2.1 pad_maximum_fusion.1.refs_0_
  81.6 8.4 %attend.5 = (bf16[64,1024]{1,0:T(8,128)(2,1)S(1)}, bf16[64,1024]{1,0:T(8,128)(2,1)S(1)}, f32[64,2048]{1,0:T(8,128)S(1)}, f32[1,2048]{1,0:T(1,128)S(1)}) custom-call(s32[145]{0:T(256)S(1)} %get-tuple-element.112.plan.refs_0_, bf16[512,768]{1,0:T(8,128)(2,1)S(1)} %copy-done.2, bf16[512,768]{1,0:T(8,128)(2,1)S(1)} %collective-permute-done.tok1.refs_3_, ...), custom_call_target="tpu_custom_call" | custom-call | flops 1 | bytes 1 | tf_op jit(solution)/shard_map/attend/pallas_call | solution.py:260
  92.2 4.3 %collective-permute-done.18 = bf16[64,1024]{1,0:T(8,128)(2,1)S(1)} collective-permute-done((bf16[64,1024]{1,0:T(8,128)(2,1)S(1)}, bf16[64,1024]{1,0:T(8,128)(2,1)S(1)}, u32[]{:S(2)}, u32[]{:S(2)}) %collective-permute-start.18) | collective-permute-done | bytes 131104 | tf_op jit(solution)/shard_map/ppermute | solution.py:940
  97.7 6.2 %collective-permute-done.20.refs_1_ = bf16[4,96,1536]{2,1,0:T(8,128)(2,1)S(1)} collective-permute-done((bf16[4,96,1536]{2,1,0:T(8,128)(2,1)S(1)}, bf16[4,96,1536]{2,1,0:T(8,128)(2,1)S(1)}, u32[]{:S(2)}, u32[]{:S(2)}) %collective-permute-start.20) | collective-permute-done | bytes 1179680 | tf_op jit(solution)/shard_map/ppermute | solution.py:934
  113.7 6.9 %feed_up.1 = (bf16[1024,1536]{1,0:T(8,128)(2,1)S(1)}, bf16[1536,1024]{1,0:T(8,128)(2,1)S(1)}, bf16[1024,1536]{1,0:T(8,128)(2,1)S(1)}, bf16[768,1024]{1,0:T(8,128)(2,1)S(1)}) custom-call(bf16[256,768]{1,0:T(8,128)(2,1)} %get-tuple-element.141.low0, bf16[256,768]{1,0:T(8,128)(2,1)} %get-tuple-element.142.low1, bf16[256,768]{1,0:T(8,128)(2,1)} %collective-permute-done.23.low2, ...), custom_call_target="tpu_custom_call" | custom-call | flops 1 | bytes 1 | tf_op jit(solution)/shard_map/feed_up/pallas_call | solution.py:541
  122.3 3.2 %feed_down.1 = (f32[512,768]{1,0:T(8,128)S(1)}, bf16[512,768]{1,0:T(8,128)(2,1)S(1)}) custom-call(bf16[1024,1536]{1,0:T(8,128)(2,1)S(1)} %get-tuple-element.143.act, bf16[1536,768]{1,0:T(8,128)(2,1)S(1)} %assemble.7.down), custom_call_target="tpu_custom_call" | custom-call | flops 1 | bytes 1 | tf_op jit(solution)/shard_map/feed_down/pallas_call | solution.py:582
  125.8 2.1 collective-permute-done.26.recv
  127.9 2.3 second_norm.1
  130.4 2.1 collective-permute-done.27.refs_3_.grad_other
  132.5 2.9 %weight_grad.2 = bf16[4,384,768]{2,1,0:T(8,128)(2,1)S(1)} custom-call(s32[1]{0:T(128)} %bitcast.12.refs_0_, bf16[1536,1024]{1,0:T(8,128)(2,1)S(1)} %get-tuple-element.151.refs_1_, bf16[512,768]{1,0:T(8,128)(2,1)S(1)} %get-tuple-element.152.refs_2_.grad_own, bf16[512,768]{1,0:T(8,128)(2,1)S(1)} %collective-permute-done.27.refs_3_.grad_other), custom_call_target="tpu_custom_call" | custom-call | flops 1 | bytes 1 | tf_op jit(solution)/shard_map/weight_grad/pallas_call | solution.py:677
  135.5 6.5 %feed_back.1 = (f32[512,768]{1,0:T(8,128)S(1)}, bf16[256,768]{1,0:T(8,128)(2,1)S(1)}, bf16[256,768]{1,0:T(8,128)(2,1)S(1)}, bf16[1024,1536]{1,0:T(8,128)(2,1)S(1)}) custom-call(bf16[512,768]{1,0:T(8,128)(2,1)S(1)} %get-tuple-element.152.refs_2_.grad_own, bf16[512,768]{1,0:T(8,128)(2,1)S(1)} %collective-permute-done.27.refs_3_.grad_other, ...), custom_call_target="tpu_custom_call" | custom-call | flops 1 | bytes 1 | tf_op jit(solution)/shard_map/feed_back/pallas_call | solution.py:626
  143.3 3.5 %weight_grad.3 = bf16[8,96,1536]{2,1,0:T(8,128)(2,1)S(1)} custom-call(s32[1]{0:T(128)} %bitcast.2.info.refs_0_, bf16[768,1024]{1,0:T(8,128)(2,1)S(1)} %get-tuple-element.157.refs_1_, bf16[1024,1536]{1,0:T(8,128)(2,1)S(1)} %get-tuple-element.158.refs_2_), custom_call_target="tpu_custom_call" | custom-call | flops 1 | bytes 1 | tf_op jit(solution)/shard_map/weight_grad/pallas_call | solution.py:677
  156.4 6.0 %collective-permute-done.32 = bf16[192,1024]{1,0:T(8,128)(2,1)S(1)} collective-permute-done((bf16[192,1024]{1,0:T(8,128)(2,1)S(1)}, bf16[192,1024]{1,0:T(8,128)(2,1)S(1)}, u32[]{:S(2)}, u32[]{:S(2)}) %collective-permute-start.32) | collective-permute-done | bytes 393248 | tf_op jit(solution)/shard_map/ppermute | solution.py:940
  162.5 13.1 %attend_back.3 = (bf16[192,1024]{1,0:T(8,128)(2,1)S(1)}, bf16[192,1024]{1,0:T(8,128)(2,1)S(1)}, bf16[8,96,640]{2,1,0:T(8,128)(2,1)S(1)}) custom-call(s32[145]{0:T(256)S(1)} %get-tuple-element.112.plan.refs_0_, s32[3]{0:T(128)S(1)} %pad_add_fusion.place.info.refs_1_, bf16[512,768]{1,0:T(8,128)(2,1)S(1)} %copy-done.2, ...), custom_call_target="tpu_custom_call" | custom-call | flops 1 | bytes 1 | tf_op jit(solution)/shard_map/attend_back/pallas_call | solution.py:396
  180.9 12.8 %attend_back.4 = (bf16[192,1024]{1,0:T(8,128)(2,1)S(1)}, bf16[192,1024]{1,0:T(8,128)(2,1)S(1)}, bf16[8,96,256]{2,1,0:T(8,128)(2,1)S(1)}) custom-call(s32[145]{0:T(256)S(1)} %get-tuple-element.112.plan.refs_0_, s32[3]{0:T(128)S(1)} %pad_add_fusion.place.info.refs_1_, bf16[512,768]{1,0:T(8,128)(2,1)S(1)} %copy-done.2, ...), custom_call_target="tpu_custom_call" | custom-call | flops 1 | bytes 1 | tf_op jit(solution)/shard_map/attend_back/pallas_call | solution.py:396
  196.6 12.8 %attend_back.5 = (bf16[192,1024]{1,0:T(8,128)(2,1)S(1)}, bf16[192,1024]{1,0:T(8,128)(2,1)S(1)}, bf16[8,96,512]{2,1,0:T(8,128)(2,1)S(1)}) custom-call(s32[145]{0:T(256)S(1)} %get-tuple-element.112.plan.refs_0_, s32[3]{0:T(128)S(1)} %pad_add_fusion.place.info.refs_1_, bf16[512,768]{1,0:T(8,128)(2,1)S(1)} %copy-done.2, ...), custom_call_target="tpu_custom_call" | custom-call | flops 1 | bytes 1 | tf_op jit(solution)/shard_map/attend_back/pallas_call | solution.py:396
  213.6 8.0 %collective-permute-done.40.refs_5_ = bf16[192,1024]{1,0:T(8,128)(2,1)S(1)} collective-permute-done((bf16[192,1024]{1,0:T(8,128)(2,1)S(1)}, bf16[192,1024]{1,0:T(8,128)(2,1)S(1)}, u32[]{:S(2)}, u32[]{:S(2)}) %collective-permute-start.40) | collective-permute-done | bytes 393248 | tf_op jit(solution)/shard_map/ppermute | solution.py:940
  222.9 3.6 %input_back.1 = (f32[512,768]{1,0:T(8,128)S(1)}, bf16[512,768]{1,0:T(8,128)(2,1)S(1)}) custom-call(bf16[192,1024]{1,0:T(8,128)(2,1)S(1)} %get-tuple-element.173.refs_0_, bf16[192,1024]{1,0:T(8,128)(2,1)S(1)} %get-tuple-element.180.refs_1_, bf16[192,1024]{1,0:T(8,128)(2,1)S(1)} %get-tuple-element.189.refs_2_, ...), custom_call_target="tpu_custom_call" | custom-call | flops 1 | bytes 1 | tf_op jit(solution)/shard_map/input_back/pallas_call | solution.py:452
  226.6 3.7 %collective-permute-done.45 = bf16[2,96,512]{2,1,0:T(8,128)(2,1)S(1)} collective-permute-done((bf16[2,96,512]{2,1,0:T(8,128)(2,1)S(1)}, bf16[2,96,512]{2,1,0:T(8,128)(2,1)S(1)}, u32[]{:S(2)}, u32[]{:S(2)}) %collective-permute-start.45) | collective-permute-done | bytes 196640 | tf_op jit(solution)/shard_map/ppermute | solution.py:934
  231.4 2.7 %collective-permute-start.48 = (bf16[1,96,640]{2,1,0:T(8,128)(2,1)S(1)}, bf16[1,96,640]{2,1,0:T(8,128)(2,1)S(1)}, u32[]{:S(2)}, u32[]{:S(2)}) collective-permute-start(bf16[1,96,640]{2,1,0:T(8,128)(2,1)S(1)} %slice.248), channel_id=1, source_target_pairs={{0,16},{4,20},{8,24},{12,28},{16,0},{20,4},{24,8},{28,12},{1,17},{... | collective-permute-start | bytes 368648 | tf_op jit(solution)/shard_map/ppermute | solution.py:934
  235.8 7.5 %collective-permute-done.48 = bf16[1,96,640]{2,1,0:T(8,128)(2,1)S(1)} collective-permute-done((bf16[1,96,640]{2,1,0:T(8,128)(2,1)S(1)}, bf16[1,96,640]{2,1,0:T(8,128)(2,1)S(1)}, u32[]{:S(2)}, u32[]{:S(2)}) %collective-permute-start.48) | collective-permute-done | bytes 122912 | tf_op jit(solution)/shard_map/ppermute | solution.py:934
  (236 shorter events, 86.6 us)
Async XLA Ops:
  6.8 21.1 %collective-permute-start.1 = (bf16[512,768]{1,0:T(8,128)(2,1)}, bf16[512,768]{1,0:T(8,128)(2,1)S(1)}, u32[]{:S(2)}, u32[]{:S(2)}) collective-permute-start(bf16[512,768]{1,0:T(8,128)(2,1)} %refs_2_.5), channel_id=1, source_target_pairs={{0,2},{1,3},{2,0},{3,1},{4,6},{5,7},{6,4},{7,5},{8,10},{9,11},{10,... | collective-permute-start | bytes 2359304 | tf_op jit(solution)/shard_map/ppermute | solution.py:940
  23.3 23.5 %collective-permute-start = (bf16[512,768]{1,0:T(8,128)(2,1)S(1)}, bf16[512,768]{1,0:T(8,128)(2,1)S(1)}, u32[]{:S(2)}, u32[]{:S(2)}) collective-permute-start(bf16[512,768]{1,0:T(8,128)(2,1)S(1)} %copy-done.2), channel_id=1, source_target_pairs={{0,1},{1,0},{2,3},{3,2},{4,5},{5,4},{6,7},{7,6},{8,9},{9,8},{10,11... | collective-permute-start | bytes 2359304 | tf_op jit(solution)/shard_map/ppermute | solution.py:937
  27.9 18.9 %collective-permute-start.6 = (bf16[512,768]{1,0:T(8,128)(2,1)S(1)}, bf16[512,768]{1,0:T(8,128)(2,1)}, u32[]{:S(2)}, u32[]{:S(2)}) collective-permute-start(bf16[512,768]{1,0:T(8,128)(2,1)S(1)} %collective-permute-done.1.tok2.refs_4_), channel_id=1, source_target_pairs={{0,1},{1,0},{2,3},{3,2},{4,5},{5,4},{6,7},{7,6},{8,9},{9,8},{10,11... | collective-permute-start | bytes 2359304 | tf_op jit(solution)/shard_map/ppermute | solution.py:937
  28.7 26.3 %collective-permute-start.9 = (bf16[4,96,768]{2,1,0:T(8,128)(2,1)}, bf16[4,96,768]{2,1,0:T(8,128)(2,1)}, u32[]{:S(2)}, u32[]{:S(2)}) collective-permute-start(bf16[4,96,768]{2,1,0:T(8,128)(2,1)} %pad_maximum_fusion.2.refs_0_), channel_id=1, source_target_pairs={{0,4},{4,0},{8,12},{12,8},{16,20},{20,16},{24,28},{28,24},{1,5},{5... | collective-permute-start | bytes 1769480 | tf_op jit(solution)/shard_map/ppermute | solution.py:934
  37.6 19.2 %collective-permute-start.11 = (bf16[1,96,1536]{2,1,0:T(8,128)(2,1)S(1)}, bf16[1,96,1536]{2,1,0:T(8,128)(2,1)}, u32[]{:S(2)}, u32[]{:S(2)}) collective-permute-start(bf16[1,96,1536]{2,1,0:T(8,128)(2,1)S(1)} %fusion.17), channel_id=1, source_target_pairs={{0,16},{4,20},{8,24},{12,28},{16,0},{20,4},{24,8},{28,12},{1,17},{... | collective-permute-start | bytes 884744 | tf_op jit(solution)/shard_map/ppermute | solution.py:934
  42.3 16.2 %collective-permute-start.10 = (bf16[1,192,768]{2,1,0:T(8,128)(2,1)}, bf16[1,192,768]{2,1,0:T(8,128)(2,1)S(1)}, u32[]{:S(2)}, u32[]{:S(2)}) collective-permute-start(bf16[1,192,768]{2,1,0:T(8,128)(2,1)} %select_bitcast_fusion), channel_id=1, source_target_pairs={{0,8},{4,12},{8,0},{12,4},{16,24},{20,28},{24,16},{28,20},{1,9},{5... | collective-permute-start | bytes 884744 | tf_op jit(solution)/shard_map/ppermute | solution.py:934
  56.7 13.7 %collective-permute-start.19 = (bf16[384,384]{1,0:T(8,128)(2,1)S(1)}, bf16[384,384]{1,0:T(8,128)(2,1)S(1)}, u32[]{:S(2)}, u32[]{:S(2)}) collective-permute-start(bf16[384,384]{1,0:T(8,128)(2,1)S(1)} %get-tuple-element.221), channel_id=1, source_target_pairs={{0,1},{1,0},{2,3},{3,2},{4,5},{5,4},{6,7},{7,6},{8,9},{9,8},{10,11... | collective-permute-start | bytes 884744 | tf_op jit(solution)/shard_map/ppermute | solution.py:937
  59.6 18.5 %collective-permute-start.13 = (bf16[2,192,768]{2,1,0:T(8,128)(2,1)S(1)}, bf16[2,192,768]{2,1,0:T(8,128)(2,1)S(1)}, u32[]{:S(2)}, u32[]{:S(2)}) collective-permute-start(bf16[2,192,768]{2,1,0:T(8,128)(2,1)S(1)} %pad_maximum_fusion.3), channel_id=1, source_target_pairs={{0,4},{4,0},{8,12},{12,8},{16,20},{20,16},{24,28},{28,24},{1,5},{5... | collective-permute-start | bytes 1769480 | tf_op jit(solution)/shard_map/ppermute | solution.py:934
  60.1 15.4 %collective-permute-start.12 = (bf16[2,96,1536]{2,1,0:T(8,128)(2,1)S(1)}, bf16[2,96,1536]{2,1,0:T(8,128)(2,1)S(1)}, u32[]{:S(2)}, u32[]{:S(2)}) collective-permute-start(bf16[2,96,1536]{2,1,0:T(8,128)(2,1)S(1)} %pad_maximum_fusion.4), channel_id=1, source_target_pairs={{0,8},{4,12},{8,0},{12,4},{16,24},{20,28},{24,16},{28,20},{1,9},{5... | collective-permute-start | bytes 1769480 | tf_op jit(solution)/shard_map/ppermute | solution.py:934
  60.1 29.9 %collective-permute-start.17 = (bf16[768,384]{1,0:T(8,128)(2,1)S(1)}, bf16[768,384]{1,0:T(8,128)(2,1)S(1)}, u32[]{:S(2)}, u32[]{:S(2)}) collective-permute-start(bf16[768,384]{1,0:T(8,128)(2,1)S(1)} %slice.223), channel_id=1, source_target_pairs={{0,2},{1,3},{2,0},{3,1},{4,6},{5,7},{6,4},{7,5},{8,10},{9,11},{10,... | collective-permute-start | bytes 1769480 | tf_op jit(solution)/shard_map/ppermute | solution.py:940
  61.6 28.5 %collective-permute-start.16 = (bf16[768,256]{1,0:T(8,128)(2,1)S(1)}, bf16[768,256]{1,0:T(8,128)(2,1)S(1)}, u32[]{:S(2)}, u32[]{:S(2)}) collective-permute-start(bf16[768,256]{1,0:T(8,128)(2,1)S(1)} %assemble.4.part), channel_id=1, source_target_pairs={{0,2},{1,3},{2,0},{3,1},{4,6},{5,7},{6,4},{7,5},{8,10},{9,11},{10,... | collective-permute-start | bytes 1179656 | tf_op jit(solution)/shard_map/ppermute | solution.py:940
  70.4 21.8 %collective-permute-start.14 = (bf16[64,1024]{1,0:T(8,128)(2,1)S(1)}, bf16[64,1024]{1,0:T(8,128)(2,1)S(1)}, u32[]{:S(2)}, u32[]{:S(2)}) collective-permute-start(bf16[64,1024]{1,0:T(8,128)(2,1)S(1)} %get-tuple-element.134), channel_id=1, source_target_pairs={{0,2},{1,3},{2,0},{3,1},{4,6},{5,7},{6,4},{7,5},{8,10},{9,11},{10,... | collective-permute-start | bytes 393224 | tf_op jit(solution)/shard_map/ppermute | solution.py:940
  76.6 27.3 %collective-permute-start.20 = (bf16[4,96,1536]{2,1,0:T(8,128)(2,1)S(1)}, bf16[4,96,1536]{2,1,0:T(8,128)(2,1)S(1)}, u32[]{:S(2)}, u32[]{:S(2)}) collective-permute-start(bf16[4,96,1536]{2,1,0:T(8,128)(2,1)S(1)} %pad_maximum_fusion.refs_0_), channel_id=1, source_target_pairs={{0,4},{4,0},{8,12},{12,8},{16,20},{20,16},{24,28},{28,24},{1,5},{5... | collective-permute-start | bytes 3538952 | tf_op jit(solution)/shard_map/ppermute | solution.py:934
  78.1 14.1 %collective-permute-start.15 = (bf16[64,1024]{1,0:T(8,128)(2,1)S(1)}, bf16[64,1024]{1,0:T(8,128)(2,1)S(1)}, u32[]{:S(2)}, u32[]{:S(2)}) collective-permute-start(bf16[64,1024]{1,0:T(8,128)(2,1)S(1)} %get-tuple-element.135), channel_id=1, source_target_pairs={{0,2},{1,3},{2,0},{3,1},{4,6},{5,7},{6,4},{7,5},{8,10},{9,11},{10,... | collective-permute-start | bytes 393224 | tf_op jit(solution)/shard_map/ppermute | solution.py:940
  90.8 29.8 %collective-permute-start.25 = (bf16[4,192,768]{2,1,0:T(8,128)(2,1)}, bf16[4,192,768]{2,1,0:T(8,128)(2,1)}, u32[]{:S(2)}, u32[]{:S(2)}) collective-permute-start(bf16[4,192,768]{2,1,0:T(8,128)(2,1)} %pad_maximum_fusion.1.refs_0_), channel_id=1, source_target_pairs={{0,2},{1,3},{2,0},{3,1},{4,6},{5,7},{6,4},{7,5},{8,10},{9,11},{10,... | collective-permute-start | bytes 3538952 | tf_op jit(solution)/shard_map/ppermute | solution.py:940
  142.6 32.9 %collective-permute-start.34 = (bf16[2,384,768]{2,1,0:T(8,128)(2,1)S(1)}, bf16[2,384,768]{2,1,0:T(8,128)(2,1)S(1)}, u32[]{:S(2)}, u32[]{:S(2)}) collective-permute-start(bf16[2,384,768]{2,1,0:T(8,128)(2,1)S(1)} %slice.232), channel_id=1, source_target_pairs={{0,8},{4,12},{8,0},{12,4},{16,24},{20,28},{24,16},{28,20},{1,9},{5... | collective-permute-start | bytes 3538952 | tf_op jit(solution)/shard_map/ppermute | solution.py:934
  148.7 28.0 %collective-permute-start.35 = (bf16[4,96,1536]{2,1,0:T(8,128)(2,1)S(1)}, bf16[4,96,1536]{2,1,0:T(8,128)(2,1)S(1)}, u32[]{:S(2)}, u32[]{:S(2)}) collective-permute-start(bf16[4,96,1536]{2,1,0:T(8,128)(2,1)S(1)} %slice.234), channel_id=1, source_target_pairs={{0,4},{4,0},{8,12},{12,8},{16,20},{20,16},{24,28},{28,24},{1,5},{5... | collective-permute-start | bytes 3538952 | tf_op jit(solution)/shard_map/ppermute | solution.py:934
  151.2 11.2 %collective-permute-start.32 = (bf16[192,1024]{1,0:T(8,128)(2,1)S(1)}, bf16[192,1024]{1,0:T(8,128)(2,1)S(1)}, u32[]{:S(2)}, u32[]{:S(2)}) collective-permute-start(bf16[192,1024]{1,0:T(8,128)(2,1)S(1)} %get-tuple-element.167), channel_id=1, source_target_pairs={{0,2},{1,3},{2,0},{3,1},{4,6},{5,7},{6,4},{7,5},{8,10},{9,11},{10,... | collective-permute-start | bytes 1179656 | tf_op jit(solution)/shard_map/ppermute | solution.py:940
  176.8 17.8 %collective-permute-start.36 = (bf16[1,384,768]{2,1,0:T(8,128)(2,1)S(1)}, bf16[1,384,768]{2,1,0:T(8,128)(2,1)S(1)}, u32[]{:S(2)}, u32[]{:S(2)}) collective-permute-start(bf16[1,384,768]{2,1,0:T(8,128)(2,1)S(1)} %slice.237), channel_id=1, source_target_pairs={{0,4},{4,0},{8,12},{12,8},{16,20},{20,16},{24,28},{28,24},{1,5},{5... | collective-permute-start | bytes 1769480 | tf_op jit(solution)/shard_map/ppermute | solution.py:934
  178.1 16.6 %collective-permute-start.37 = (bf16[2,96,1536]{2,1,0:T(8,128)(2,1)S(1)}, bf16[2,96,1536]{2,1,0:T(8,128)(2,1)S(1)}, u32[]{:S(2)}, u32[]{:S(2)}) collective-permute-start(bf16[2,96,1536]{2,1,0:T(8,128)(2,1)S(1)} %slice.239), channel_id=1, source_target_pairs={{0,8},{4,12},{8,0},{12,4},{16,24},{20,28},{24,16},{28,20},{1,9},{5... | collective-permute-start | bytes 1769480 | tf_op jit(solution)/shard_map/ppermute | solution.py:934
  179.6 15.1 %collective-permute-start.38 = (bf16[192,1024]{1,0:T(8,128)(2,1)S(1)}, bf16[192,1024]{1,0:T(8,128)(2,1)S(1)}, u32[]{:S(2)}, u32[]{:S(2)}) collective-permute-start(bf16[192,1024]{1,0:T(8,128)(2,1)S(1)} %get-tuple-element.183), channel_id=1, source_target_pairs={{0,2},{1,3},{2,0},{3,1},{4,6},{5,7},{6,4},{7,5},{8,10},{9,11},{10,... | collective-permute-start | bytes 1179656 | tf_op jit(solution)/shard_map/ppermute | solution.py:940
  193.7 17.1 %collective-permute-start.39 = (bf16[192,1024]{1,0:T(8,128)(2,1)S(1)}, bf16[192,1024]{1,0:T(8,128)(2,1)S(1)}, u32[]{:S(2)}, u32[]{:S(2)}) collective-permute-start(bf16[192,1024]{1,0:T(8,128)(2,1)S(1)} %get-tuple-element.190), channel_id=1, source_target_pairs={{0,2},{1,3},{2,0},{3,1},{4,6},{5,7},{6,4},{7,5},{8,10},{9,11},{10,... | collective-permute-start | bytes 1179656 | tf_op jit(solution)/shard_map/ppermute | solution.py:940
  194.9 16.0 %collective-permute-start.41 = (bf16[1,96,1536]{2,1,0:T(8,128)(2,1)S(1)}, bf16[1,96,1536]{2,1,0:T(8,128)(2,1)S(1)}, u32[]{:S(2)}, u32[]{:S(2)}) collective-permute-start(bf16[1,96,1536]{2,1,0:T(8,128)(2,1)S(1)} %slice.242), channel_id=1, source_target_pairs={{0,16},{4,20},{8,24},{12,28},{16,0},{20,4},{24,8},{28,12},{1,17},{... | collective-permute-start | bytes 884744 | tf_op jit(solution)/shard_map/ppermute | solution.py:934
  195.4 15.6 %collective-permute-start.42 = (bf16[4,96,640]{2,1,0:T(8,128)(2,1)S(1)}, bf16[4,96,640]{2,1,0:T(8,128)(2,1)S(1)}, u32[]{:S(2)}, u32[]{:S(2)}) collective-permute-start(bf16[4,96,640]{2,1,0:T(8,128)(2,1)S(1)} %slice.196), channel_id=1, source_target_pairs={{0,4},{4,0},{8,12},{12,8},{16,20},{20,16},{24,28},{28,24},{1,5},{5... | collective-permute-start | bytes 1474568 | tf_op jit(solution)/shard_map/ppermute | solution.py:934
  209.5 12.1 %collective-permute-start.40 = (bf16[192,1024]{1,0:T(8,128)(2,1)S(1)}, bf16[192,1024]{1,0:T(8,128)(2,1)S(1)}, u32[]{:S(2)}, u32[]{:S(2)}) collective-permute-start(bf16[192,1024]{1,0:T(8,128)(2,1)S(1)} %get-tuple-element.191), channel_id=1, source_target_pairs={{0,2},{1,3},{2,0},{3,1},{4,6},{5,7},{6,4},{7,5},{8,10},{9,11},{10,... | collective-permute-start | bytes 1179656 | tf_op jit(solution)/shard_map/ppermute | solution.py:940
  212.5 18.0 %collective-permute-start.49 = (bf16[384,768]{1,0:T(8,128)(2,1)S(1)}, bf16[384,768]{1,0:T(8,128)(2,1)S(1)}, u32[]{:S(2)}, u32[]{:S(2)}) collective-permute-start(bf16[384,768]{1,0:T(8,128)(2,1)S(1)} %fusion), channel_id=1, source_target_pairs={{0,1},{1,17},{2,3},{3,19},{4,5},{5,21},{6,7},{7,23},{8,9},{9,25},{... | collective-permute-start | bytes 1769480 | tf_op jit(solution)/shard_map/ppermute | solution.py:948
  212.5 14.1 %collective-permute-start.46 = (bf16[96,1536]{1,0:T(8,128)(2,1)S(1)}, bf16[96,1536]{1,0:T(8,128)(2,1)S(1)}, u32[]{:S(2)}, u32[]{:S(2)}) collective-permute-start(bf16[96,1536]{1,0:T(8,128)(2,1)S(1)} %fusion.3), channel_id=1, source_target_pairs={{0,2},{1,3},{2,0},{3,1},{4,6},{5,7},{6,4},{7,5},{8,10},{9,11},{10,... | collective-permute-start | bytes 884744 | tf_op jit(solution)/shard_map/ppermute | solution.py:940
  213.3 17.1 %collective-permute-start.47 = (bf16[2,96,640]{2,1,0:T(8,128)(2,1)S(1)}, bf16[2,96,640]{2,1,0:T(8,128)(2,1)S(1)}, u32[]{:S(2)}, u32[]{:S(2)}) collective-permute-start(bf16[2,96,640]{2,1,0:T(8,128)(2,1)S(1)} %slice.246), channel_id=1, source_target_pairs={{0,8},{4,12},{8,0},{12,4},{16,24},{20,28},{24,16},{28,20},{1,9},{5... | collective-permute-start | bytes 737288 | tf_op jit(solution)/shard_map/ppermute | solution.py:934
  226.5 20.7 %collective-permute-start.44 = (bf16[512,768]{1,0:T(8,128)(2,1)S(1)}, bf16[512,768]{1,0:T(8,128)(2,1)S(1)}, u32[]{:S(2)}, u32[]{:S(2)}) collective-permute-start(bf16[512,768]{1,0:T(8,128)(2,1)S(1)} %get-tuple-element.202), channel_id=1, source_target_pairs={{0,1},{1,0},{2,3},{3,2},{4,5},{5,4},{6,7},{7,6},{8,9},{9,8},{10,11... | collective-permute-start | bytes 2359304 | tf_op jit(solution)/shard_map/ppermute | solution.py:937
  230.9 15.0 %collective-permute-start.55 = (bf16[96,1536]{1,0:T(8,128)(2,1)S(1)}, bf16[96,1536]{1,0:T(8,128)(2,1)S(1)}, u32[]{:S(2)}, u32[]{:S(2)}) collective-permute-start(bf16[96,1536]{1,0:T(8,128)(2,1)S(1)} %add_convert_fusion.7), channel_id=1, source_target_pairs={{0,1},{1,0},{2,3},{3,2},{4,5},{5,4},{6,7},{7,6},{8,9},{9,8},{10,11... | collective-permute-start | bytes 884744 | tf_op jit(solution)/shard_map/ppermute | solution.py:937
  231.4 11.8 %collective-permute-start.48 = (bf16[1,96,640]{2,1,0:T(8,128)(2,1)S(1)}, bf16[1,96,640]{2,1,0:T(8,128)(2,1)S(1)}, u32[]{:S(2)}, u32[]{:S(2)}) collective-permute-start(bf16[1,96,640]{2,1,0:T(8,128)(2,1)S(1)} %slice.248), channel_id=1, source_target_pairs={{0,16},{4,20},{8,24},{12,28},{16,0},{20,4},{24,8},{28,12},{1,17},{... | collective-permute-start | bytes 368648 | tf_op jit(solution)/shard_map/ppermute | solution.py:934
  234.4 12.7 %collective-permute-start.53 = (bf16[192,768]{1,0:T(8,128)(2,1)S(1)}, bf16[192,768]{1,0:T(8,128)(2,1)S(1)}, u32[]{:S(2)}, u32[]{:S(2)}) collective-permute-start(bf16[192,768]{1,0:T(8,128)(2,1)S(1)} %select_select_fusion), channel_id=1, source_target_pairs={{0,2},{1,3},{2,0},{3,1},{4,6},{5,7},{6,4},{7,5},{8,10},{9,11},{10,... | collective-permute-start | bytes 884744 | tf_op jit(solution)/shard_map/ppermute | solution.py:940
  (55 other events, 359.9 us)

commit v2 on v1

--- a/solution.py
+++ b/solution.py
@@ -685,23 +685,21 @@
     )(shard[None], left, *rights)
 
 
-def mix_back_kernel(mixer, grad0, grad1, grad2, grad3, g_own, g_send):
-    quarter = g_own.shape[0]
+def mix_back_kernel(mixer, grad0, grad1, grad2, grad3, *outs):
     rows = grad0.shape[0]
     for p, grad in enumerate((grad0, grad1, grad2, grad3)):
         value = dot(mixer[...], grad[...], 1, 1).astype(BF)
-        g_own[:, p * rows : (p + 1) * rows] = value[:quarter]
-        g_send[:, p * rows : (p + 1) * rows] = value[quarter:]
+        for j, out in enumerate(outs):
+            out[:, p * rows : (p + 1) * rows] = value[j * HEAD_DIM : (j + 1) * HEAD_DIM]
 
 
 def mix_back(mixer, grads):
-    half_width = mixer.shape[0]
     rows = grads[0].shape[0] * 4
     return pl.pallas_call(
         mix_back_kernel,
-        out_shape=(shape((half_width // 2, rows), BF),) * 2,
+        out_shape=(shape((HEAD_DIM, rows), BF),) * 6,
         in_specs=[VMEM] * 5,
-        out_specs=(VMEM,) * 2,
+        out_specs=(VMEM,) * 6,
         compiler_params=params(16),
         cost_estimate=FREE,
         name="mix_back",
@@ -735,7 +733,7 @@
     )(info, context, *grads)
 
 
-def mix_place_kernel(blocks, info, own, recv, out, scratch):
+def mix_place_kernel(blocks, info, own, recv, behind, out, scratch):
     half_width = own.shape[1]
     quarter = half_width // 2
     x, c, shard = info[0], info[1], info[2]
@@ -745,21 +743,24 @@
             scratch[pl.ds(at, quarter), :] = ref[dx * quarter : (dx + 1) * quarter, :].astype(F32)
     block = out.shape[1]
     for b in range(blocks):
-        out[order_of(range(blocks), shard, b)] = scratch[b * block : (b + 1) * block, :].astype(BF)
-
-
-def mix_place(info, own, recv, blocks):
+        to = order_of(range(blocks), shard, b)
+        out[to, :, :half_width] = scratch[b * block : (b + 1) * block, :].astype(BF)
+    out[:, :, half_width:] = behind[...]
+
+
+def mix_place(info, own, recv, behind):
     half_width = own.shape[1]
+    blocks, block, cols = behind.shape
     return pl.pallas_call(
         partial(mix_place_kernel, blocks),
-        out_shape=shape((blocks, 2 * half_width // blocks, half_width), BF),
-        in_specs=[SMEM, VMEM, VMEM],
+        out_shape=shape((blocks, block, half_width + cols), BF),
+        in_specs=[SMEM] + [VMEM] * 3,
         out_specs=VMEM,
         scratch_shapes=[pltpu.VMEM((2 * half_width, half_width), F32)],
         compiler_params=params(8),
         cost_estimate=FREE,
         name="mix_place",
-    )(info, own, recv)
+    )(info, own, recv, behind)
 
 
 def row_tiles(rows, step, body):
@@ -1011,9 +1012,9 @@
     a2 = gather_a.steps(middle, plan)
     a3 = gather_a.steps(1)
     b2 = gather_b.steps(middle, a2, up_half, down_half)
+    toks.append(swap_core(after(over_x, b2)))
     d1 = to_core(after(down_half, b1), False)
-    toks.append(swap_core(after(over_x, b2)))
-    b2 = after(b2, a3)
+    b2 = after(b2, a3, d1)
     gather_b.pieces[1] = b2
     b3 = gather_b.steps(1)
     part_a = assemble(gather_a.pieces, gather_a.offsets, shard)
@@ -1090,31 +1091,31 @@
         grad_two, first_own, [recv0, recv1], normed_one, inverse_one, vectors, late
     )
     attn = [attn0, attn1, swap_core(attn0), swap_core(attn1)]
-    g_own, g_send = mix_back(mixer, attn)
-    mixer_own, mixer_send = mix_grad(place, after(context, g_send), attn)
-    g_recv = swap_x(g_send)
-    mixer_grad = mix_place(place, mixer_own, swap_core(mixer_send), n_shard)
+    gs = mix_back(mixer, attn)
+    g_recv = [swap_x(g) for g in gs[3:]]
+    mixer_own, mixer_send = mix_grad(place, after(context, *gs), attn)
+    mixer_recv = swap_core(mixer_send)
 
     def head_back(j, before, *gate):
-        at = j * HEAD_DIM
         return attend_back(
             plan, place, toks, head_weights[j], after(ids_row, *gate),
-            g_own[at : at + HEAD_DIM], g_recv[at : at + HEAD_DIM], *saved[j],
+            gs[j], g_recv[j], *saved[j],
             sums if j == 2 else None, before, n_shard,
         )
 
     keeps, sends = [None] * 3, [None] * 3
-    keeps[0], sends[0], early = head_back(0, mixer_grad)
+    keeps[0], sends[0], part = head_back(0, None, mixer_own)
     fars = [swap_x(sends[0])]
-    narrow_grad = fold(narrow_grad, after(n1, early))
+    narrow_grad = fold(narrow_grad, after(n1, part, *g_recv[1:]))
     for bit in bits[-3:0:-1]:
         narrow_grad = fold(narrow_grad, swap(upper(narrow_grad), bit))
     n2 = swap(upper(narrow_grad), bits[0])
-    widen_grad = fold(widen_grad, after(w1, narrow_grad))
+    early = mix_place(place, mixer_own, mixer_recv, after(part, narrow_grad))
+    widen_grad = fold(widen_grad, after(w1, early))
     for bit in bits[1:-2]:
         widen_grad = fold(widen_grad, swap(upper(widen_grad), bit))
     w2 = swap(upper(widen_grad), bits[-2])
-    keeps[1], sends[1], part = head_back(1, None, narrow_grad, widen_grad)
+    keeps[1], sends[1], part = head_back(1, None, early, widen_grad)
     fars.append(swap_x(sends[1]))
     narrow_grad = fold(narrow_grad, after(n2, part))[0]
     n3 = to_core(narrow_grad, True)
@@ -1132,18 +1133,19 @@
     w4 = swap_x(widen_grad)
     late = fold(late, after(l1, fars[2]))
     l2 = swap(upper(late), bits[1])
-    fars[2] = after(fars[2], late)
-    back_own, back_core = input_back(keeps + fars, head_weights + far_weights, rows)
-    back_near = swap_core(back_core)
-    late = fold(late, after(l2, w4, back_core))
-    for bit in bits[2:-1]:
-        late = fold(late, swap(upper(late), bit))
-    l3 = swap(upper(late), bits[-1])
     early = fold(early, after(e2, late))
     for bit in bits[2:-1]:
         early = fold(early, swap(upper(early), bit))
     e3 = swap(upper(early), bits[-1])
-    narrow_grad = (narrow_grad.astype(F32) + after(n3, early).astype(F32)).astype(BF)
+    fars[2] = after(fars[2], late)
+    back_own, back_core = input_back(keeps + fars, head_weights + far_weights, rows)
+    back_near = swap_core(back_core)
+    early = fold(early, after(e3, back_core))[0]
+    late = fold(late, after(l2, w4, early))
+    for bit in bits[2:-1]:
+        late = fold(late, swap(upper(late), bit))
+    l3 = swap(upper(late), bits[-1])
+    narrow_grad = (narrow_grad.astype(F32) + after(n3, late).astype(F32)).astype(BF)
     halves = narrow_grad.reshape(2, -1, width)
     narrow_half = swap_core(pick(halves, 1 - cb, 0))
     narrow_half = jnp.where(owner, pick(halves, cb, 0), narrow_half)
@@ -1151,8 +1153,7 @@
     widen_grad = (widen_grad.astype(F32) + after(w4, late).astype(F32)).astype(BF)
     widen_other = swap_core(widen_grad)
     input_grad = grad_one + back_own + after(back_near, late).astype(F32)
-    early = fold(early, after(e3, narrow_half))[0]
-    late = fold(late, after(l3, early))[0]
+    late = fold(late, after(l3, narrow_half))[0]
     mine = jnp.concatenate([early, late], 1)
     theirs = swap_x(mine)
     narrow_half = (narrow_half.astype(F32) + after(n4, mine).astype(F32)).astype(BF)

time: 258 us -> 252 us (0.977)
  waiting for transfers between devices: 66.4 us -> 57.1 us
  starting transfers between devices: 56.2 us -> 60 us
    ppermute x14 -> x16, waiting for transfers between devices: 19.7 us -> 14.9 us  [swap_x(): return lax.ppermute(value, 'seq', [(i, i ^ 2) for i in range(4)])]
    ppermute x2, waiting for transfers between devices: 4.57 us -> 0.01 us  [to_core(): return lax.ppermute(value, ('shard', 'seq'), pairs)]
    ppermute x14 -> x16, starting transfers between devices: 16.8 us -> 18.2 us  [swap_x(): return lax.ppermute(value, 'seq', [(i, i ^ 2) for i in range(4)])]
  transfers between devices with their start and end apart: 57 -> 59, of which waited for: 25 -> 28; matrix products, arithmetic and copies ran while one was open for 7% -> 7% of each run, Pallas kernels for 35% -> 38%
where the time goes in v2:
time: 252 us; the launch traced here: 251 us
  Pallas kernels  110 us (44%)
  starting transfers between devices  60 us (24%)
  waiting for transfers between devices  57.1 us (23%)
  other arithmetic  15 us (6%)
  local copies, waits for them, and re-layouts  6.24 us (2%)
    pallas_call x3, Pallas kernels, attend_back(): pl.pallas_call(kernel, out_shape=(shape((TRIO, total // 2), BF),) * 2 + (...  38.7 us
    ppermute x22, starting transfers between devices, swap(): return lax.ppermute(value, 'shard', [(i, i ^ mask) for i in range(n_shard)])  36.4 us
    ppermute x22, waiting for transfers between devices, swap(): return lax.ppermute(value, 'shard', [(i, i ^ mask) for i in range(n_shard)])  31.3 us
    pallas_call x3, Pallas kernels, attend(): pl.pallas_call(attend_kernel, out_shape=(shape((HEAD_DIM, half), BF), sha...  24.7 us
    ppermute x16, starting transfers between devices, swap_x(): return lax.ppermute(value, 'seq', [(i, i ^ 2) for i in range(4)])  18.2 us
    ppermute x16, waiting for transfers between devices, swap_x(): return lax.ppermute(value, 'seq', [(i, i ^ 2) for i in range(4)])  14.9 us
    ppermute x19, waiting for transfers between devices, swap_core(): return lax.ppermute(value, 'seq', [(i, i ^ 1) for i in range(4)])  11 us
    pallas_call x1, Pallas kernels, feed_up(): pl.pallas_call(feed_up_kernel, out_shape=(shape((4 * rows, hidden), BF),...  6.87 us
  transfers between devices with their start and end apart: 59, of which 28 were waited for; matrix products, arithmetic and copies ran while one was open for 7% of the time, Pallas kernels for 38%

profile of v2, /device:TPU:0, one launch (start us, length us, event | category | flops | bytes accessed | tf_op | source)
XLA Modules:
  0.0 250.9 jit_solution(6244800383511145048)
XLA Ops:
  2.7 4.1 %collective-permute-start.2 = (bf16[1,96,256]{2,1,0:T(8,128)(2,1)S(1)}, bf16[1,96,256]{2,1,0:T(8,128)(2,1)S(1)}, u32[]{:S(2)}, u32[]{:S(2)}) collective-permute-start(bf16[1,96,256]{2,1,0:T(8,128)(2,1)S(1)} %bitcast.32), channel_id=1, source_target_pairs={{0,16},{4,20},{8,24},{12,28},{16,0},{20,4},{24,8},{28,12},{1,17},{... | collective-permute-start | bytes 147464 | tf_op jit(solution)/shard_map/ppermute | solution.py:935
  9.4 2.4 collective-permute-start.3
  14.4 2.0 collective-permute-start.4
  21.0 1.9 collective-permute-start.8
  24.5 5.7 %collective-permute-done.5 = bf16[2,96,768]{2,1,0:T(8,128)(2,1)S(1)} collective-permute-done((bf16[2,96,768]{2,1,0:T(8,128)(2,1)S(1)}, bf16[2,96,768]{2,1,0:T(8,128)(2,1)S(1)}, u32[]{:S(2)}, u32[]{:S(2)}) %collective-permute-start.5) | collective-permute-done | bytes 294944 | tf_op jit(solution)/shard_map/ppermute | solution.py:935
  37.5 1.9 collective-permute-start.10
  39.4 8.2 %attend.3 = (bf16[64,1024]{1,0:T(8,128)(2,1)S(1)}, bf16[64,1024]{1,0:T(8,128)(2,1)S(1)}, f32[64,2048]{1,0:T(8,128)S(1)}, f32[1,2048]{1,0:T(1,128)S(1)}) custom-call(s32[145]{0:T(256)S(1)} %get-tuple-element.118.plan.refs_0_, bf16[512,768]{1,0:T(8,128)(2,1)S(1)} %copy-done.2, bf16[512,768]{1,0:T(8,128)(2,1)S(1)} %collective-permute-done.tok1.refs_3_, ...), custom_call_target="tpu_custom_call" | custom-call | flops 1 | bytes 1 | tf_op jit(solution)/shard_map/attend/pallas_call | solution.py:260
  49.4 2.0 collective-permute-done.11
  56.5 8.2 %attend.4 = (bf16[64,1024]{1,0:T(8,128)(2,1)S(1)}, bf16[64,1024]{1,0:T(8,128)(2,1)S(1)}, f32[64,2048]{1,0:T(8,128)S(1)}, f32[1,2048]{1,0:T(1,128)S(1)}) custom-call(s32[145]{0:T(256)S(1)} %get-tuple-element.118.plan.refs_0_, bf16[512,768]{1,0:T(8,128)(2,1)S(1)} %copy-done.2, bf16[512,768]{1,0:T(8,128)(2,1)S(1)} %collective-permute-done.tok1.refs_3_, ...), custom_call_target="tpu_custom_call" | custom-call | flops 1 | bytes 1 | tf_op jit(solution)/shard_map/attend/pallas_call | solution.py:260
  66.4 3.0 %collective-permute-done.12 = bf16[2,96,1536]{2,1,0:T(8,128)(2,1)S(1)} collective-permute-done((bf16[2,96,1536]{2,1,0:T(8,128)(2,1)S(1)}, bf16[2,96,1536]{2,1,0:T(8,128)(2,1)S(1)}, u32[]{:S(2)}, u32[]{:S(2)}) %collective-permute-start.12) | collective-permute-done | bytes 589856 | tf_op jit(solution)/shard_map/ppermute | solution.py:935
  73.7 2.1 pad_maximum_fusion.1.refs_0_
  75.8 8.4 %attend.5 = (bf16[64,1024]{1,0:T(8,128)(2,1)S(1)}, bf16[64,1024]{1,0:T(8,128)(2,1)S(1)}, f32[64,2048]{1,0:T(8,128)S(1)}, f32[1,2048]{1,0:T(1,128)S(1)}) custom-call(s32[145]{0:T(256)S(1)} %get-tuple-element.118.plan.refs_0_, bf16[512,768]{1,0:T(8,128)(2,1)S(1)} %copy-done.2, bf16[512,768]{1,0:T(8,128)(2,1)S(1)} %collective-permute-done.tok1.refs_3_, ...), custom_call_target="tpu_custom_call" | custom-call | flops 1 | bytes 1 | tf_op jit(solution)/shard_map/attend/pallas_call | solution.py:260
  86.4 4.3 %collective-permute-done.18 = bf16[64,1024]{1,0:T(8,128)(2,1)S(1)} collective-permute-done((bf16[64,1024]{1,0:T(8,128)(2,1)S(1)}, bf16[64,1024]{1,0:T(8,128)(2,1)S(1)}, u32[]{:S(2)}, u32[]{:S(2)}) %collective-permute-start.18) | collective-permute-done | bytes 131104 | tf_op jit(solution)/shard_map/ppermute | solution.py:941
  91.9 5.4 %collective-permute-done.20.refs_1_ = bf16[4,96,1536]{2,1,0:T(8,128)(2,1)S(1)} collective-permute-done((bf16[4,96,1536]{2,1,0:T(8,128)(2,1)S(1)}, bf16[4,96,1536]{2,1,0:T(8,128)(2,1)S(1)}, u32[]{:S(2)}, u32[]{:S(2)}) %collective-permute-start.20) | collective-permute-done | bytes 1179680 | tf_op jit(solution)/shard_map/ppermute | solution.py:935
  100.7 2.0 first_norm.1
  107.1 6.9 %feed_up.1 = (bf16[1024,1536]{1,0:T(8,128)(2,1)S(1)}, bf16[1536,1024]{1,0:T(8,128)(2,1)S(1)}, bf16[1024,1536]{1,0:T(8,128)(2,1)S(1)}, bf16[768,1024]{1,0:T(8,128)(2,1)S(1)}) custom-call(bf16[256,768]{1,0:T(8,128)(2,1)} %get-tuple-element.147.low0, bf16[256,768]{1,0:T(8,128)(2,1)} %get-tuple-element.148.low1, bf16[256,768]{1,0:T(8,128)(2,1)} %collective-permute-done.23.low2, ...), custom_call_target="tpu_custom_call" | custom-call | flops 1 | bytes 1 | tf_op jit(solution)/shard_map/feed_up/pallas_call | solution.py:541
  115.7 3.2 %feed_down.1 = (f32[512,768]{1,0:T(8,128)S(1)}, bf16[512,768]{1,0:T(8,128)(2,1)S(1)}) custom-call(bf16[1024,1536]{1,0:T(8,128)(2,1)S(1)} %get-tuple-element.149.act, bf16[1536,768]{1,0:T(8,128)(2,1)S(1)} %assemble.7.down), custom_call_target="tpu_custom_call" | custom-call | flops 1 | bytes 1 | tf_op jit(solution)/shard_map/feed_down/pallas_call | solution.py:582
  119.1 2.2 collective-permute-done.26.recv
  121.3 2.3 second_norm.1
  123.8 2.1 collective-permute-done.27.refs_3_.grad_other
  125.9 3.0 %weight_grad.2 = bf16[4,384,768]{2,1,0:T(8,128)(2,1)S(1)} custom-call(s32[1]{0:T(128)} %bitcast.12.refs_0_, bf16[1536,1024]{1,0:T(8,128)(2,1)S(1)} %get-tuple-element.157.refs_1_, bf16[512,768]{1,0:T(8,128)(2,1)S(1)} %get-tuple-element.158.refs_2_.grad_own, bf16[512,768]{1,0:T(8,128)(2,1)S(1)} %collective-permute-done.27.refs_3_.grad_other), custom_call_target="tpu_custom_call" | custom-call | flops 1 | bytes 1 | tf_op jit(solution)/shard_map/weight_grad/pallas_call | solution.py:677
  129.6 6.5 %feed_back.1 = (f32[512,768]{1,0:T(8,128)S(1)}, bf16[256,768]{1,0:T(8,128)(2,1)S(1)}, bf16[256,768]{1,0:T(8,128)(2,1)S(1)}, bf16[1024,1536]{1,0:T(8,128)(2,1)S(1)}) custom-call(bf16[512,768]{1,0:T(8,128)(2,1)S(1)} %get-tuple-element.158.refs_2_.grad_own, bf16[512,768]{1,0:T(8,128)(2,1)S(1)} %collective-permute-done.27.refs_3_.grad_other, ...), custom_call_target="tpu_custom_call" | custom-call | flops 1 | bytes 1 | tf_op jit(solution)/shard_map/feed_back/pallas_call | solution.py:626
  136.7 3.5 %weight_grad.3 = bf16[8,96,1536]{2,1,0:T(8,128)(2,1)S(1)} custom-call(s32[1]{0:T(128)} %bitcast.2.info.refs_0_, bf16[768,1024]{1,0:T(8,128)(2,1)S(1)} %get-tuple-element.163.refs_1_, bf16[1024,1536]{1,0:T(8,128)(2,1)S(1)} %get-tuple-element.164.refs_2_), custom_call_target="tpu_custom_call" | custom-call | flops 1 | bytes 1 | tf_op jit(solution)/shard_map/weight_grad/pallas_call | solution.py:677
  152.7 13.0 %attend_back.3 = (bf16[192,1024]{1,0:T(8,128)(2,1)S(1)}, bf16[192,1024]{1,0:T(8,128)(2,1)S(1)}, bf16[8,96,256]{2,1,0:T(8,128)(2,1)S(1)}) custom-call(s32[145]{0:T(256)S(1)} %get-tuple-element.118.plan.refs_0_, s32[3]{0:T(128)S(1)} %pad_add_fusion.place.info.refs_1_, bf16[512,768]{1,0:T(8,128)(2,1)S(1)} %copy-done.2, ...), custom_call_target="tpu_custom_call" | custom-call | flops 1 | bytes 1 | tf_op jit(solution)/shard_map/attend_back/pallas_call | solution.py:396
  173.1 12.8 %attend_back.4 = (bf16[192,1024]{1,0:T(8,128)(2,1)S(1)}, bf16[192,1024]{1,0:T(8,128)(2,1)S(1)}, bf16[8,96,256]{2,1,0:T(8,128)(2,1)S(1)}) custom-call(s32[145]{0:T(256)S(1)} %get-tuple-element.118.plan.refs_0_, s32[3]{0:T(128)S(1)} %pad_add_fusion.place.info.refs_1_, bf16[512,768]{1,0:T(8,128)(2,1)S(1)} %copy-done.2, ...), custom_call_target="tpu_custom_call" | custom-call | flops 1 | bytes 1 | tf_op jit(solution)/shard_map/attend_back/pallas_call | solution.py:396
  189.0 12.8 %attend_back.5 = (bf16[192,1024]{1,0:T(8,128)(2,1)S(1)}, bf16[192,1024]{1,0:T(8,128)(2,1)S(1)}, bf16[8,96,512]{2,1,0:T(8,128)(2,1)S(1)}) custom-call(s32[145]{0:T(256)S(1)} %get-tuple-element.118.plan.refs_0_, s32[3]{0:T(128)S(1)} %pad_add_fusion.place.info.refs_1_, bf16[512,768]{1,0:T(8,128)(2,1)S(1)} %copy-done.2, ...), custom_call_target="tpu_custom_call" | custom-call | flops 1 | bytes 1 | tf_op jit(solution)/shard_map/attend_back/pallas_call | solution.py:396
  207.3 6.7 %collective-permute-done.42.refs_5_ = bf16[192,1024]{1,0:T(8,128)(2,1)S(1)} collective-permute-done((bf16[192,1024]{1,0:T(8,128)(2,1)S(1)}, bf16[192,1024]{1,0:T(8,128)(2,1)S(1)}, u32[]{:S(2)}, u32[]{:S(2)}) %collective-permute-start.42) | collective-permute-done | bytes 393248 | tf_op jit(solution)/shard_map/ppermute | solution.py:941
  215.3 7.2 %collective-permute-start.50 = (bf16[1,96,640]{2,1,0:T(8,128)(2,1)S(1)}, bf16[1,96,640]{2,1,0:T(8,128)(2,1)S(1)}, u32[]{:S(2)}, u32[]{:S(2)}) collective-permute-start(bf16[1,96,640]{2,1,0:T(8,128)(2,1)S(1)} %slice.221), channel_id=1, source_target_pairs={{0,16},{4,20},{8,24},{12,28},{16,0},{20,4},{24,8},{28,12},{1,17},{... | collective-permute-start | bytes 368648 | tf_op jit(solution)/shard_map/ppermute | solution.py:935
  222.8 3.6 %input_back.1 = (f32[512,768]{1,0:T(8,128)S(1)}, bf16[512,768]{1,0:T(8,128)(2,1)S(1)}) custom-call(bf16[192,1024]{1,0:T(8,128)(2,1)S(1)} %get-tuple-element.183.refs_0_, bf16[192,1024]{1,0:T(8,128)(2,1)S(1)} %get-tuple-element.192.refs_1_, bf16[192,1024]{1,0:T(8,128)(2,1)S(1)} %get-tuple-element.201.refs_2_, ...), custom_call_target="tpu_custom_call" | custom-call | flops 1 | bytes 1 | tf_op jit(solution)/shard_map/input_back/pallas_call | solution.py:452
  227.8 2.0 collective-permute-done.47
  232.3 5.4 %collective-permute-done.51 = bf16[1,96,512]{2,1,0:T(8,128)(2,1)S(1)} collective-permute-done((bf16[1,96,512]{2,1,0:T(8,128)(2,1)S(1)}, bf16[1,96,512]{2,1,0:T(8,128)(2,1)S(1)}, u32[]{:S(2)}, u32[]{:S(2)}) %collective-permute-start.51) | collective-permute-done | bytes 98336 | tf_op jit(solution)/shard_map/ppermute | solution.py:935
  248.2 1.9 place_qkv.1
  (240 shorter events, 92.5 us)
Async XLA Ops:
  6.8 23.5 %collective-permute-start.1 = (bf16[512,768]{1,0:T(8,128)(2,1)}, bf16[512,768]{1,0:T(8,128)(2,1)S(1)}, u32[]{:S(2)}, u32[]{:S(2)}) collective-permute-start(bf16[512,768]{1,0:T(8,128)(2,1)} %refs_2_.5), channel_id=1, source_target_pairs={{0,2},{1,3},{2,0},{3,1},{4,6},{5,7},{6,4},{7,5},{8,10},{9,11},{10,... | collective-permute-start | bytes 2359304 | tf_op jit(solution)/shard_map/ppermute | solution.py:941
  19.1 11.1 %collective-permute-start.5 = (bf16[2,96,768]{2,1,0:T(8,128)(2,1)S(1)}, bf16[2,96,768]{2,1,0:T(8,128)(2,1)S(1)}, u32[]{:S(2)}, u32[]{:S(2)}) collective-permute-start(bf16[2,96,768]{2,1,0:T(8,128)(2,1)S(1)} %pad_maximum_fusion.6), channel_id=1, source_target_pairs={{0,8},{4,12},{8,0},{12,4},{16,24},{20,28},{24,16},{28,20},{1,9},{5... | collective-permute-start | bytes 884744 | tf_op jit(solution)/shard_map/ppermute | solution.py:935
  24.5 14.9 %collective-permute-start = (bf16[512,768]{1,0:T(8,128)(2,1)S(1)}, bf16[512,768]{1,0:T(8,128)(2,1)S(1)}, u32[]{:S(2)}, u32[]{:S(2)}) collective-permute-start(bf16[512,768]{1,0:T(8,128)(2,1)S(1)} %copy-done.2), channel_id=1, source_target_pairs={{0,1},{1,0},{2,3},{3,2},{4,5},{5,4},{6,7},{7,6},{8,9},{9,8},{10,11... | collective-permute-start | bytes 2359304 | tf_op jit(solution)/shard_map/ppermute | solution.py:938
  31.8 16.1 %collective-permute-start.9 = (bf16[4,96,768]{2,1,0:T(8,128)(2,1)}, bf16[4,96,768]{2,1,0:T(8,128)(2,1)}, u32[]{:S(2)}, u32[]{:S(2)}) collective-permute-start(bf16[4,96,768]{2,1,0:T(8,128)(2,1)} %pad_maximum_fusion.2.refs_0_), channel_id=1, source_target_pairs={{0,4},{4,0},{8,12},{12,8},{16,20},{20,16},{24,28},{28,24},{1,5},{5... | collective-permute-start | bytes 1769480 | tf_op jit(solution)/shard_map/ppermute | solution.py:935
  35.2 16.2 %collective-permute-start.11 = (bf16[1,96,1536]{2,1,0:T(8,128)(2,1)S(1)}, bf16[1,96,1536]{2,1,0:T(8,128)(2,1)}, u32[]{:S(2)}, u32[]{:S(2)}) collective-permute-start(bf16[1,96,1536]{2,1,0:T(8,128)(2,1)S(1)} %fusion.15), channel_id=1, source_target_pairs={{0,16},{4,20},{8,24},{12,28},{16,0},{20,4},{24,8},{28,12},{1,17},{... | collective-permute-start | bytes 884744 | tf_op jit(solution)/shard_map/ppermute | solution.py:935
  37.5 15.2 %collective-permute-start.10 = (bf16[1,192,768]{2,1,0:T(8,128)(2,1)}, bf16[1,192,768]{2,1,0:T(8,128)(2,1)S(1)}, u32[]{:S(2)}, u32[]{:S(2)}) collective-permute-start(bf16[1,192,768]{2,1,0:T(8,128)(2,1)} %select_bitcast_fusion), channel_id=1, source_target_pairs={{0,8},{4,12},{8,0},{12,4},{16,24},{20,28},{24,16},{28,20},{1,9},{5... | collective-permute-start | bytes 884744 | tf_op jit(solution)/shard_map/ppermute | solution.py:935
  49.4 15.4 %collective-permute-start.19 = (bf16[384,384]{1,0:T(8,128)(2,1)S(1)}, bf16[384,384]{1,0:T(8,128)(2,1)S(1)}, u32[]{:S(2)}, u32[]{:S(2)}) collective-permute-start(bf16[384,384]{1,0:T(8,128)(2,1)S(1)} %get-tuple-element.233), channel_id=1, source_target_pairs={{0,1},{1,0},{2,3},{3,2},{4,5},{5,4},{6,7},{7,6},{8,9},{9,8},{10,11... | collective-permute-start | bytes 884744 | tf_op jit(solution)/shard_map/ppermute | solution.py:938
  53.9 18.4 %collective-permute-start.13 = (bf16[2,192,768]{2,1,0:T(8,128)(2,1)S(1)}, bf16[2,192,768]{2,1,0:T(8,128)(2,1)S(1)}, u32[]{:S(2)}, u32[]{:S(2)}) collective-permute-start(bf16[2,192,768]{2,1,0:T(8,128)(2,1)S(1)} %pad_maximum_fusion.3), channel_id=1, source_target_pairs={{0,4},{4,0},{8,12},{12,8},{16,20},{20,16},{24,28},{28,24},{1,5},{5... | collective-permute-start | bytes 1769480 | tf_op jit(solution)/shard_map/ppermute | solution.py:935
  54.5 15.0 %collective-permute-start.12 = (bf16[2,96,1536]{2,1,0:T(8,128)(2,1)S(1)}, bf16[2,96,1536]{2,1,0:T(8,128)(2,1)S(1)}, u32[]{:S(2)}, u32[]{:S(2)}) collective-permute-start(bf16[2,96,1536]{2,1,0:T(8,128)(2,1)S(1)} %pad_maximum_fusion.4), channel_id=1, source_target_pairs={{0,8},{4,12},{8,0},{12,4},{16,24},{20,28},{24,16},{28,20},{1,9},{5... | collective-permute-start | bytes 1769480 | tf_op jit(solution)/shard_map/ppermute | solution.py:935
  54.5 29.8 %collective-permute-start.17 = (bf16[768,384]{1,0:T(8,128)(2,1)S(1)}, bf16[768,384]{1,0:T(8,128)(2,1)S(1)}, u32[]{:S(2)}, u32[]{:S(2)}) collective-permute-start(bf16[768,384]{1,0:T(8,128)(2,1)S(1)} %slice.199), channel_id=1, source_target_pairs={{0,2},{1,3},{2,0},{3,1},{4,6},{5,7},{6,4},{7,5},{8,10},{9,11},{10,... | collective-permute-start | bytes 1769480 | tf_op jit(solution)/shard_map/ppermute | solution.py:941
  55.9 28.3 %collective-permute-start.16 = (bf16[768,256]{1,0:T(8,128)(2,1)S(1)}, bf16[768,256]{1,0:T(8,128)(2,1)S(1)}, u32[]{:S(2)}, u32[]{:S(2)}) collective-permute-start(bf16[768,256]{1,0:T(8,128)(2,1)S(1)} %assemble.4.part), channel_id=1, source_target_pairs={{0,2},{1,3},{2,0},{3,1},{4,6},{5,7},{6,4},{7,5},{8,10},{9,11},{10,... | collective-permute-start | bytes 1179656 | tf_op jit(solution)/shard_map/ppermute | solution.py:941
  64.7 21.6 %collective-permute-start.14 = (bf16[64,1024]{1,0:T(8,128)(2,1)S(1)}, bf16[64,1024]{1,0:T(8,128)(2,1)S(1)}, u32[]{:S(2)}, u32[]{:S(2)}) collective-permute-start(bf16[64,1024]{1,0:T(8,128)(2,1)S(1)} %get-tuple-element.140), channel_id=1, source_target_pairs={{0,2},{1,3},{2,0},{3,1},{4,6},{5,7},{6,4},{7,5},{8,10},{9,11},{10,... | collective-permute-start | bytes 393224 | tf_op jit(solution)/shard_map/ppermute | solution.py:941
  70.5 26.8 %collective-permute-start.20 = (bf16[4,96,1536]{2,1,0:T(8,128)(2,1)S(1)}, bf16[4,96,1536]{2,1,0:T(8,128)(2,1)S(1)}, u32[]{:S(2)}, u32[]{:S(2)}) collective-permute-start(bf16[4,96,1536]{2,1,0:T(8,128)(2,1)S(1)} %pad_maximum_fusion.refs_0_), channel_id=1, source_target_pairs={{0,4},{4,0},{8,12},{12,8},{16,20},{20,16},{24,28},{28,24},{1,5},{5... | collective-permute-start | bytes 3538952 | tf_op jit(solution)/shard_map/ppermute | solution.py:935
  72.3 14.1 %collective-permute-start.15 = (bf16[64,1024]{1,0:T(8,128)(2,1)S(1)}, bf16[64,1024]{1,0:T(8,128)(2,1)S(1)}, u32[]{:S(2)}, u32[]{:S(2)}) collective-permute-start(bf16[64,1024]{1,0:T(8,128)(2,1)S(1)} %get-tuple-element.141), channel_id=1, source_target_pairs={{0,2},{1,3},{2,0},{3,1},{4,6},{5,7},{6,4},{7,5},{8,10},{9,11},{10,... | collective-permute-start | bytes 393224 | tf_op jit(solution)/shard_map/ppermute | solution.py:941
  84.9 29.1 %collective-permute-start.25 = (bf16[4,192,768]{2,1,0:T(8,128)(2,1)}, bf16[4,192,768]{2,1,0:T(8,128)(2,1)}, u32[]{:S(2)}, u32[]{:S(2)}) collective-permute-start(bf16[4,192,768]{2,1,0:T(8,128)(2,1)} %pad_maximum_fusion.1.refs_0_), channel_id=1, source_target_pairs={{0,2},{1,3},{2,0},{3,1},{4,6},{5,7},{6,4},{7,5},{8,10},{9,11},{10,... | collective-permute-start | bytes 3538952 | tf_op jit(solution)/shard_map/ppermute | solution.py:941
  129.0 36.8 %collective-permute-start.34 = (bf16[2,384,768]{2,1,0:T(8,128)(2,1)S(1)}, bf16[2,384,768]{2,1,0:T(8,128)(2,1)S(1)}, u32[]{:S(2)}, u32[]{:S(2)}) collective-permute-start(bf16[2,384,768]{2,1,0:T(8,128)(2,1)S(1)} %slice.207), channel_id=1, source_target_pairs={{0,8},{4,12},{8,0},{12,4},{16,24},{20,28},{24,16},{28,20},{1,9},{5... | collective-permute-start | bytes 3538952 | tf_op jit(solution)/shard_map/ppermute | solution.py:935
  140.3 28.0 %collective-permute-start.37 = (bf16[4,96,1536]{2,1,0:T(8,128)(2,1)S(1)}, bf16[4,96,1536]{2,1,0:T(8,128)(2,1)S(1)}, u32[]{:S(2)}, u32[]{:S(2)}) collective-permute-start(bf16[4,96,1536]{2,1,0:T(8,128)(2,1)S(1)} %slice.209), channel_id=1, source_target_pairs={{0,4},{4,0},{8,12},{12,8},{16,20},{20,16},{24,28},{28,24},{1,5},{5... | collective-permute-start | bytes 3538952 | tf_op jit(solution)/shard_map/ppermute | solution.py:935
  147.8 18.0 %collective-permute-start.35 = (bf16[64,1024]{1,0:T(8,128)(2,1)S(1)}, bf16[64,1024]{1,0:T(8,128)(2,1)S(1)}, u32[]{:S(2)}, u32[]{:S(2)}) collective-permute-start(bf16[64,1024]{1,0:T(8,128)(2,1)S(1)} %get-tuple-element.176), channel_id=1, source_target_pairs={{0,2},{1,3},{2,0},{3,1},{4,6},{5,7},{6,4},{7,5},{8,10},{9,11},{10,... | collective-permute-start | bytes 393224 | tf_op jit(solution)/shard_map/ppermute | solution.py:941
  148.4 17.4 %collective-permute-start.36 = (bf16[64,1024]{1,0:T(8,128)(2,1)S(1)}, bf16[64,1024]{1,0:T(8,128)(2,1)S(1)}, u32[]{:S(2)}, u32[]{:S(2)}) collective-permute-start(bf16[64,1024]{1,0:T(8,128)(2,1)S(1)} %get-tuple-element.177), channel_id=1, source_target_pairs={{0,2},{1,3},{2,0},{3,1},{4,6},{5,7},{6,4},{7,5},{8,10},{9,11},{10,... | collective-permute-start | bytes 393224 | tf_op jit(solution)/shard_map/ppermute | solution.py:941
  152.7 13.4 %collective-permute-start.33 = (bf16[384,384]{1,0:T(8,128)(2,1)S(1)}, bf16[384,384]{1,0:T(8,128)(2,1)S(1)}, u32[]{:S(2)}, u32[]{:S(2)}) collective-permute-start(bf16[384,384]{1,0:T(8,128)(2,1)S(1)} %get-tuple-element.184), channel_id=1, source_target_pairs={{0,1},{1,0},{2,3},{3,2},{4,5},{5,4},{6,7},{7,6},{8,9},{9,8},{10,11... | collective-permute-start | bytes 884744 | tf_op jit(solution)/shard_map/ppermute | solution.py:938
  168.3 18.3 %collective-permute-start.38 = (bf16[1,384,768]{2,1,0:T(8,128)(2,1)S(1)}, bf16[1,384,768]{2,1,0:T(8,128)(2,1)S(1)}, u32[]{:S(2)}, u32[]{:S(2)}) collective-permute-start(bf16[1,384,768]{2,1,0:T(8,128)(2,1)S(1)} %slice.211), channel_id=1, source_target_pairs={{0,4},{4,0},{8,12},{12,8},{16,20},{20,16},{24,28},{28,24},{1,5},{5... | collective-permute-start | bytes 1769480 | tf_op jit(solution)/shard_map/ppermute | solution.py:935
  170.2 16.6 %collective-permute-start.39 = (bf16[2,96,1536]{2,1,0:T(8,128)(2,1)S(1)}, bf16[2,96,1536]{2,1,0:T(8,128)(2,1)S(1)}, u32[]{:S(2)}, u32[]{:S(2)}) collective-permute-start(bf16[2,96,1536]{2,1,0:T(8,128)(2,1)S(1)} %slice.213), channel_id=1, source_target_pairs={{0,8},{4,12},{8,0},{12,4},{16,24},{20,28},{24,16},{28,20},{1,9},{5... | collective-permute-start | bytes 1769480 | tf_op jit(solution)/shard_map/ppermute | solution.py:935
  171.6 15.1 %collective-permute-start.40 = (bf16[192,1024]{1,0:T(8,128)(2,1)S(1)}, bf16[192,1024]{1,0:T(8,128)(2,1)S(1)}, u32[]{:S(2)}, u32[]{:S(2)}) collective-permute-start(bf16[192,1024]{1,0:T(8,128)(2,1)S(1)} %get-tuple-element.195), channel_id=1, source_target_pairs={{0,2},{1,3},{2,0},{3,1},{4,6},{5,7},{6,4},{7,5},{8,10},{9,11},{10,... | collective-permute-start | bytes 1179656 | tf_op jit(solution)/shard_map/ppermute | solution.py:941
  185.9 17.5 %collective-permute-start.41 = (bf16[192,1024]{1,0:T(8,128)(2,1)S(1)}, bf16[192,1024]{1,0:T(8,128)(2,1)S(1)}, u32[]{:S(2)}, u32[]{:S(2)}) collective-permute-start(bf16[192,1024]{1,0:T(8,128)(2,1)S(1)} %get-tuple-element.202), channel_id=1, source_target_pairs={{0,2},{1,3},{2,0},{3,1},{4,6},{5,7},{6,4},{7,5},{8,10},{9,11},{10,... | collective-permute-start | bytes 1179656 | tf_op jit(solution)/shard_map/ppermute | solution.py:941
  186.9 16.5 %collective-permute-start.43 = (bf16[1,96,1536]{2,1,0:T(8,128)(2,1)S(1)}, bf16[1,96,1536]{2,1,0:T(8,128)(2,1)S(1)}, u32[]{:S(2)}, u32[]{:S(2)}) collective-permute-start(bf16[1,96,1536]{2,1,0:T(8,128)(2,1)S(1)} %slice.215), channel_id=1, source_target_pairs={{0,16},{4,20},{8,24},{12,28},{16,0},{20,4},{24,8},{28,12},{1,17},{... | collective-permute-start | bytes 884744 | tf_op jit(solution)/shard_map/ppermute | solution.py:935
  188.4 15.0 %collective-permute-start.44 = (bf16[4,96,640]{2,1,0:T(8,128)(2,1)S(1)}, bf16[4,96,640]{2,1,0:T(8,128)(2,1)S(1)}, u32[]{:S(2)}, u32[]{:S(2)}) collective-permute-start(bf16[4,96,640]{2,1,0:T(8,128)(2,1)S(1)} %slice.172), channel_id=1, source_target_pairs={{0,4},{4,0},{8,12},{12,8},{16,20},{20,16},{24,28},{28,24},{1,5},{5... | collective-permute-start | bytes 1474568 | tf_op jit(solution)/shard_map/ppermute | solution.py:935
  201.9 12.1 %collective-permute-start.42 = (bf16[192,1024]{1,0:T(8,128)(2,1)S(1)}, bf16[192,1024]{1,0:T(8,128)(2,1)S(1)}, u32[]{:S(2)}, u32[]{:S(2)}) collective-permute-start(bf16[192,1024]{1,0:T(8,128)(2,1)S(1)} %get-tuple-element.203), channel_id=1, source_target_pairs={{0,2},{1,3},{2,0},{3,1},{4,6},{5,7},{6,4},{7,5},{8,10},{9,11},{10,... | collective-permute-start | bytes 1179656 | tf_op jit(solution)/shard_map/ppermute | solution.py:941
  203.7 10.3 %collective-permute-start.45 = (bf16[4,96,512]{2,1,0:T(8,128)(2,1)S(1)}, bf16[4,96,512]{2,1,0:T(8,128)(2,1)S(1)}, u32[]{:S(2)}, u32[]{:S(2)}) collective-permute-start(bf16[4,96,512]{2,1,0:T(8,128)(2,1)S(1)} %slice.174), channel_id=1, source_target_pairs={{0,4},{4,0},{8,12},{12,8},{16,20},{20,16},{24,28},{28,24},{1,5},{5... | collective-permute-start | bytes 1179656 | tf_op jit(solution)/shard_map/ppermute | solution.py:935
  205.3 24.6 %collective-permute-start.52 = (bf16[384,768]{1,0:T(8,128)(2,1)S(1)}, bf16[384,768]{1,0:T(8,128)(2,1)S(1)}, u32[]{:S(2)}, u32[]{:S(2)}) collective-permute-start(bf16[384,768]{1,0:T(8,128)(2,1)S(1)} %fusion), channel_id=1, source_target_pairs={{0,1},{1,17},{2,3},{3,19},{4,5},{5,21},{6,7},{7,23},{8,9},{9,25},{... | collective-permute-start | bytes 1769480 | tf_op jit(solution)/shard_map/ppermute | solution.py:949
  205.3 22.5 %collective-permute-start.48 = (bf16[96,1536]{1,0:T(8,128)(2,1)S(1)}, bf16[96,1536]{1,0:T(8,128)(2,1)S(1)}, u32[]{:S(2)}, u32[]{:S(2)}) collective-permute-start(bf16[96,1536]{1,0:T(8,128)(2,1)S(1)} %fusion.3), channel_id=1, source_target_pairs={{0,2},{1,3},{2,0},{3,1},{4,6},{5,7},{6,4},{7,5},{8,10},{9,11},{10,... | collective-permute-start | bytes 884744 | tf_op jit(solution)/shard_map/ppermute | solution.py:941
  215.3 12.4 %collective-permute-start.50 = (bf16[1,96,640]{2,1,0:T(8,128)(2,1)S(1)}, bf16[1,96,640]{2,1,0:T(8,128)(2,1)S(1)}, u32[]{:S(2)}, u32[]{:S(2)}) collective-permute-start(bf16[1,96,640]{2,1,0:T(8,128)(2,1)S(1)} %slice.221), channel_id=1, source_target_pairs={{0,16},{4,20},{8,24},{12,28},{16,0},{20,4},{24,8},{28,12},{1,17},{... | collective-permute-start | bytes 368648 | tf_op jit(solution)/shard_map/ppermute | solution.py:935
  226.4 14.9 %collective-permute-start.46 = (bf16[512,768]{1,0:T(8,128)(2,1)S(1)}, bf16[512,768]{1,0:T(8,128)(2,1)S(1)}, u32[]{:S(2)}, u32[]{:S(2)}) collective-permute-start(bf16[512,768]{1,0:T(8,128)(2,1)S(1)} %get-tuple-element.214), channel_id=1, source_target_pairs={{0,1},{1,0},{2,3},{3,2},{4,5},{5,4},{6,7},{7,6},{8,9},{9,8},{10,11... | collective-permute-start | bytes 2359304 | tf_op jit(solution)/shard_map/ppermute | solution.py:938
  (58 other events, 385.6 us)

commit v3 on v2

--- a/solution.py
+++ b/solution.py
@@ -461,9 +461,12 @@
     )(*grads, *weights)
 
 
-def place_qkv_kernel(start, info, chip, other, out, sums_out):
+def place_qkv_kernel(start, info, chip, other, out, mixed_out, sums_out):
     part = out.shape[1] // 3
     x, c = info[0] == 0, info[1] == 0
+    near, far = chip[:, :start].astype(F32), other[:, :start].astype(F32)
+    mixed_out[:, :start] = jnp.where(c, near, far)
+    mixed_out[:, start:] = jnp.where(c, far, near)
     values = [
         ref[:, start + dx * 768 : start + (dx + 1) * 768].astype(F32)
         for ref in (chip, other)
@@ -496,9 +499,11 @@
     block = chip.shape[0]
     return pl.pallas_call(
         partial(place_qkv_kernel, start),
-        out_shape=(shape((block, 3 * width), F32), shape((block, 8), F32)),
+        out_shape=(
+            shape((block, 3 * width), F32), shape((block, width), F32), shape((block, 8), F32)
+        ),
         in_specs=[SMEM] + [VMEM] * 2,
-        out_specs=(VMEM, VMEM),
+        out_specs=(VMEM,) * 3,
         compiler_params=params(8),
         cost_estimate=FREE,
         name="place_qkv",
@@ -800,7 +805,7 @@
         first_norm_kernel,
         grid=(1,),
         out_shape=(shape((rows // 2, width), BF),) * 2
-        + (shape((rows, width), F32), shape((rows, 1), F32)),
+        + (pltpu.HBM((rows, width), F32), pltpu.HBM((rows, 1), F32)),
         in_specs=[pl.BlockSpec((rows, width), lambda i: (0, 0))] * 2
         + [pl.BlockSpec((rows // 2, width), lambda i: (0, 0))] * 2
         + [pl.BlockSpec(vectors.shape, lambda i: (0, 0))],
@@ -1165,13 +1170,12 @@
     mixer_grad = (mine[:, :half_width].astype(F32) + theirs[:, :half_width].astype(F32)).astype(BF)
     chip = jnp.concatenate([mixer_grad, mine[:, half_width:], theirs[:, half_width:]], 1)
     other = swap_core(chip)
-    mixer_grad = ordered(cb, mixer_grad, other[:, :half_width], 1)
-    qkv_grad, sums = place_qkv(place, chip, other, half_width, width)
+    qkv_grad, mixer_grad, sums = place_qkv(place, chip, other, half_width, width)
     return (
         result,
         input_grad,
         qkv_grad,
-        mixer_grad.astype(F32),
+        mixer_grad,
         widen_grad,
         narrow_grad,
         sums[:, 0],

time: 252 us -> 250 us (level)
  starting transfers between devices: 60 us -> 66.9 us
  Pallas kernels: 110 us -> 105 us
    ppermute x22, starting transfers between devices: 36.4 us -> 42.5 us  [swap(): return lax.ppermute(value, 'shard', [(i, i ^ mask) for i in range(n_shard)])]
    pallas_call x3, Pallas kernels: 38.7 us -> 35.5 us  [attend_back(): pl.pallas_call(kernel, out_shape=(shape((TRIO, total // 2), BF),) * 2 + (...]
  transfers between devices with their start and end apart: 59 -> 59, of which waited for: 28 -> 27; matrix products, arithmetic and copies ran while one was open for 7% -> 7% of each run, Pallas kernels for 38% -> 36%
where the time goes in v3:
time: 250 us; the launch traced here: 249 us
  Pallas kernels  105 us (42%)
  starting transfers between devices  66.9 us (27%)
  waiting for transfers between devices  56.1 us (22%)
  other arithmetic  14.1 us (6%)
  local copies, waits for them, and re-layouts  4.39 us (2%)
    ppermute x22, starting transfers between devices, swap(): return lax.ppermute(value, 'shard', [(i, i ^ mask) for i in range(n_shard)])  42.5 us
    pallas_call x3, Pallas kernels, attend_back(): pl.pallas_call(kernel, out_shape=(shape((TRIO, total // 2), BF),) * 2 + (...  35.5 us
    ppermute x22, waiting for transfers between devices, swap(): return lax.ppermute(value, 'shard', [(i, i ^ mask) for i in range(n_shard)])  31.9 us
    pallas_call x3, Pallas kernels, attend(): pl.pallas_call(attend_kernel, out_shape=(shape((HEAD_DIM, half), BF), sha...  22.4 us
    ppermute x16, starting transfers between devices, swap_x(): return lax.ppermute(value, 'seq', [(i, i ^ 2) for i in range(4)])  19 us
    ppermute x16, waiting for transfers between devices, swap_x(): return lax.ppermute(value, 'seq', [(i, i ^ 2) for i in range(4)])  13.3 us
    ppermute x19, waiting for transfers between devices, swap_core(): return lax.ppermute(value, 'seq', [(i, i ^ 1) for i in range(4)])  11 us
    pallas_call x1, Pallas kernels, feed_up(): pl.pallas_call(feed_up_kernel, out_shape=(shape((4 * rows, hidden), BF),...  6.94 us
  transfers between devices with their start and end apart: 59, of which 27 were waited for; matrix products, arithmetic and copies ran while one was open for 7% of the time, Pallas kernels for 36%

profile of v3, /device:TPU:0, one launch (start us, length us, event | category | flops | bytes accessed | tf_op | source)
XLA Modules:
  0.0 249.3 jit_solution(13227044772636457994)
XLA Ops:
  2.7 4.1 %collective-permute-start.2 = (bf16[1,96,256]{2,1,0:T(8,128)(2,1)S(1)}, bf16[1,96,256]{2,1,0:T(8,128)(2,1)S(1)}, u32[]{:S(2)}, u32[]{:S(2)}) collective-permute-start(bf16[1,96,256]{2,1,0:T(8,128)(2,1)S(1)} %bitcast.32), channel_id=1, source_target_pairs={{0,16},{4,20},{8,24},{12,28},{16,0},{20,4},{24,8},{28,12},{1,17},{... | collective-permute-start | bytes 147464 | tf_op jit(solution)/shard_map/ppermute | solution.py:940
  9.4 2.4 collective-permute-start.3
  14.4 2.0 collective-permute-start.4
  24.5 5.7 %collective-permute-done.5 = bf16[2,96,768]{2,1,0:T(8,128)(2,1)S(1)} collective-permute-done((bf16[2,96,768]{2,1,0:T(8,128)(2,1)S(1)}, bf16[2,96,768]{2,1,0:T(8,128)(2,1)S(1)}, u32[]{:S(2)}, u32[]{:S(2)}) %collective-permute-start.5) | collective-permute-done | bytes 294944 | tf_op jit(solution)/shard_map/ppermute | solution.py:940
  39.4 7.4 %attend.3 = (bf16[64,1024]{1,0:T(8,128)(2,1)S(1)}, bf16[64,1024]{1,0:T(8,128)(2,1)S(1)}, f32[64,2048]{1,0:T(8,128)S(1)}, f32[1,2048]{1,0:T(1,128)S(1)}) custom-call(s32[145]{0:T(256)S(1)} %get-tuple-element.119.plan.refs_0_, bf16[512,768]{1,0:T(8,128)(2,1)S(1)} %copy-done.2, bf16[512,768]{1,0:T(8,128)(2,1)S(1)} %collective-permute-done.tok1.refs_3_, ...), custom_call_target="tpu_custom_call" | custom-call | flops 1 | bytes 1 | tf_op jit(solution)/shard_map/attend/pallas_call | solution.py:260
  56.5 7.4 %attend.4 = (bf16[64,1024]{1,0:T(8,128)(2,1)S(1)}, bf16[64,1024]{1,0:T(8,128)(2,1)S(1)}, f32[64,2048]{1,0:T(8,128)S(1)}, f32[1,2048]{1,0:T(1,128)S(1)}) custom-call(s32[145]{0:T(256)S(1)} %get-tuple-element.119.plan.refs_0_, bf16[512,768]{1,0:T(8,128)(2,1)S(1)} %copy-done.2, bf16[512,768]{1,0:T(8,128)(2,1)S(1)} %collective-permute-done.tok1.refs_3_, ...), custom_call_target="tpu_custom_call" | custom-call | flops 1 | bytes 1 | tf_op jit(solution)/shard_map/attend/pallas_call | solution.py:260
  65.7 3.8 %collective-permute-done.12 = bf16[2,96,1536]{2,1,0:T(8,128)(2,1)S(1)} collective-permute-done((bf16[2,96,1536]{2,1,0:T(8,128)(2,1)S(1)}, bf16[2,96,1536]{2,1,0:T(8,128)(2,1)S(1)}, u32[]{:S(2)}, u32[]{:S(2)}) %collective-permute-start.12) | collective-permute-done | bytes 589856 | tf_op jit(solution)/shard_map/ppermute | solution.py:940
  73.7 2.1 pad_maximum_fusion.1.refs_0_
  75.8 7.6 %attend.5 = (bf16[64,1024]{1,0:T(8,128)(2,1)S(1)}, bf16[64,1024]{1,0:T(8,128)(2,1)S(1)}, f32[64,2048]{1,0:T(8,128)S(1)}, f32[1,2048]{1,0:T(1,128)S(1)}) custom-call(s32[145]{0:T(256)S(1)} %get-tuple-element.119.plan.refs_0_, bf16[512,768]{1,0:T(8,128)(2,1)S(1)} %copy-done.2, bf16[512,768]{1,0:T(8,128)(2,1)S(1)} %collective-permute-done.tok1.refs_3_, ...), custom_call_target="tpu_custom_call" | custom-call | flops 1 | bytes 1 | tf_op jit(solution)/shard_map/attend/pallas_call | solution.py:260
  85.7 4.3 %collective-permute-done.18 = bf16[64,1024]{1,0:T(8,128)(2,1)S(1)} collective-permute-done((bf16[64,1024]{1,0:T(8,128)(2,1)S(1)}, bf16[64,1024]{1,0:T(8,128)(2,1)S(1)}, u32[]{:S(2)}, u32[]{:S(2)}) %collective-permute-start.18) | collective-permute-done | bytes 131104 | tf_op jit(solution)/shard_map/ppermute | solution.py:946
  91.1 6.2 %collective-permute-done.20.refs_1_ = bf16[4,96,1536]{2,1,0:T(8,128)(2,1)S(1)} collective-permute-done((bf16[4,96,1536]{2,1,0:T(8,128)(2,1)S(1)}, bf16[4,96,1536]{2,1,0:T(8,128)(2,1)S(1)}, u32[]{:S(2)}, u32[]{:S(2)}) %collective-permute-start.20) | collective-permute-done | bytes 1179680 | tf_op jit(solution)/shard_map/ppermute | solution.py:940
  100.7 2.5 %first_norm.1 = (bf16[256,768]{1,0:T(8,128)(2,1)}, bf16[256,768]{1,0:T(8,128)(2,1)}, f32[512,768]{1,0:T(8,128)}, f32[512,1]{1,0:T(8,128)}) custom-call(bf16[512,768]{1,0:T(8,128)(2,1)S(1)} %copy-done.2, f32[1024,768]{1,0:T(8,128)S(1)} %fusion.11.mixed, bf16[256,768]{1,0:T(8,128)(2,1)S(1)} %collective-permute-done.21.recv0, ...), custom_call_target="tpu_custom_call" | custom-call | flops 1 | bytes 1 | tf_op jit(solution)/shard_map/first_norm/pallas_call | solution.py:804
  105.8 6.9 %feed_up.1 = (bf16[1024,1536]{1,0:T(8,128)(2,1)S(1)}, bf16[1536,1024]{1,0:T(8,128)(2,1)S(1)}, bf16[1024,1536]{1,0:T(8,128)(2,1)S(1)}, bf16[768,1024]{1,0:T(8,128)(2,1)S(1)}) custom-call(bf16[256,768]{1,0:T(8,128)(2,1)} %get-tuple-element.148.low0, bf16[256,768]{1,0:T(8,128)(2,1)} %get-tuple-element.149.low1, bf16[256,768]{1,0:T(8,128)(2,1)} %collective-permute-done.23.low2, ...), custom_call_target="tpu_custom_call" | custom-call | flops 1 | bytes 1 | tf_op jit(solution)/shard_map/feed_up/pallas_call | solution.py:546
  114.5 3.2 %feed_down.1 = (f32[512,768]{1,0:T(8,128)S(1)}, bf16[512,768]{1,0:T(8,128)(2,1)S(1)}) custom-call(bf16[1024,1536]{1,0:T(8,128)(2,1)S(1)} %get-tuple-element.150.act, bf16[1536,768]{1,0:T(8,128)(2,1)S(1)} %assemble.7.down), custom_call_target="tpu_custom_call" | custom-call | flops 1 | bytes 1 | tf_op jit(solution)/shard_map/feed_down/pallas_call | solution.py:587
  117.9 2.1 collective-permute-done.26.recv
  120.1 2.4 second_norm.1
  122.6 2.1 collective-permute-done.27.refs_3_.grad_other
  124.7 3.0 %weight_grad.2 = bf16[4,384,768]{2,1,0:T(8,128)(2,1)S(1)} custom-call(s32[1]{0:T(128)} %bitcast.12.refs_0_, bf16[1536,1024]{1,0:T(8,128)(2,1)S(1)} %get-tuple-element.158.refs_1_, bf16[512,768]{1,0:T(8,128)(2,1)S(1)} %get-tuple-element.159.refs_2_.grad_own, bf16[512,768]{1,0:T(8,128)(2,1)S(1)} %collective-permute-done.27.refs_3_.grad_other), custom_call_target="tpu_custom_call" | custom-call | flops 1 | bytes 1 | tf_op jit(solution)/shard_map/weight_grad/pallas_call | solution.py:682
  129.1 6.5 %feed_back.1 = (f32[512,768]{1,0:T(8,128)S(1)}, bf16[256,768]{1,0:T(8,128)(2,1)S(1)}, bf16[256,768]{1,0:T(8,128)(2,1)S(1)}, bf16[1024,1536]{1,0:T(8,128)(2,1)S(1)}) custom-call(bf16[512,768]{1,0:T(8,128)(2,1)S(1)} %get-tuple-element.159.refs_2_.grad_own, bf16[512,768]{1,0:T(8,128)(2,1)S(1)} %collective-permute-done.27.refs_3_.grad_other, ...), custom_call_target="tpu_custom_call" | custom-call | flops 1 | bytes 1 | tf_op jit(solution)/shard_map/feed_back/pallas_call | solution.py:631
  136.2 3.5 %weight_grad.3 = bf16[8,96,1536]{2,1,0:T(8,128)(2,1)S(1)} custom-call(s32[1]{0:T(128)} %bitcast.2.info.refs_0_, bf16[768,1024]{1,0:T(8,128)(2,1)S(1)} %get-tuple-element.164.refs_1_, bf16[1024,1536]{1,0:T(8,128)(2,1)S(1)} %get-tuple-element.165.refs_2_), custom_call_target="tpu_custom_call" | custom-call | flops 1 | bytes 1 | tf_op jit(solution)/shard_map/weight_grad/pallas_call | solution.py:682
  151.6 12.0 %attend_back.3 = (bf16[192,1024]{1,0:T(8,128)(2,1)S(1)}, bf16[192,1024]{1,0:T(8,128)(2,1)S(1)}, bf16[8,96,256]{2,1,0:T(8,128)(2,1)S(1)}) custom-call(s32[145]{0:T(256)S(1)} %get-tuple-element.119.plan.refs_0_, s32[3]{0:T(128)S(1)} %pad_add_fusion.place.info.refs_1_, bf16[512,768]{1,0:T(8,128)(2,1)S(1)} %copy-done.2, ...), custom_call_target="tpu_custom_call" | custom-call | flops 1 | bytes 1 | tf_op jit(solution)/shard_map/attend_back/pallas_call | solution.py:396
  164.7 3.0 %collective-permute-done.37 = bf16[4,96,1536]{2,1,0:T(8,128)(2,1)S(1)} collective-permute-done((bf16[4,96,1536]{2,1,0:T(8,128)(2,1)S(1)}, bf16[4,96,1536]{2,1,0:T(8,128)(2,1)S(1)}, u32[]{:S(2)}, u32[]{:S(2)}) %collective-permute-start.37) | collective-permute-done | bytes 1179680 | tf_op jit(solution)/shard_map/ppermute | solution.py:940
  171.9 11.7 %attend_back.4 = (bf16[192,1024]{1,0:T(8,128)(2,1)S(1)}, bf16[192,1024]{1,0:T(8,128)(2,1)S(1)}, bf16[8,96,256]{2,1,0:T(8,128)(2,1)S(1)}) custom-call(s32[145]{0:T(256)S(1)} %get-tuple-element.119.plan.refs_0_, s32[3]{0:T(128)S(1)} %pad_add_fusion.place.info.refs_1_, bf16[512,768]{1,0:T(8,128)(2,1)S(1)} %copy-done.2, ...), custom_call_target="tpu_custom_call" | custom-call | flops 1 | bytes 1 | tf_op jit(solution)/shard_map/attend_back/pallas_call | solution.py:396
  184.7 2.9 %collective-permute-start.43 = (bf16[1,96,1536]{2,1,0:T(8,128)(2,1)S(1)}, bf16[1,96,1536]{2,1,0:T(8,128)(2,1)S(1)}, u32[]{:S(2)}, u32[]{:S(2)}) collective-permute-start(bf16[1,96,1536]{2,1,0:T(8,128)(2,1)S(1)} %slice.211), channel_id=1, source_target_pairs={{0,16},{4,20},{8,24},{12,28},{16,0},{20,4},{24,8},{28,12},{1,17},{... | collective-permute-start | bytes 884744 | tf_op jit(solution)/shard_map/ppermute | solution.py:940
  189.1 11.8 %attend_back.5 = (bf16[192,1024]{1,0:T(8,128)(2,1)S(1)}, bf16[192,1024]{1,0:T(8,128)(2,1)S(1)}, bf16[8,96,512]{2,1,0:T(8,128)(2,1)S(1)}) custom-call(s32[145]{0:T(256)S(1)} %get-tuple-element.119.plan.refs_0_, s32[3]{0:T(128)S(1)} %pad_add_fusion.place.info.refs_1_, bf16[512,768]{1,0:T(8,128)(2,1)S(1)} %copy-done.2, ...), custom_call_target="tpu_custom_call" | custom-call | flops 1 | bytes 1 | tf_op jit(solution)/shard_map/attend_back/pallas_call | solution.py:396
  201.8 3.0 %collective-permute-start.45 = (bf16[4,96,512]{2,1,0:T(8,128)(2,1)S(1)}, bf16[4,96,512]{2,1,0:T(8,128)(2,1)S(1)}, u32[]{:S(2)}, u32[]{:S(2)}) collective-permute-start(bf16[4,96,512]{2,1,0:T(8,128)(2,1)S(1)} %slice.171), channel_id=1, source_target_pairs={{0,4},{4,0},{8,12},{12,8},{16,20},{20,16},{24,28},{28,24},{1,5},{5... | collective-permute-start | bytes 1179656 | tf_op jit(solution)/shard_map/ppermute | solution.py:940
  206.8 6.1 %collective-permute-done.42.refs_5_ = bf16[192,1024]{1,0:T(8,128)(2,1)S(1)} collective-permute-done((bf16[192,1024]{1,0:T(8,128)(2,1)S(1)}, bf16[192,1024]{1,0:T(8,128)(2,1)S(1)}, u32[]{:S(2)}, u32[]{:S(2)}) %collective-permute-start.42) | collective-permute-done | bytes 393248 | tf_op jit(solution)/shard_map/ppermute | solution.py:946
  213.8 7.1 %collective-permute-start.50 = (bf16[1,96,640]{2,1,0:T(8,128)(2,1)S(1)}, bf16[1,96,640]{2,1,0:T(8,128)(2,1)S(1)}, u32[]{:S(2)}, u32[]{:S(2)}) collective-permute-start(bf16[1,96,640]{2,1,0:T(8,128)(2,1)S(1)} %slice.217), channel_id=1, source_target_pairs={{0,16},{4,20},{8,24},{12,28},{16,0},{20,4},{24,8},{28,12},{1,17},{... | collective-permute-start | bytes 368648 | tf_op jit(solution)/shard_map/ppermute | solution.py:940
  221.1 3.0 %collective-permute-start.47 = (bf16[2,96,512]{2,1,0:T(8,128)(2,1)S(1)}, bf16[2,96,512]{2,1,0:T(8,128)(2,1)S(1)}, u32[]{:S(2)}, u32[]{:S(2)}) collective-permute-start(bf16[2,96,512]{2,1,0:T(8,128)(2,1)S(1)} %slice.213), channel_id=1, source_target_pairs={{0,8},{4,12},{8,0},{12,4},{16,24},{20,28},{24,16},{28,20},{1,9},{5... | collective-permute-start | bytes 589832 | tf_op jit(solution)/shard_map/ppermute | solution.py:940
  224.2 3.6 %input_back.1 = (f32[512,768]{1,0:T(8,128)S(1)}, bf16[512,768]{1,0:T(8,128)(2,1)S(1)}) custom-call(bf16[192,1024]{1,0:T(8,128)(2,1)S(1)} %get-tuple-element.184.refs_0_, bf16[192,1024]{1,0:T(8,128)(2,1)S(1)} %get-tuple-element.193.refs_1_, bf16[192,1024]{1,0:T(8,128)(2,1)S(1)} %get-tuple-element.202.refs_2_, ...), custom_call_target="tpu_custom_call" | custom-call | flops 1 | bytes 1 | tf_op jit(solution)/shard_map/input_back/pallas_call | solution.py:452
  232.7 4.9 %collective-permute-done.51 = bf16[1,96,512]{2,1,0:T(8,128)(2,1)S(1)} collective-permute-done((bf16[1,96,512]{2,1,0:T(8,128)(2,1)S(1)}, bf16[1,96,512]{2,1,0:T(8,128)(2,1)S(1)}, u32[]{:S(2)}, u32[]{:S(2)}) %collective-permute-start.51) | collective-permute-done | bytes 98336 | tf_op jit(solution)/shard_map/ppermute | solution.py:940
  246.6 2.0 place_qkv.1
  (234 shorter events, 91.3 us)
Async XLA Ops:
  6.8 23.5 %collective-permute-start.1 = (bf16[512,768]{1,0:T(8,128)(2,1)}, bf16[512,768]{1,0:T(8,128)(2,1)S(1)}, u32[]{:S(2)}, u32[]{:S(2)}) collective-permute-start(bf16[512,768]{1,0:T(8,128)(2,1)} %refs_2_.5), channel_id=1, source_target_pairs={{0,2},{1,3},{2,0},{3,1},{4,6},{5,7},{6,4},{7,5},{8,10},{9,11},{10,... | collective-permute-start | bytes 2359304 | tf_op jit(solution)/shard_map/ppermute | solution.py:946
  19.1 11.1 %collective-permute-start.5 = (bf16[2,96,768]{2,1,0:T(8,128)(2,1)S(1)}, bf16[2,96,768]{2,1,0:T(8,128)(2,1)S(1)}, u32[]{:S(2)}, u32[]{:S(2)}) collective-permute-start(bf16[2,96,768]{2,1,0:T(8,128)(2,1)S(1)} %pad_maximum_fusion.6), channel_id=1, source_target_pairs={{0,8},{4,12},{8,0},{12,4},{16,24},{20,28},{24,16},{28,20},{1,9},{5... | collective-permute-start | bytes 884744 | tf_op jit(solution)/shard_map/ppermute | solution.py:940
  24.5 14.9 %collective-permute-start = (bf16[512,768]{1,0:T(8,128)(2,1)S(1)}, bf16[512,768]{1,0:T(8,128)(2,1)S(1)}, u32[]{:S(2)}, u32[]{:S(2)}) collective-permute-start(bf16[512,768]{1,0:T(8,128)(2,1)S(1)} %copy-done.2), channel_id=1, source_target_pairs={{0,1},{1,0},{2,3},{3,2},{4,5},{5,4},{6,7},{7,6},{8,9},{9,8},{10,11... | collective-permute-start | bytes 2359304 | tf_op jit(solution)/shard_map/ppermute | solution.py:943
  31.8 16.1 %collective-permute-start.9 = (bf16[4,96,768]{2,1,0:T(8,128)(2,1)}, bf16[4,96,768]{2,1,0:T(8,128)(2,1)}, u32[]{:S(2)}, u32[]{:S(2)}) collective-permute-start(bf16[4,96,768]{2,1,0:T(8,128)(2,1)} %pad_maximum_fusion.2.refs_0_), channel_id=1, source_target_pairs={{0,4},{4,0},{8,12},{12,8},{16,20},{20,16},{24,28},{28,24},{1,5},{5... | collective-permute-start | bytes 1769480 | tf_op jit(solution)/shard_map/ppermute | solution.py:940
  35.2 16.2 %collective-permute-start.11 = (bf16[1,96,1536]{2,1,0:T(8,128)(2,1)S(1)}, bf16[1,96,1536]{2,1,0:T(8,128)(2,1)}, u32[]{:S(2)}, u32[]{:S(2)}) collective-permute-start(bf16[1,96,1536]{2,1,0:T(8,128)(2,1)S(1)} %fusion.14), channel_id=1, source_target_pairs={{0,16},{4,20},{8,24},{12,28},{16,0},{20,4},{24,8},{28,12},{1,17},{... | collective-permute-start | bytes 884744 | tf_op jit(solution)/shard_map/ppermute | solution.py:940
  37.5 15.2 %collective-permute-start.10 = (bf16[1,192,768]{2,1,0:T(8,128)(2,1)}, bf16[1,192,768]{2,1,0:T(8,128)(2,1)S(1)}, u32[]{:S(2)}, u32[]{:S(2)}) collective-permute-start(bf16[1,192,768]{2,1,0:T(8,128)(2,1)} %select_bitcast_fusion), channel_id=1, source_target_pairs={{0,8},{4,12},{8,0},{12,4},{16,24},{20,28},{24,16},{28,20},{1,9},{5... | collective-permute-start | bytes 884744 | tf_op jit(solution)/shard_map/ppermute | solution.py:940
  49.4 14.6 %collective-permute-start.19 = (bf16[384,384]{1,0:T(8,128)(2,1)S(1)}, bf16[384,384]{1,0:T(8,128)(2,1)S(1)}, u32[]{:S(2)}, u32[]{:S(2)}) collective-permute-start(bf16[384,384]{1,0:T(8,128)(2,1)S(1)} %get-tuple-element.235), channel_id=1, source_target_pairs={{0,1},{1,0},{2,3},{3,2},{4,5},{5,4},{6,7},{7,6},{8,9},{9,8},{10,11... | collective-permute-start | bytes 884744 | tf_op jit(solution)/shard_map/ppermute | solution.py:943
  53.9 18.4 %collective-permute-start.13 = (bf16[2,192,768]{2,1,0:T(8,128)(2,1)S(1)}, bf16[2,192,768]{2,1,0:T(8,128)(2,1)S(1)}, u32[]{:S(2)}, u32[]{:S(2)}) collective-permute-start(bf16[2,192,768]{2,1,0:T(8,128)(2,1)S(1)} %pad_maximum_fusion.3), channel_id=1, source_target_pairs={{0,4},{4,0},{8,12},{12,8},{16,20},{20,16},{24,28},{28,24},{1,5},{5... | collective-permute-start | bytes 1769480 | tf_op jit(solution)/shard_map/ppermute | solution.py:940
  54.5 15.0 %collective-permute-start.12 = (bf16[2,96,1536]{2,1,0:T(8,128)(2,1)S(1)}, bf16[2,96,1536]{2,1,0:T(8,128)(2,1)S(1)}, u32[]{:S(2)}, u32[]{:S(2)}) collective-permute-start(bf16[2,96,1536]{2,1,0:T(8,128)(2,1)S(1)} %pad_maximum_fusion.4), channel_id=1, source_target_pairs={{0,8},{4,12},{8,0},{12,4},{16,24},{20,28},{24,16},{28,20},{1,9},{5... | collective-permute-start | bytes 1769480 | tf_op jit(solution)/shard_map/ppermute | solution.py:940
  54.5 29.0 %collective-permute-start.17 = (bf16[768,384]{1,0:T(8,128)(2,1)S(1)}, bf16[768,384]{1,0:T(8,128)(2,1)S(1)}, u32[]{:S(2)}, u32[]{:S(2)}) collective-permute-start(bf16[768,384]{1,0:T(8,128)(2,1)S(1)} %slice.195), channel_id=1, source_target_pairs={{0,2},{1,3},{2,0},{3,1},{4,6},{5,7},{6,4},{7,5},{8,10},{9,11},{10,... | collective-permute-start | bytes 1769480 | tf_op jit(solution)/shard_map/ppermute | solution.py:946
  55.9 27.6 %collective-permute-start.16 = (bf16[768,256]{1,0:T(8,128)(2,1)S(1)}, bf16[768,256]{1,0:T(8,128)(2,1)S(1)}, u32[]{:S(2)}, u32[]{:S(2)}) collective-permute-start(bf16[768,256]{1,0:T(8,128)(2,1)S(1)} %assemble.4.part), channel_id=1, source_target_pairs={{0,2},{1,3},{2,0},{3,1},{4,6},{5,7},{6,4},{7,5},{8,10},{9,11},{10,... | collective-permute-start | bytes 1179656 | tf_op jit(solution)/shard_map/ppermute | solution.py:946
  64.0 21.6 %collective-permute-start.14 = (bf16[64,1024]{1,0:T(8,128)(2,1)S(1)}, bf16[64,1024]{1,0:T(8,128)(2,1)S(1)}, u32[]{:S(2)}, u32[]{:S(2)}) collective-permute-start(bf16[64,1024]{1,0:T(8,128)(2,1)S(1)} %get-tuple-element.141), channel_id=1, source_target_pairs={{0,2},{1,3},{2,0},{3,1},{4,6},{5,7},{6,4},{7,5},{8,10},{9,11},{10,... | collective-permute-start | bytes 393224 | tf_op jit(solution)/shard_map/ppermute | solution.py:946
  70.5 26.8 %collective-permute-start.20 = (bf16[4,96,1536]{2,1,0:T(8,128)(2,1)S(1)}, bf16[4,96,1536]{2,1,0:T(8,128)(2,1)S(1)}, u32[]{:S(2)}, u32[]{:S(2)}) collective-permute-start(bf16[4,96,1536]{2,1,0:T(8,128)(2,1)S(1)} %pad_maximum_fusion.refs_0_), channel_id=1, source_target_pairs={{0,4},{4,0},{8,12},{12,8},{16,20},{20,16},{24,28},{28,24},{1,5},{5... | collective-permute-start | bytes 3538952 | tf_op jit(solution)/shard_map/ppermute | solution.py:940
  72.3 13.4 %collective-permute-start.15 = (bf16[64,1024]{1,0:T(8,128)(2,1)S(1)}, bf16[64,1024]{1,0:T(8,128)(2,1)S(1)}, u32[]{:S(2)}, u32[]{:S(2)}) collective-permute-start(bf16[64,1024]{1,0:T(8,128)(2,1)S(1)} %get-tuple-element.142), channel_id=1, source_target_pairs={{0,2},{1,3},{2,0},{3,1},{4,6},{5,7},{6,4},{7,5},{8,10},{9,11},{10,... | collective-permute-start | bytes 393224 | tf_op jit(solution)/shard_map/ppermute | solution.py:946
  84.2 28.6 %collective-permute-start.25 = (bf16[4,192,768]{2,1,0:T(8,128)(2,1)}, bf16[4,192,768]{2,1,0:T(8,128)(2,1)}, u32[]{:S(2)}, u32[]{:S(2)}) collective-permute-start(bf16[4,192,768]{2,1,0:T(8,128)(2,1)} %pad_maximum_fusion.1.refs_0_), channel_id=1, source_target_pairs={{0,2},{1,3},{2,0},{3,1},{4,6},{5,7},{6,4},{7,5},{8,10},{9,11},{10,... | collective-permute-start | bytes 3538952 | tf_op jit(solution)/shard_map/ppermute | solution.py:946
  127.8 35.8 %collective-permute-start.34 = (bf16[2,384,768]{2,1,0:T(8,128)(2,1)S(1)}, bf16[2,384,768]{2,1,0:T(8,128)(2,1)S(1)}, u32[]{:S(2)}, u32[]{:S(2)}) collective-permute-start(bf16[2,384,768]{2,1,0:T(8,128)(2,1)S(1)} %slice.203), channel_id=1, source_target_pairs={{0,8},{4,12},{8,0},{12,4},{16,24},{20,28},{24,16},{28,20},{1,9},{5... | collective-permute-start | bytes 3538952 | tf_op jit(solution)/shard_map/ppermute | solution.py:940
  139.7 28.0 %collective-permute-start.37 = (bf16[4,96,1536]{2,1,0:T(8,128)(2,1)S(1)}, bf16[4,96,1536]{2,1,0:T(8,128)(2,1)S(1)}, u32[]{:S(2)}, u32[]{:S(2)}) collective-permute-start(bf16[4,96,1536]{2,1,0:T(8,128)(2,1)S(1)} %slice.205), channel_id=1, source_target_pairs={{0,4},{4,0},{8,12},{12,8},{16,20},{20,16},{24,28},{28,24},{1,5},{5... | collective-permute-start | bytes 3538952 | tf_op jit(solution)/shard_map/ppermute | solution.py:940
  146.7 16.9 %collective-permute-start.35 = (bf16[64,1024]{1,0:T(8,128)(2,1)S(1)}, bf16[64,1024]{1,0:T(8,128)(2,1)S(1)}, u32[]{:S(2)}, u32[]{:S(2)}) collective-permute-start(bf16[64,1024]{1,0:T(8,128)(2,1)S(1)} %get-tuple-element.177), channel_id=1, source_target_pairs={{0,2},{1,3},{2,0},{3,1},{4,6},{5,7},{6,4},{7,5},{8,10},{9,11},{10,... | collective-permute-start | bytes 393224 | tf_op jit(solution)/shard_map/ppermute | solution.py:946
  147.3 16.3 %collective-permute-start.36 = (bf16[64,1024]{1,0:T(8,128)(2,1)S(1)}, bf16[64,1024]{1,0:T(8,128)(2,1)S(1)}, u32[]{:S(2)}, u32[]{:S(2)}) collective-permute-start(bf16[64,1024]{1,0:T(8,128)(2,1)S(1)} %get-tuple-element.178), channel_id=1, source_target_pairs={{0,2},{1,3},{2,0},{3,1},{4,6},{5,7},{6,4},{7,5},{8,10},{9,11},{10,... | collective-permute-start | bytes 393224 | tf_op jit(solution)/shard_map/ppermute | solution.py:946
  151.6 12.3 %collective-permute-start.33 = (bf16[384,384]{1,0:T(8,128)(2,1)S(1)}, bf16[384,384]{1,0:T(8,128)(2,1)S(1)}, u32[]{:S(2)}, u32[]{:S(2)}) collective-permute-start(bf16[384,384]{1,0:T(8,128)(2,1)S(1)} %get-tuple-element.185), channel_id=1, source_target_pairs={{0,1},{1,0},{2,3},{3,2},{4,5},{5,4},{6,7},{7,6},{8,9},{9,8},{10,11... | collective-permute-start | bytes 884744 | tf_op jit(solution)/shard_map/ppermute | solution.py:943
  167.7 16.6 %collective-permute-start.38 = (bf16[1,384,768]{2,1,0:T(8,128)(2,1)S(1)}, bf16[1,384,768]{2,1,0:T(8,128)(2,1)S(1)}, u32[]{:S(2)}, u32[]{:S(2)}) collective-permute-start(bf16[1,384,768]{2,1,0:T(8,128)(2,1)S(1)} %slice.207), channel_id=1, source_target_pairs={{0,4},{4,0},{8,12},{12,8},{16,20},{20,16},{24,28},{28,24},{1,5},{5... | collective-permute-start | bytes 1769480 | tf_op jit(solution)/shard_map/ppermute | solution.py:940
  169.0 15.5 %collective-permute-start.39 = (bf16[2,96,1536]{2,1,0:T(8,128)(2,1)S(1)}, bf16[2,96,1536]{2,1,0:T(8,128)(2,1)S(1)}, u32[]{:S(2)}, u32[]{:S(2)}) collective-permute-start(bf16[2,96,1536]{2,1,0:T(8,128)(2,1)S(1)} %slice.209), channel_id=1, source_target_pairs={{0,8},{4,12},{8,0},{12,4},{16,24},{20,28},{24,16},{28,20},{1,9},{5... | collective-permute-start | bytes 1769480 | tf_op jit(solution)/shard_map/ppermute | solution.py:940
  170.5 14.0 %collective-permute-start.40 = (bf16[192,1024]{1,0:T(8,128)(2,1)S(1)}, bf16[192,1024]{1,0:T(8,128)(2,1)S(1)}, u32[]{:S(2)}, u32[]{:S(2)}) collective-permute-start(bf16[192,1024]{1,0:T(8,128)(2,1)S(1)} %get-tuple-element.196), channel_id=1, source_target_pairs={{0,2},{1,3},{2,0},{3,1},{4,6},{5,7},{6,4},{7,5},{8,10},{9,11},{10,... | collective-permute-start | bytes 1179656 | tf_op jit(solution)/shard_map/ppermute | solution.py:946
  183.7 17.9 %collective-permute-start.41 = (bf16[192,1024]{1,0:T(8,128)(2,1)S(1)}, bf16[192,1024]{1,0:T(8,128)(2,1)S(1)}, u32[]{:S(2)}, u32[]{:S(2)}) collective-permute-start(bf16[192,1024]{1,0:T(8,128)(2,1)S(1)} %get-tuple-element.203), channel_id=1, source_target_pairs={{0,2},{1,3},{2,0},{3,1},{4,6},{5,7},{6,4},{7,5},{8,10},{9,11},{10,... | collective-permute-start | bytes 1179656 | tf_op jit(solution)/shard_map/ppermute | solution.py:946
  184.7 16.9 %collective-permute-start.43 = (bf16[1,96,1536]{2,1,0:T(8,128)(2,1)S(1)}, bf16[1,96,1536]{2,1,0:T(8,128)(2,1)S(1)}, u32[]{:S(2)}, u32[]{:S(2)}) collective-permute-start(bf16[1,96,1536]{2,1,0:T(8,128)(2,1)S(1)} %slice.211), channel_id=1, source_target_pairs={{0,16},{4,20},{8,24},{12,28},{16,0},{20,4},{24,8},{28,12},{1,17},{... | collective-permute-start | bytes 884744 | tf_op jit(solution)/shard_map/ppermute | solution.py:940
  187.6 14.0 %collective-permute-start.44 = (bf16[4,96,640]{2,1,0:T(8,128)(2,1)S(1)}, bf16[4,96,640]{2,1,0:T(8,128)(2,1)S(1)}, u32[]{:S(2)}, u32[]{:S(2)}) collective-permute-start(bf16[4,96,640]{2,1,0:T(8,128)(2,1)S(1)} %slice.169), channel_id=1, source_target_pairs={{0,4},{4,0},{8,12},{12,8},{16,20},{20,16},{24,28},{28,24},{1,5},{5... | collective-permute-start | bytes 1474568 | tf_op jit(solution)/shard_map/ppermute | solution.py:940
  200.9 12.0 %collective-permute-start.42 = (bf16[192,1024]{1,0:T(8,128)(2,1)S(1)}, bf16[192,1024]{1,0:T(8,128)(2,1)S(1)}, u32[]{:S(2)}, u32[]{:S(2)}) collective-permute-start(bf16[192,1024]{1,0:T(8,128)(2,1)S(1)} %get-tuple-element.204), channel_id=1, source_target_pairs={{0,2},{1,3},{2,0},{3,1},{4,6},{5,7},{6,4},{7,5},{8,10},{9,11},{10,... | collective-permute-start | bytes 1179656 | tf_op jit(solution)/shard_map/ppermute | solution.py:946
  201.8 11.1 %collective-permute-start.45 = (bf16[4,96,512]{2,1,0:T(8,128)(2,1)S(1)}, bf16[4,96,512]{2,1,0:T(8,128)(2,1)S(1)}, u32[]{:S(2)}, u32[]{:S(2)}) collective-permute-start(bf16[4,96,512]{2,1,0:T(8,128)(2,1)S(1)} %slice.171), channel_id=1, source_target_pairs={{0,4},{4,0},{8,12},{12,8},{16,20},{20,16},{24,28},{28,24},{1,5},{5... | collective-permute-start | bytes 1179656 | tf_op jit(solution)/shard_map/ppermute | solution.py:940
  204.8 24.0 %collective-permute-start.52 = (bf16[384,768]{1,0:T(8,128)(2,1)S(1)}, bf16[384,768]{1,0:T(8,128)(2,1)S(1)}, u32[]{:S(2)}, u32[]{:S(2)}) collective-permute-start(bf16[384,768]{1,0:T(8,128)(2,1)S(1)} %fusion), channel_id=1, source_target_pairs={{0,1},{1,17},{2,3},{3,19},{4,5},{5,21},{6,7},{7,23},{8,9},{9,25},{... | collective-permute-start | bytes 1769480 | tf_op jit(solution)/shard_map/ppermute | solution.py:954
  204.8 23.1 %collective-permute-start.48 = (bf16[96,1536]{1,0:T(8,128)(2,1)S(1)}, bf16[96,1536]{1,0:T(8,128)(2,1)S(1)}, u32[]{:S(2)}, u32[]{:S(2)}) collective-permute-start(bf16[96,1536]{1,0:T(8,128)(2,1)S(1)} %fusion.3), channel_id=1, source_target_pairs={{0,2},{1,3},{2,0},{3,1},{4,6},{5,7},{6,4},{7,5},{8,10},{9,11},{10,... | collective-permute-start | bytes 884744 | tf_op jit(solution)/shard_map/ppermute | solution.py:946
  213.8 14.0 %collective-permute-start.50 = (bf16[1,96,640]{2,1,0:T(8,128)(2,1)S(1)}, bf16[1,96,640]{2,1,0:T(8,128)(2,1)S(1)}, u32[]{:S(2)}, u32[]{:S(2)}) collective-permute-start(bf16[1,96,640]{2,1,0:T(8,128)(2,1)S(1)} %slice.217), channel_id=1, source_target_pairs={{0,16},{4,20},{8,24},{12,28},{16,0},{20,4},{24,8},{28,12},{1,17},{... | collective-permute-start | bytes 368648 | tf_op jit(solution)/shard_map/ppermute | solution.py:940
  227.8 12.8 %collective-permute-start.46 = (bf16[512,768]{1,0:T(8,128)(2,1)S(1)}, bf16[512,768]{1,0:T(8,128)(2,1)S(1)}, u32[]{:S(2)}, u32[]{:S(2)}) collective-permute-start(bf16[512,768]{1,0:T(8,128)(2,1)S(1)} %get-tuple-element.215), channel_id=1, source_target_pairs={{0,1},{1,0},{2,3},{3,2},{4,5},{5,4},{6,7},{7,6},{8,9},{9,8},{10,11... | collective-permute-start | bytes 2359304 | tf_op jit(solution)/shard_map/ppermute | solution.py:943
  (56 other events, 392.0 us)

commit v4 on v3

--- a/solution.py
+++ b/solution.py
@@ -1042,8 +1042,9 @@
     ctx = head(0, part_a[:, :TRIO], b2, vectors, gather_down.pieces[0])
     b3, d2, u1 = after(b3, ctx), after(d2, ctx), after(u1, ctx)
     gather_b.pieces[1], gather_down.pieces[1], gather_up.pieces[1] = b3, d2, u1
+    u2 = gather_up.steps(middle)
+    gather_down.pieces[1] = after(d2, gather_up.pieces[0])
     d3 = gather_down.steps(1)
-    u2 = gather_up.steps(middle)
     part_b = assemble(gather_b.pieces, gather_b.offsets, shard)
     far_a = swap_x(after(part_a, ctx))
     far_b = swap_x(part_b[:, : 2 * TRIO])

time: 250 us -> 250 us (level)
    ppermute x22, waiting for transfers between devices: 31.9 us -> 35.7 us  [swap(): return lax.ppermute(value, 'shard', [(i, i ^ mask) for i in range(n_shard)])]
where the time goes in v4:
time: 250 us; the launch traced here: 248 us
  Pallas kernels  103 us (41%)
  starting transfers between devices  65.8 us (26%)
  waiting for transfers between devices  58.1 us (23%)
  other arithmetic  14.1 us (6%)
  local copies, waits for them, and re-layouts  4.53 us (2%)
    ppermute x22, starting transfers between devices, swap(): return lax.ppermute(value, 'shard', [(i, i ^ mask) for i in range(n_shard)])  41.7 us
    ppermute x22, waiting for transfers between devices, swap(): return lax.ppermute(value, 'shard', [(i, i ^ mask) for i in range(n_shard)])  35.7 us
    pallas_call x3, Pallas kernels, attend_back(): pl.pallas_call(kernel, out_shape=(shape((TRIO, total // 2), BF),) * 2 + (...  34.1 us
    pallas_call x3, Pallas kernels, attend(): pl.pallas_call(attend_kernel, out_shape=(shape((HEAD_DIM, half), BF), sha...  21.7 us
    ppermute x16, starting transfers between devices, swap_x(): return lax.ppermute(value, 'seq', [(i, i ^ 2) for i in range(4)])  18.6 us
    ppermute x16, waiting for transfers between devices, swap_x(): return lax.ppermute(value, 'seq', [(i, i ^ 2) for i in range(4)])  12.3 us
    ppermute x19, waiting for transfers between devices, swap_core(): return lax.ppermute(value, 'seq', [(i, i ^ 1) for i in range(4)])  10.2 us
    pallas_call x1, Pallas kernels, feed_up(): pl.pallas_call(feed_up_kernel, out_shape=(shape((4 * rows, hidden), BF),...  6.94 us
  transfers between devices with their start and end apart: 59, of which 27 were waited for; matrix products, arithmetic and copies ran while one was open for 7% of the time, Pallas kernels for 36%

profile of v4, /device:TPU:0, one launch (start us, length us, event | category | flops | bytes accessed | tf_op | source)
XLA Modules:
  0.0 248.1 jit_solution(13227044772636457994)
XLA Ops:
  2.7 4.1 %collective-permute-start.2 = (bf16[1,96,256]{2,1,0:T(8,128)(2,1)S(1)}, bf16[1,96,256]{2,1,0:T(8,128)(2,1)S(1)}, u32[]{:S(2)}, u32[]{:S(2)}) collective-permute-start(bf16[1,96,256]{2,1,0:T(8,128)(2,1)S(1)} %bitcast.32), channel_id=1, source_target_pairs={{0,16},{4,20},{8,24},{12,28},{16,0},{20,4},{24,8},{28,12},{1,17},{... | collective-permute-start | bytes 147464 | tf_op jit(solution)/shard_map/ppermute | solution.py:940
  9.4 2.4 collective-permute-start.3
  24.5 5.7 %collective-permute-done.5 = bf16[2,96,768]{2,1,0:T(8,128)(2,1)S(1)} collective-permute-done((bf16[2,96,768]{2,1,0:T(8,128)(2,1)S(1)}, bf16[2,96,768]{2,1,0:T(8,128)(2,1)S(1)}, u32[]{:S(2)}, u32[]{:S(2)}) %collective-permute-start.5) | collective-permute-done | bytes 294944 | tf_op jit(solution)/shard_map/ppermute | solution.py:940
  39.4 7.2 %attend.3 = (bf16[64,1024]{1,0:T(8,128)(2,1)S(1)}, bf16[64,1024]{1,0:T(8,128)(2,1)S(1)}, f32[64,2048]{1,0:T(8,128)S(1)}, f32[1,2048]{1,0:T(1,128)S(1)}) custom-call(s32[145]{0:T(256)S(1)} %get-tuple-element.120.plan.refs_0_, bf16[512,768]{1,0:T(8,128)(2,1)S(1)} %copy-done.2, bf16[512,768]{1,0:T(8,128)(2,1)S(1)} %collective-permute-done.tok1.refs_3_, ...), custom_call_target="tpu_custom_call" | custom-call | flops 1 | bytes 1 | tf_op jit(solution)/shard_map/attend/pallas_call | solution.py:260
  56.5 7.2 %attend.4 = (bf16[64,1024]{1,0:T(8,128)(2,1)S(1)}, bf16[64,1024]{1,0:T(8,128)(2,1)S(1)}, f32[64,2048]{1,0:T(8,128)S(1)}, f32[1,2048]{1,0:T(1,128)S(1)}) custom-call(s32[145]{0:T(256)S(1)} %get-tuple-element.120.plan.refs_0_, bf16[512,768]{1,0:T(8,128)(2,1)S(1)} %copy-done.2, bf16[512,768]{1,0:T(8,128)(2,1)S(1)} %collective-permute-done.tok1.refs_3_, ...), custom_call_target="tpu_custom_call" | custom-call | flops 1 | bytes 1 | tf_op jit(solution)/shard_map/attend/pallas_call | solution.py:260
  65.4 4.0 %collective-permute-done.12 = bf16[2,96,1536]{2,1,0:T(8,128)(2,1)S(1)} collective-permute-done((bf16[2,96,1536]{2,1,0:T(8,128)(2,1)S(1)}, bf16[2,96,1536]{2,1,0:T(8,128)(2,1)S(1)}, u32[]{:S(2)}, u32[]{:S(2)}) %collective-permute-start.12) | collective-permute-done | bytes 589856 | tf_op jit(solution)/shard_map/ppermute | solution.py:940
  73.7 2.1 pad_maximum_fusion.1.refs_0_
  75.8 7.3 %attend.5 = (bf16[64,1024]{1,0:T(8,128)(2,1)S(1)}, bf16[64,1024]{1,0:T(8,128)(2,1)S(1)}, f32[64,2048]{1,0:T(8,128)S(1)}, f32[1,2048]{1,0:T(1,128)S(1)}) custom-call(s32[145]{0:T(256)S(1)} %get-tuple-element.120.plan.refs_0_, bf16[512,768]{1,0:T(8,128)(2,1)S(1)} %copy-done.2, bf16[512,768]{1,0:T(8,128)(2,1)S(1)} %collective-permute-done.tok1.refs_3_, ...), custom_call_target="tpu_custom_call" | custom-call | flops 1 | bytes 1 | tf_op jit(solution)/shard_map/attend/pallas_call | solution.py:260
  85.4 4.3 %collective-permute-done.18 = bf16[64,1024]{1,0:T(8,128)(2,1)S(1)} collective-permute-done((bf16[64,1024]{1,0:T(8,128)(2,1)S(1)}, bf16[64,1024]{1,0:T(8,128)(2,1)S(1)}, u32[]{:S(2)}, u32[]{:S(2)}) %collective-permute-start.18) | collective-permute-done | bytes 131104 | tf_op jit(solution)/shard_map/ppermute | solution.py:946
  90.8 6.4 %collective-permute-done.20.refs_1_ = bf16[4,96,1536]{2,1,0:T(8,128)(2,1)S(1)} collective-permute-done((bf16[4,96,1536]{2,1,0:T(8,128)(2,1)S(1)}, bf16[4,96,1536]{2,1,0:T(8,128)(2,1)S(1)}, u32[]{:S(2)}, u32[]{:S(2)}) %collective-permute-start.20) | collective-permute-done | bytes 1179680 | tf_op jit(solution)/shard_map/ppermute | solution.py:940
  100.7 2.5 %first_norm.1 = (bf16[256,768]{1,0:T(8,128)(2,1)}, bf16[256,768]{1,0:T(8,128)(2,1)}, f32[512,768]{1,0:T(8,128)}, f32[512,1]{1,0:T(8,128)}) custom-call(bf16[512,768]{1,0:T(8,128)(2,1)S(1)} %copy-done.2, f32[1024,768]{1,0:T(8,128)S(1)} %fusion.11.mixed, bf16[256,768]{1,0:T(8,128)(2,1)S(1)} %collective-permute-done.21.recv0, ...), custom_call_target="tpu_custom_call" | custom-call | flops 1 | bytes 1 | tf_op jit(solution)/shard_map/first_norm/pallas_call | solution.py:804
  105.8 6.9 %feed_up.1 = (bf16[1024,1536]{1,0:T(8,128)(2,1)S(1)}, bf16[1536,1024]{1,0:T(8,128)(2,1)S(1)}, bf16[1024,1536]{1,0:T(8,128)(2,1)S(1)}, bf16[768,1024]{1,0:T(8,128)(2,1)S(1)}) custom-call(bf16[256,768]{1,0:T(8,128)(2,1)} %get-tuple-element.150.low0, bf16[256,768]{1,0:T(8,128)(2,1)} %get-tuple-element.151.low1, bf16[256,768]{1,0:T(8,128)(2,1)} %collective-permute-done.23.low2, ...), custom_call_target="tpu_custom_call" | custom-call | flops 1 | bytes 1 | tf_op jit(solution)/shard_map/feed_up/pallas_call | solution.py:546
  114.5 3.2 %feed_down.1 = (f32[512,768]{1,0:T(8,128)S(1)}, bf16[512,768]{1,0:T(8,128)(2,1)S(1)}) custom-call(bf16[1024,1536]{1,0:T(8,128)(2,1)S(1)} %get-tuple-element.152.act, bf16[1536,768]{1,0:T(8,128)(2,1)S(1)} %assemble.7.down), custom_call_target="tpu_custom_call" | custom-call | flops 1 | bytes 1 | tf_op jit(solution)/shard_map/feed_down/pallas_call | solution.py:587
  117.9 2.1 collective-permute-done.26.recv
  120.1 2.4 second_norm.1
  122.6 2.1 collective-permute-done.27.refs_3_.grad_other
  124.7 3.0 %weight_grad.2 = bf16[4,384,768]{2,1,0:T(8,128)(2,1)S(1)} custom-call(s32[1]{0:T(128)} %bitcast.12.refs_0_, bf16[1536,1024]{1,0:T(8,128)(2,1)S(1)} %get-tuple-element.160.refs_1_, bf16[512,768]{1,0:T(8,128)(2,1)S(1)} %get-tuple-element.161.refs_2_.grad_own, bf16[512,768]{1,0:T(8,128)(2,1)S(1)} %collective-permute-done.27.refs_3_.grad_other), custom_call_target="tpu_custom_call" | custom-call | flops 1 | bytes 1 | tf_op jit(solution)/shard_map/weight_grad/pallas_call | solution.py:682
  129.3 6.5 %feed_back.1 = (f32[512,768]{1,0:T(8,128)S(1)}, bf16[256,768]{1,0:T(8,128)(2,1)S(1)}, bf16[256,768]{1,0:T(8,128)(2,1)S(1)}, bf16[1024,1536]{1,0:T(8,128)(2,1)S(1)}) custom-call(bf16[512,768]{1,0:T(8,128)(2,1)S(1)} %get-tuple-element.161.refs_2_.grad_own, bf16[512,768]{1,0:T(8,128)(2,1)S(1)} %collective-permute-done.27.refs_3_.grad_other, ...), custom_call_target="tpu_custom_call" | custom-call | flops 1 | bytes 1 | tf_op jit(solution)/shard_map/feed_back/pallas_call | solution.py:631
  136.4 3.5 %weight_grad.3 = bf16[8,96,1536]{2,1,0:T(8,128)(2,1)S(1)} custom-call(s32[1]{0:T(128)} %bitcast.2.info.refs_0_, bf16[768,1024]{1,0:T(8,128)(2,1)S(1)} %get-tuple-element.166.refs_1_, bf16[1024,1536]{1,0:T(8,128)(2,1)S(1)} %get-tuple-element.167.refs_2_), custom_call_target="tpu_custom_call" | custom-call | flops 1 | bytes 1 | tf_op jit(solution)/shard_map/weight_grad/pallas_call | solution.py:682
  151.7 11.5 %attend_back.3 = (bf16[192,1024]{1,0:T(8,128)(2,1)S(1)}, bf16[192,1024]{1,0:T(8,128)(2,1)S(1)}, bf16[8,96,256]{2,1,0:T(8,128)(2,1)S(1)}) custom-call(s32[145]{0:T(256)S(1)} %get-tuple-element.120.plan.refs_0_, s32[3]{0:T(128)S(1)} %pad_add_fusion.place.info.refs_1_, bf16[512,768]{1,0:T(8,128)(2,1)S(1)} %copy-done.2, ...), custom_call_target="tpu_custom_call" | custom-call | flops 1 | bytes 1 | tf_op jit(solution)/shard_map/attend_back/pallas_call | solution.py:396
  164.4 3.6 %collective-permute-done.37 = bf16[4,96,1536]{2,1,0:T(8,128)(2,1)S(1)} collective-permute-done((bf16[4,96,1536]{2,1,0:T(8,128)(2,1)S(1)}, bf16[4,96,1536]{2,1,0:T(8,128)(2,1)S(1)}, u32[]{:S(2)}, u32[]{:S(2)}) %collective-permute-start.37) | collective-permute-done | bytes 1179680 | tf_op jit(solution)/shard_map/ppermute | solution.py:940
  171.9 11.3 %attend_back.4 = (bf16[192,1024]{1,0:T(8,128)(2,1)S(1)}, bf16[192,1024]{1,0:T(8,128)(2,1)S(1)}, bf16[8,96,256]{2,1,0:T(8,128)(2,1)S(1)}) custom-call(s32[145]{0:T(256)S(1)} %get-tuple-element.120.plan.refs_0_, s32[3]{0:T(128)S(1)} %pad_add_fusion.place.info.refs_1_, bf16[512,768]{1,0:T(8,128)(2,1)S(1)} %copy-done.2, ...), custom_call_target="tpu_custom_call" | custom-call | flops 1 | bytes 1 | tf_op jit(solution)/shard_map/attend_back/pallas_call | solution.py:396
  184.2 3.4 %collective-permute-start.43 = (bf16[1,96,1536]{2,1,0:T(8,128)(2,1)S(1)}, bf16[1,96,1536]{2,1,0:T(8,128)(2,1)S(1)}, u32[]{:S(2)}, u32[]{:S(2)}) collective-permute-start(bf16[1,96,1536]{2,1,0:T(8,128)(2,1)S(1)} %slice.211), channel_id=1, source_target_pairs={{0,16},{4,20},{8,24},{12,28},{16,0},{20,4},{24,8},{28,12},{1,17},{... | collective-permute-start | bytes 884744 | tf_op jit(solution)/shard_map/ppermute | solution.py:940
  188.7 11.3 %attend_back.5 = (bf16[192,1024]{1,0:T(8,128)(2,1)S(1)}, bf16[192,1024]{1,0:T(8,128)(2,1)S(1)}, bf16[8,96,512]{2,1,0:T(8,128)(2,1)S(1)}) custom-call(s32[145]{0:T(256)S(1)} %get-tuple-element.120.plan.refs_0_, s32[3]{0:T(128)S(1)} %pad_add_fusion.place.info.refs_1_, bf16[512,768]{1,0:T(8,128)(2,1)S(1)} %copy-done.2, ...), custom_call_target="tpu_custom_call" | custom-call | flops 1 | bytes 1 | tf_op jit(solution)/shard_map/attend_back/pallas_call | solution.py:396
  200.9 2.0 collective-permute-start.45
  203.5 3.6 %collective-permute-start.49 = (bf16[2,96,640]{2,1,0:T(8,128)(2,1)S(1)}, bf16[2,96,640]{2,1,0:T(8,128)(2,1)S(1)}, u32[]{:S(2)}, u32[]{:S(2)}) collective-permute-start(bf16[2,96,640]{2,1,0:T(8,128)(2,1)S(1)} %slice.215), channel_id=1, source_target_pairs={{0,8},{4,12},{8,0},{12,4},{16,24},{20,28},{24,16},{28,20},{1,9},{5... | collective-permute-start | bytes 737288 | tf_op jit(solution)/shard_map/ppermute | solution.py:940
  207.1 4.8 %collective-permute-done.42.refs_5_ = bf16[192,1024]{1,0:T(8,128)(2,1)S(1)} collective-permute-done((bf16[192,1024]{1,0:T(8,128)(2,1)S(1)}, bf16[192,1024]{1,0:T(8,128)(2,1)S(1)}, u32[]{:S(2)}, u32[]{:S(2)}) %collective-permute-start.42) | collective-permute-done | bytes 393248 | tf_op jit(solution)/shard_map/ppermute | solution.py:946
  212.1 3.6 %collective-permute-done.49 = bf16[2,96,640]{2,1,0:T(8,128)(2,1)S(1)} collective-permute-done((bf16[2,96,640]{2,1,0:T(8,128)(2,1)S(1)}, bf16[2,96,640]{2,1,0:T(8,128)(2,1)S(1)}, u32[]{:S(2)}, u32[]{:S(2)}) %collective-permute-start.49) | collective-permute-done | bytes 245792 | tf_op jit(solution)/shard_map/ppermute | solution.py:940
  215.8 5.6 %collective-permute-start.50 = (bf16[1,96,640]{2,1,0:T(8,128)(2,1)S(1)}, bf16[1,96,640]{2,1,0:T(8,128)(2,1)S(1)}, u32[]{:S(2)}, u32[]{:S(2)}) collective-permute-start(bf16[1,96,640]{2,1,0:T(8,128)(2,1)S(1)} %slice.217), channel_id=1, source_target_pairs={{0,16},{4,20},{8,24},{12,28},{16,0},{20,4},{24,8},{28,12},{1,17},{... | collective-permute-start | bytes 368648 | tf_op jit(solution)/shard_map/ppermute | solution.py:940
  223.2 3.6 %input_back.1 = (f32[512,768]{1,0:T(8,128)S(1)}, bf16[512,768]{1,0:T(8,128)(2,1)S(1)}) custom-call(bf16[192,1024]{1,0:T(8,128)(2,1)S(1)} %get-tuple-element.186.refs_0_, bf16[192,1024]{1,0:T(8,128)(2,1)S(1)} %get-tuple-element.195.refs_1_, bf16[192,1024]{1,0:T(8,128)(2,1)S(1)} %get-tuple-element.204.refs_2_, ...), custom_call_target="tpu_custom_call" | custom-call | flops 1 | bytes 1 | tf_op jit(solution)/shard_map/input_back/pallas_call | solution.py:452
  231.4 4.8 %collective-permute-done.51 = bf16[1,96,512]{2,1,0:T(8,128)(2,1)S(1)} collective-permute-done((bf16[1,96,512]{2,1,0:T(8,128)(2,1)S(1)}, bf16[1,96,512]{2,1,0:T(8,128)(2,1)S(1)}, u32[]{:S(2)}, u32[]{:S(2)}) %collective-permute-start.51) | collective-permute-done | bytes 98336 | tf_op jit(solution)/shard_map/ppermute | solution.py:940
  245.3 2.0 place_qkv.1
  (234 shorter events, 92.3 us)
Async XLA Ops:
  6.8 23.5 %collective-permute-start.1 = (bf16[512,768]{1,0:T(8,128)(2,1)}, bf16[512,768]{1,0:T(8,128)(2,1)S(1)}, u32[]{:S(2)}, u32[]{:S(2)}) collective-permute-start(bf16[512,768]{1,0:T(8,128)(2,1)} %refs_2_.5), channel_id=1, source_target_pairs={{0,2},{1,3},{2,0},{3,1},{4,6},{5,7},{6,4},{7,5},{8,10},{9,11},{10,... | collective-permute-start | bytes 2359304 | tf_op jit(solution)/shard_map/ppermute | solution.py:946
  19.1 11.1 %collective-permute-start.5 = (bf16[2,96,768]{2,1,0:T(8,128)(2,1)S(1)}, bf16[2,96,768]{2,1,0:T(8,128)(2,1)S(1)}, u32[]{:S(2)}, u32[]{:S(2)}) collective-permute-start(bf16[2,96,768]{2,1,0:T(8,128)(2,1)S(1)} %pad_maximum_fusion.6), channel_id=1, source_target_pairs={{0,8},{4,12},{8,0},{12,4},{16,24},{20,28},{24,16},{28,20},{1,9},{5... | collective-permute-start | bytes 884744 | tf_op jit(solution)/shard_map/ppermute | solution.py:940
  24.5 14.9 %collective-permute-start = (bf16[512,768]{1,0:T(8,128)(2,1)S(1)}, bf16[512,768]{1,0:T(8,128)(2,1)S(1)}, u32[]{:S(2)}, u32[]{:S(2)}) collective-permute-start(bf16[512,768]{1,0:T(8,128)(2,1)S(1)} %copy-done.2), channel_id=1, source_target_pairs={{0,1},{1,0},{2,3},{3,2},{4,5},{5,4},{6,7},{7,6},{8,9},{9,8},{10,11... | collective-permute-start | bytes 2359304 | tf_op jit(solution)/shard_map/ppermute | solution.py:943
  31.8 16.1 %collective-permute-start.9 = (bf16[4,96,768]{2,1,0:T(8,128)(2,1)}, bf16[4,96,768]{2,1,0:T(8,128)(2,1)}, u32[]{:S(2)}, u32[]{:S(2)}) collective-permute-start(bf16[4,96,768]{2,1,0:T(8,128)(2,1)} %pad_maximum_fusion.2.refs_0_), channel_id=1, source_target_pairs={{0,4},{4,0},{8,12},{12,8},{16,20},{20,16},{24,28},{28,24},{1,5},{5... | collective-permute-start | bytes 1769480 | tf_op jit(solution)/shard_map/ppermute | solution.py:940
  35.2 16.2 %collective-permute-start.11 = (bf16[1,96,1536]{2,1,0:T(8,128)(2,1)S(1)}, bf16[1,96,1536]{2,1,0:T(8,128)(2,1)}, u32[]{:S(2)}, u32[]{:S(2)}) collective-permute-start(bf16[1,96,1536]{2,1,0:T(8,128)(2,1)S(1)} %fusion.14), channel_id=1, source_target_pairs={{0,16},{4,20},{8,24},{12,28},{16,0},{20,4},{24,8},{28,12},{1,17},{... | collective-permute-start | bytes 884744 | tf_op jit(solution)/shard_map/ppermute | solution.py:940
  37.5 15.2 %collective-permute-start.10 = (bf16[1,192,768]{2,1,0:T(8,128)(2,1)}, bf16[1,192,768]{2,1,0:T(8,128)(2,1)S(1)}, u32[]{:S(2)}, u32[]{:S(2)}) collective-permute-start(bf16[1,192,768]{2,1,0:T(8,128)(2,1)} %select_bitcast_fusion), channel_id=1, source_target_pairs={{0,8},{4,12},{8,0},{12,4},{16,24},{20,28},{24,16},{28,20},{1,9},{5... | collective-permute-start | bytes 884744 | tf_op jit(solution)/shard_map/ppermute | solution.py:940
  49.4 14.4 %collective-permute-start.19 = (bf16[384,384]{1,0:T(8,128)(2,1)S(1)}, bf16[384,384]{1,0:T(8,128)(2,1)S(1)}, u32[]{:S(2)}, u32[]{:S(2)}) collective-permute-start(bf16[384,384]{1,0:T(8,128)(2,1)S(1)} %get-tuple-element.237), channel_id=1, source_target_pairs={{0,1},{1,0},{2,3},{3,2},{4,5},{5,4},{6,7},{7,6},{8,9},{9,8},{10,11... | collective-permute-start | bytes 884744 | tf_op jit(solution)/shard_map/ppermute | solution.py:943
  53.9 18.4 %collective-permute-start.13 = (bf16[2,192,768]{2,1,0:T(8,128)(2,1)S(1)}, bf16[2,192,768]{2,1,0:T(8,128)(2,1)S(1)}, u32[]{:S(2)}, u32[]{:S(2)}) collective-permute-start(bf16[2,192,768]{2,1,0:T(8,128)(2,1)S(1)} %pad_maximum_fusion.4), channel_id=1, source_target_pairs={{0,4},{4,0},{8,12},{12,8},{16,20},{20,16},{24,28},{28,24},{1,5},{5... | collective-permute-start | bytes 1769480 | tf_op jit(solution)/shard_map/ppermute | solution.py:940
  54.5 15.0 %collective-permute-start.12 = (bf16[2,96,1536]{2,1,0:T(8,128)(2,1)S(1)}, bf16[2,96,1536]{2,1,0:T(8,128)(2,1)S(1)}, u32[]{:S(2)}, u32[]{:S(2)}) collective-permute-start(bf16[2,96,1536]{2,1,0:T(8,128)(2,1)S(1)} %pad_maximum_fusion.3), channel_id=1, source_target_pairs={{0,8},{4,12},{8,0},{12,4},{16,24},{20,28},{24,16},{28,20},{1,9},{5... | collective-permute-start | bytes 1769480 | tf_op jit(solution)/shard_map/ppermute | solution.py:940
  54.5 28.8 %collective-permute-start.17 = (bf16[768,384]{1,0:T(8,128)(2,1)S(1)}, bf16[768,384]{1,0:T(8,128)(2,1)S(1)}, u32[]{:S(2)}, u32[]{:S(2)}) collective-permute-start(bf16[768,384]{1,0:T(8,128)(2,1)S(1)} %slice.195), channel_id=1, source_target_pairs={{0,2},{1,3},{2,0},{3,1},{4,6},{5,7},{6,4},{7,5},{8,10},{9,11},{10,... | collective-permute-start | bytes 1769480 | tf_op jit(solution)/shard_map/ppermute | solution.py:946
  55.9 27.3 %collective-permute-start.16 = (bf16[768,256]{1,0:T(8,128)(2,1)S(1)}, bf16[768,256]{1,0:T(8,128)(2,1)S(1)}, u32[]{:S(2)}, u32[]{:S(2)}) collective-permute-start(bf16[768,256]{1,0:T(8,128)(2,1)S(1)} %assemble.4.part), channel_id=1, source_target_pairs={{0,2},{1,3},{2,0},{3,1},{4,6},{5,7},{6,4},{7,5},{8,10},{9,11},{10,... | collective-permute-start | bytes 1179656 | tf_op jit(solution)/shard_map/ppermute | solution.py:946
  63.7 21.6 %collective-permute-start.14 = (bf16[64,1024]{1,0:T(8,128)(2,1)S(1)}, bf16[64,1024]{1,0:T(8,128)(2,1)S(1)}, u32[]{:S(2)}, u32[]{:S(2)}) collective-permute-start(bf16[64,1024]{1,0:T(8,128)(2,1)S(1)} %get-tuple-element.143), channel_id=1, source_target_pairs={{0,2},{1,3},{2,0},{3,1},{4,6},{5,7},{6,4},{7,5},{8,10},{9,11},{10,... | collective-permute-start | bytes 393224 | tf_op jit(solution)/shard_map/ppermute | solution.py:946
  70.5 26.8 %collective-permute-start.20 = (bf16[4,96,1536]{2,1,0:T(8,128)(2,1)S(1)}, bf16[4,96,1536]{2,1,0:T(8,128)(2,1)S(1)}, u32[]{:S(2)}, u32[]{:S(2)}) collective-permute-start(bf16[4,96,1536]{2,1,0:T(8,128)(2,1)S(1)} %pad_maximum_fusion.refs_0_), channel_id=1, source_target_pairs={{0,4},{4,0},{8,12},{12,8},{16,20},{20,16},{24,28},{28,24},{1,5},{5... | collective-permute-start | bytes 3538952 | tf_op jit(solution)/shard_map/ppermute | solution.py:940
  72.3 13.1 %collective-permute-start.15 = (bf16[64,1024]{1,0:T(8,128)(2,1)S(1)}, bf16[64,1024]{1,0:T(8,128)(2,1)S(1)}, u32[]{:S(2)}, u32[]{:S(2)}) collective-permute-start(bf16[64,1024]{1,0:T(8,128)(2,1)S(1)} %get-tuple-element.144), channel_id=1, source_target_pairs={{0,2},{1,3},{2,0},{3,1},{4,6},{5,7},{6,4},{7,5},{8,10},{9,11},{10,... | collective-permute-start | bytes 393224 | tf_op jit(solution)/shard_map/ppermute | solution.py:946
  83.9 28.9 %collective-permute-start.25 = (bf16[4,192,768]{2,1,0:T(8,128)(2,1)}, bf16[4,192,768]{2,1,0:T(8,128)(2,1)}, u32[]{:S(2)}, u32[]{:S(2)}) collective-permute-start(bf16[4,192,768]{2,1,0:T(8,128)(2,1)} %pad_maximum_fusion.1.refs_0_), channel_id=1, source_target_pairs={{0,2},{1,3},{2,0},{3,1},{4,6},{5,7},{6,4},{7,5},{8,10},{9,11},{10,... | collective-permute-start | bytes 3538952 | tf_op jit(solution)/shard_map/ppermute | solution.py:946
  127.8 35.5 %collective-permute-start.34 = (bf16[2,384,768]{2,1,0:T(8,128)(2,1)S(1)}, bf16[2,384,768]{2,1,0:T(8,128)(2,1)S(1)}, u32[]{:S(2)}, u32[]{:S(2)}) collective-permute-start(bf16[2,384,768]{2,1,0:T(8,128)(2,1)S(1)} %slice.203), channel_id=1, source_target_pairs={{0,8},{4,12},{8,0},{12,4},{16,24},{20,28},{24,16},{28,20},{1,9},{5... | collective-permute-start | bytes 3538952 | tf_op jit(solution)/shard_map/ppermute | solution.py:940
  140.0 28.0 %collective-permute-start.37 = (bf16[4,96,1536]{2,1,0:T(8,128)(2,1)S(1)}, bf16[4,96,1536]{2,1,0:T(8,128)(2,1)S(1)}, u32[]{:S(2)}, u32[]{:S(2)}) collective-permute-start(bf16[4,96,1536]{2,1,0:T(8,128)(2,1)S(1)} %slice.205), channel_id=1, source_target_pairs={{0,4},{4,0},{8,12},{12,8},{16,20},{20,16},{24,28},{28,24},{1,5},{5... | collective-permute-start | bytes 3538952 | tf_op jit(solution)/shard_map/ppermute | solution.py:940
  146.7 16.5 %collective-permute-start.35 = (bf16[64,1024]{1,0:T(8,128)(2,1)S(1)}, bf16[64,1024]{1,0:T(8,128)(2,1)S(1)}, u32[]{:S(2)}, u32[]{:S(2)}) collective-permute-start(bf16[64,1024]{1,0:T(8,128)(2,1)S(1)} %get-tuple-element.179), channel_id=1, source_target_pairs={{0,2},{1,3},{2,0},{3,1},{4,6},{5,7},{6,4},{7,5},{8,10},{9,11},{10,... | collective-permute-start | bytes 393224 | tf_op jit(solution)/shard_map/ppermute | solution.py:946
  147.4 15.8 %collective-permute-start.36 = (bf16[64,1024]{1,0:T(8,128)(2,1)S(1)}, bf16[64,1024]{1,0:T(8,128)(2,1)S(1)}, u32[]{:S(2)}, u32[]{:S(2)}) collective-permute-start(bf16[64,1024]{1,0:T(8,128)(2,1)S(1)} %get-tuple-element.180), channel_id=1, source_target_pairs={{0,2},{1,3},{2,0},{3,1},{4,6},{5,7},{6,4},{7,5},{8,10},{9,11},{10,... | collective-permute-start | bytes 393224 | tf_op jit(solution)/shard_map/ppermute | solution.py:946
  151.7 11.8 %collective-permute-start.33 = (bf16[384,384]{1,0:T(8,128)(2,1)S(1)}, bf16[384,384]{1,0:T(8,128)(2,1)S(1)}, u32[]{:S(2)}, u32[]{:S(2)}) collective-permute-start(bf16[384,384]{1,0:T(8,128)(2,1)S(1)} %get-tuple-element.187), channel_id=1, source_target_pairs={{0,1},{1,0},{2,3},{3,2},{4,5},{5,4},{6,7},{7,6},{8,9},{9,8},{10,11... | collective-permute-start | bytes 884744 | tf_op jit(solution)/shard_map/ppermute | solution.py:943
  168.0 15.9 %collective-permute-start.38 = (bf16[1,384,768]{2,1,0:T(8,128)(2,1)S(1)}, bf16[1,384,768]{2,1,0:T(8,128)(2,1)S(1)}, u32[]{:S(2)}, u32[]{:S(2)}) collective-permute-start(bf16[1,384,768]{2,1,0:T(8,128)(2,1)S(1)} %slice.207), channel_id=1, source_target_pairs={{0,4},{4,0},{8,12},{12,8},{16,20},{20,16},{24,28},{28,24},{1,5},{5... | collective-permute-start | bytes 1769480 | tf_op jit(solution)/shard_map/ppermute | solution.py:940
  169.0 15.0 %collective-permute-start.39 = (bf16[2,96,1536]{2,1,0:T(8,128)(2,1)S(1)}, bf16[2,96,1536]{2,1,0:T(8,128)(2,1)S(1)}, u32[]{:S(2)}, u32[]{:S(2)}) collective-permute-start(bf16[2,96,1536]{2,1,0:T(8,128)(2,1)S(1)} %slice.209), channel_id=1, source_target_pairs={{0,8},{4,12},{8,0},{12,4},{16,24},{20,28},{24,16},{28,20},{1,9},{5... | collective-permute-start | bytes 1769480 | tf_op jit(solution)/shard_map/ppermute | solution.py:940
  170.5 13.5 %collective-permute-start.40 = (bf16[192,1024]{1,0:T(8,128)(2,1)S(1)}, bf16[192,1024]{1,0:T(8,128)(2,1)S(1)}, u32[]{:S(2)}, u32[]{:S(2)}) collective-permute-start(bf16[192,1024]{1,0:T(8,128)(2,1)S(1)} %get-tuple-element.198), channel_id=1, source_target_pairs={{0,2},{1,3},{2,0},{3,1},{4,6},{5,7},{6,4},{7,5},{8,10},{9,11},{10,... | collective-permute-start | bytes 1179656 | tf_op jit(solution)/shard_map/ppermute | solution.py:946
  183.2 17.4 %collective-permute-start.41 = (bf16[192,1024]{1,0:T(8,128)(2,1)S(1)}, bf16[192,1024]{1,0:T(8,128)(2,1)S(1)}, u32[]{:S(2)}, u32[]{:S(2)}) collective-permute-start(bf16[192,1024]{1,0:T(8,128)(2,1)S(1)} %get-tuple-element.205), channel_id=1, source_target_pairs={{0,2},{1,3},{2,0},{3,1},{4,6},{5,7},{6,4},{7,5},{8,10},{9,11},{10,... | collective-permute-start | bytes 1179656 | tf_op jit(solution)/shard_map/ppermute | solution.py:946
  184.2 16.4 %collective-permute-start.43 = (bf16[1,96,1536]{2,1,0:T(8,128)(2,1)S(1)}, bf16[1,96,1536]{2,1,0:T(8,128)(2,1)S(1)}, u32[]{:S(2)}, u32[]{:S(2)}) collective-permute-start(bf16[1,96,1536]{2,1,0:T(8,128)(2,1)S(1)} %slice.211), channel_id=1, source_target_pairs={{0,16},{4,20},{8,24},{12,28},{16,0},{20,4},{24,8},{28,12},{1,17},{... | collective-permute-start | bytes 884744 | tf_op jit(solution)/shard_map/ppermute | solution.py:940
  187.7 13.0 %collective-permute-start.44 = (bf16[4,96,640]{2,1,0:T(8,128)(2,1)S(1)}, bf16[4,96,640]{2,1,0:T(8,128)(2,1)S(1)}, u32[]{:S(2)}, u32[]{:S(2)}) collective-permute-start(bf16[4,96,640]{2,1,0:T(8,128)(2,1)S(1)} %slice.169), channel_id=1, source_target_pairs={{0,4},{4,0},{8,12},{12,8},{16,20},{20,16},{24,28},{28,24},{1,5},{5... | collective-permute-start | bytes 1474568 | tf_op jit(solution)/shard_map/ppermute | solution.py:940
  200.0 12.0 %collective-permute-start.42 = (bf16[192,1024]{1,0:T(8,128)(2,1)S(1)}, bf16[192,1024]{1,0:T(8,128)(2,1)S(1)}, u32[]{:S(2)}, u32[]{:S(2)}) collective-permute-start(bf16[192,1024]{1,0:T(8,128)(2,1)S(1)} %get-tuple-element.206), channel_id=1, source_target_pairs={{0,2},{1,3},{2,0},{3,1},{4,6},{5,7},{6,4},{7,5},{8,10},{9,11},{10,... | collective-permute-start | bytes 1179656 | tf_op jit(solution)/shard_map/ppermute | solution.py:946
  200.9 11.1 %collective-permute-start.45 = (bf16[4,96,512]{2,1,0:T(8,128)(2,1)S(1)}, bf16[4,96,512]{2,1,0:T(8,128)(2,1)S(1)}, u32[]{:S(2)}, u32[]{:S(2)}) collective-permute-start(bf16[4,96,512]{2,1,0:T(8,128)(2,1)S(1)} %slice.171), channel_id=1, source_target_pairs={{0,4},{4,0},{8,12},{12,8},{16,20},{20,16},{24,28},{28,24},{1,5},{5... | collective-permute-start | bytes 1179656 | tf_op jit(solution)/shard_map/ppermute | solution.py:940
  202.9 24.5 %collective-permute-start.52 = (bf16[384,768]{1,0:T(8,128)(2,1)S(1)}, bf16[384,768]{1,0:T(8,128)(2,1)S(1)}, u32[]{:S(2)}, u32[]{:S(2)}) collective-permute-start(bf16[384,768]{1,0:T(8,128)(2,1)S(1)} %fusion), channel_id=1, source_target_pairs={{0,1},{1,17},{2,3},{3,19},{4,5},{5,21},{6,7},{7,23},{8,9},{9,25},{... | collective-permute-start | bytes 1769480 | tf_op jit(solution)/shard_map/ppermute | solution.py:954
  202.9 24.0 %collective-permute-start.48 = (bf16[96,1536]{1,0:T(8,128)(2,1)S(1)}, bf16[96,1536]{1,0:T(8,128)(2,1)S(1)}, u32[]{:S(2)}, u32[]{:S(2)}) collective-permute-start(bf16[96,1536]{1,0:T(8,128)(2,1)S(1)} %fusion.3), channel_id=1, source_target_pairs={{0,2},{1,3},{2,0},{3,1},{4,6},{5,7},{6,4},{7,5},{8,10},{9,11},{10,... | collective-permute-start | bytes 884744 | tf_op jit(solution)/shard_map/ppermute | solution.py:946
  203.5 12.2 %collective-permute-start.49 = (bf16[2,96,640]{2,1,0:T(8,128)(2,1)S(1)}, bf16[2,96,640]{2,1,0:T(8,128)(2,1)S(1)}, u32[]{:S(2)}, u32[]{:S(2)}) collective-permute-start(bf16[2,96,640]{2,1,0:T(8,128)(2,1)S(1)} %slice.215), channel_id=1, source_target_pairs={{0,8},{4,12},{8,0},{12,4},{16,24},{20,28},{24,16},{28,20},{1,9},{5... | collective-permute-start | bytes 737288 | tf_op jit(solution)/shard_map/ppermute | solution.py:940
  226.8 12.7 %collective-permute-start.46 = (bf16[512,768]{1,0:T(8,128)(2,1)S(1)}, bf16[512,768]{1,0:T(8,128)(2,1)S(1)}, u32[]{:S(2)}, u32[]{:S(2)}) collective-permute-start(bf16[512,768]{1,0:T(8,128)(2,1)S(1)} %get-tuple-element.217), channel_id=1, source_target_pairs={{0,1},{1,0},{2,3},{3,2},{4,5},{5,4},{6,7},{7,6},{8,9},{9,8},{10,11... | collective-permute-start | bytes 2359304 | tf_op jit(solution)/shard_map/ppermute | solution.py:943
  (56 other events, 392.2 us)
